TPU v7x, 32 devices: a whole 2x2x4 slice. The times are simulated.
32 devices in a mesh: dp: 4 (over y, core), tm: 8 (over z, x).
Axes of the slice: x: 2, y: 2, z: 4, core: 2. Of those that a mesh axis runs over, the one named last changes fastest.
Arguments:
- features: bfloat16 [4, 8192, 512], P('dp', 'tm'), may hold values from -52 to 52
- conv_wide: bfloat16 [1536, 512], replicated, may hold values from -0.15625 to 0.15625
- conv_narrow: bfloat16 [1024, 512], replicated, may hold values from -0.1875 to 0.1875
- conv_bias: float32 [2, 512], replicated, may hold values from -4 to 4
- norm_gain: float32 [2, 512], replicated, may hold values from 0.1 to 1.9
- norm_bias: float32 [2, 512], replicated, may hold values from -3 to 3
- proj_gain: float32 [512], replicated, may hold values from 0.1 to 1.9
- proj_weight: bfloat16 [512, 1920], replicated, may hold values from -0.25 to 0.25
- proj_bias: float32 [1920], replicated, may hold values from -3 to 3
- upstream: bfloat16 [64, 2048, 120], P(('dp', 'tm')), may hold values from -6 to 6
Outputs:
- attn_input: bfloat16 [64, 2048, 120], P(('dp', 'tm'))
- feature_grad: bfloat16 [4, 8192, 512], P('dp', 'tm')
- grad_conv_wide: float32 [786432], P(('dp', 'tm'))
- grad_conv_narrow: float32 [524288], P(('dp', 'tm'))
All inputs are finite; a program needn't handle non-finite values.
Results may differ from a plain program's by a relative error of at most 0.02.
Values may be sent and summed in bfloat16 or wider, within the bound.
No kernel may reach another device: no remote copies, remote signals or barrier semaphores. Data moves between devices by JAX's collectives and lax.ppermute only.
A program may use at most 128 MiB of HBM per device.

v0:
```python
import math

import jax
import jax.numpy as jnp
from jax import lax
from jax.sharding import PartitionSpec as P

HEADS = 16
HEAD_DIM = 120


EPSILON = 1e-05
SQRT_HALF = 0.7071067811865476
INV_ROOT_TAU = 0.3989422804014327


def passed_along(value, axis, steps):
    count = lax.axis_size(axis)
    leading, last = (max(0, -steps), min(count, count - steps))
    return lax.ppermute(value, axis, [(source, source + steps) for source in range(leading, last)])


def gelu_exact(values):
    return 0.5 * values * (1.0 + lax.erf(values * SQRT_HALF))


def gelu_slope(values):
    cumulative = 0.5 * (1.0 + lax.erf(values * SQRT_HALF))
    density = jnp.exp(-0.5 * values * values) * INV_ROOT_TAU
    return cumulative + values * density


def wide_patches(signal, first_next):
    recs_local, length, channels = signal.shape
    paired = signal.reshape(recs_local, length // 2, 2 * channels)
    following = jnp.concatenate([paired[:, 1:, :channels], first_next], axis=1)
    return jnp.concatenate([paired, following], axis=2)


def narrow_patches(signal):
    recs_local, length, channels = signal.shape
    return signal.reshape(recs_local, length // 2, 2 * channels)


def conv_forward(patches, weight, bias_conv, gain_row, bias_row):
    recs_local, out_rows, patch_width = patches.shape
    conv_out = jnp.dot(
        patches.reshape(recs_local * out_rows, patch_width),
        weight,
        preferred_element_type=jnp.float32,
    )
    conv_out = conv_out.reshape(recs_local, out_rows, weight.shape[1]) + bias_conv
    center = jnp.mean(conv_out, axis=2, keepdims=True)
    centered = conv_out - center
    inverse = lax.rsqrt(jnp.mean(centered * centered, axis=2, keepdims=True) + EPSILON)
    normed = centered * inverse
    preact = normed * gain_row + bias_row
    activated = gelu_exact(preact).astype(jnp.bfloat16)
    return (activated, (patches, normed, preact, inverse))


def conv_backward(grad_act, weight, gain_row, stored):
    patches, normed, preact, inverse = stored
    recs_local, out_rows, patch_width = patches.shape
    grad_normed = grad_act.astype(jnp.float32) * gelu_slope(preact) * gain_row
    avg_grad = jnp.mean(grad_normed, axis=2, keepdims=True)
    avg_cross = jnp.mean(grad_normed * normed, axis=2, keepdims=True)
    grad_conv = (inverse * (grad_normed - avg_grad - normed * avg_cross)).astype(jnp.bfloat16)
    flat_patches = patches.reshape(recs_local * out_rows, patch_width)
    flat_grad = grad_conv.reshape(recs_local * out_rows, weight.shape[1])
    weight_grad = lax.dot_general(
        flat_patches, flat_grad, (((0,), (0,)), ((), ())), preferred_element_type=jnp.float32
    )
    grad_patch = lax.dot_general(
        flat_grad, weight, (((1,), (1,)), ((), ())), preferred_element_type=jnp.float32
    )
    return (weight_grad, grad_patch.reshape(recs_local, out_rows, patch_width))


def wide_input_grad(grad_patch, channels):
    recs_local, out_rows, patch_width = grad_patch.shape
    tail = grad_patch[:, :, 2 * channels :]
    incoming = passed_along(tail[:, -1:], "tm", 1)
    shifted = jnp.concatenate([incoming, tail[:, :-1]], axis=1)
    first_half = grad_patch[:, :, :channels] + shifted
    combined = jnp.concatenate([first_half, grad_patch[:, :, channels : 2 * channels]], axis=2)
    return combined.reshape(recs_local, 2 * out_rows, channels).astype(jnp.bfloat16)


def narrow_input_grad(grad_patch, channels):
    recs_local, out_rows, patch_width = grad_patch.shape
    return grad_patch.reshape(recs_local, 2 * out_rows, channels).astype(jnp.bfloat16)


def share_grad(weight_grad, factor):
    flat = (weight_grad * factor).reshape(-1)
    result = lax.psum_scatter(flat, ("dp", "tm"), scatter_dimension=0, tiled=True)
    return result


def shards(
    features,
    conv_wide,
    conv_narrow,
    conv_bias,
    norm_gain,
    norm_bias,
    proj_gain,
    proj_weight,
    proj_bias,
    upstream,
):
    recs_local, length, channels = features.shape
    tm_count = lax.axis_size("tm")
    frames_total = upstream.shape[1]
    frames_local = frames_total // tm_count
    factor = 1.0 / math.sqrt(recs_local * lax.axis_size("dp") * frames_total)
    grad_frames = lax.all_to_all(upstream, "tm", split_axis=1, concat_axis=0, tiled=True)
    first_next = passed_along(features[:, :1], "tm", -1)
    act_wide, stored_wide = conv_forward(
        wide_patches(features, first_next), conv_wide, conv_bias[0], norm_gain[0], norm_bias[0]
    )
    act_narrow, stored_narrow = conv_forward(
        narrow_patches(act_wide), conv_narrow, conv_bias[1], norm_gain[1], norm_bias[1]
    )
    widened = act_narrow.astype(jnp.float32)
    centered = widened - jnp.mean(widened, axis=2, keepdims=True)
    row_inverse = lax.rsqrt(jnp.mean(centered * centered, axis=2, keepdims=True) + EPSILON)
    unit_rows = centered * row_inverse
    normed_in = (unit_rows * proj_gain).astype(jnp.bfloat16)
    weight_heads = proj_weight.reshape(channels, HEADS, HEAD_DIM)
    projected = jnp.einsum(
        "rfc,chd->rhfd", normed_in, weight_heads, preferred_element_type=jnp.float32
    ) + proj_bias.reshape(HEADS, 1, HEAD_DIM)
    heads_local = projected.astype(jnp.bfloat16).reshape(recs_local * HEADS, frames_local, HEAD_DIM)
    attn_input = lax.all_to_all(heads_local, "tm", split_axis=0, concat_axis=1, tiled=True)
    grad_heads = grad_frames.reshape(recs_local, HEADS, frames_local, HEAD_DIM)
    grad_unit = (
        jnp.einsum("rhfd,chd->rfc", grad_heads, weight_heads, preferred_element_type=jnp.float32)
        * proj_gain
    )
    grad_last = (
        row_inverse
        * (
            grad_unit
            - jnp.mean(grad_unit, axis=2, keepdims=True)
            - unit_rows * jnp.mean(grad_unit * unit_rows, axis=2, keepdims=True)
        )
    ).astype(jnp.bfloat16)
    weight_narrow, patch_narrow = conv_backward(grad_last, conv_narrow, norm_gain[1], stored_narrow)
    grad_conv_narrow = share_grad(weight_narrow, factor)
    grad_first = narrow_input_grad(patch_narrow, channels)
    weight_wide, patch_wide = conv_backward(grad_first, conv_wide, norm_gain[0], stored_wide)
    grad_conv_wide = share_grad(weight_wide, factor)
    feature_grad = wide_input_grad(patch_wide, channels)
    return (attn_input, feature_grad, grad_conv_wide, grad_conv_narrow)


def solution(mesh):
    in_specs = (
        P("dp", "tm", None),
        P(),
        P(),
        P(),
        P(),
        P(),
        P(),
        P(),
        P(),
        P(("dp", "tm"), None, None),
    )
    out_specs = (P(("dp", "tm"), None, None), P("dp", "tm", None), P(("dp", "tm")), P(("dp", "tm")))
    return jax.shard_map(shards, mesh=mesh, in_specs=in_specs, out_specs=out_specs, check_vma=False)
```

profile of v0, /device:TPU:0, one launch (start us, length us, event | category | flops | bytes accessed | tf_op | source)
XLA Modules:
  0.0 249.9 jit_solution(17104895292761374461)
XLA Ops:
  7.2 0.0 copy-start
  7.2 1.4 slice.43
  8.6 1.4 collective-permute-start
  10.0 3.7 %copy.26 = bf16[2,2048,120]{2,0,1:T(2,128)(2,1)} copy(bf16[2,2048,120]{1,2,0:T(8,128)(2,1)} %param.19) | data formatting | bytes 1966080 | tf_op args[9]
  13.7 9.0 %all-to-all-start.1 = ((bf16[2,2048,120]{2,0,1:T(2,128)(2,1)}), bf16[2,2048,120]{2,0,1:T(2,128)(2,1)}, u32[]{:S(2)}, u32[]{:S(2)}) async-start(bf16[2,2048,120]{2,0,1:T(2,128)(2,1)} %copy.26), calls=%async_computation.1 | async-start | bytes 2097152 | tf_op jit(solution)/shard_map/all_to_all | solution.py:118
  22.7 0.0 all-reduce.5.cloned.1.call-start
  22.7 0.6 fusion.40
  23.3 0.0 copy-done.21
  23.3 0.6 fusion.41
  23.9 0.6 fusion.42
  24.5 2.2 reshape.279
  26.7 2.0 slice.54
  28.7 2.3 copy.24
  31.0 0.8 add.125
  31.8 0.0 collective-permute-done
  31.8 0.0 copy-done
  31.8 2.4 fusion.43
  34.3 0.2 multiply_reduce_fusion.1
  34.5 0.4 multiply_convert_fusion.1
  34.9 1.0 copy.23
  35.9 2.0 reshape_reshape.2
  37.9 1.9 fusion.44
  39.8 0.0 copy-start.12
  39.8 0.2 multiply_reduce_fusion.3
  40.1 0.3 convert_reduce_fusion
  40.4 0.2 fusion.21
  40.6 7.8 %all-to-all-done.1 = bf16[2,2048,120]{2,0,1:T(2,128)(2,1)} async-done(((bf16[2,2048,120]{2,0,1:T(2,128)(2,1)}), bf16[2,2048,120]{2,0,1:T(2,128)(2,1)}, u32[]{:S(2)}, u32[]{:S(2)}) %all-to-all-start.1) | async-done | bytes 983072 | tf_op jit(solution)/shard_map/all_to_all | solution.py:118
  48.4 3.6 %copy.27 = bf16[2,8,256,120]{2,3,0,1:T(8,128)(2,1)} copy(bf16[2,8,256,120]{3,0,2,1:T(2,128)(2,1)} %bitcast.16) | data formatting | bytes 1966080 | tf_op jit(solution)/shard_map/all_to_all | solution.py:118
  52.0 2.7 %fusion.37 = (f32[256]{0:T(256)S(1)}, f32[256]{0:T(256)S(1)}, f32[256,512]{1,0:T(8,128)S(1)}) fusion(f32[256]{0:T(256)S(1)} %add_rsqrt_fusion.1, f32[256]{0:T(256)S(1)} %broadcast_multiply_fusion.7, bf16[256,512]{1,0:T(8,128)(2,1)S(1)} %get-tuple-element.15, f32[512]{0:T(512)S(1)} %copy-done.12, bf16[16,256,120]{1,2,0:T(8,128)(2,1)} %bitcast.62, ...), kind=kOutput, calls=%fused_computation.78 | convolution fusion | flops 504233472 | bytes 3741696 | tf_op jit(solution)/shard_map/rhfd,chd->rfc/dot_general | solution.py:139
  54.7 0.6 fusion.36
  55.4 0.2 multiply_convert_fusion.2
  55.6 0.3 copy-done.6
  55.9 1.4 fusion.1
  57.4 1.8 multiply_bitcast_fusion
  59.2 2.4 reshape.287
  61.6 2.5 %copy.28 = f32[512,512]{0,1:T(8,128)} copy(f32[512,512]{1,0:T(8,128)} %reshape.287) | data formatting | bytes 2097152 | tf_op jit(solution)/shard_map/convert_element_type | solution.py:65
  64.1 2.0 fusion.35
  66.1 0.0 copy-start.7
  66.2 0.3 multiply_convert_fusion
  66.5 0.8 copy-done.9
  67.3 0.1 copy-done.7
  67.4 0.3 copy-done.11
  67.7 1.7 fusion
  69.4 2.5 copy.30
  71.9 1.9 copy.31
  73.9 0.0 all-reduce.5.cloned.1.call-update
  73.9 1.5 copy-done.3
  75.4 1.9 fusion.28
  77.4 1.3 fusion.10
  78.6 4.2 %all-to-all-start = ((bf16[16,256,120]{1,2,0:T(8,128)(2,1)}), bf16[16,256,120]{1,2,0:T(8,128)(2,1)}, u32[]{:S(2)}, u32[]{:S(2)}) async-start(bf16[16,256,120]{1,2,0:T(8,128)(2,1)} %fusion.10), calls=%async_computation | async-start | bytes 1966080 | tf_op jit(solution)/shard_map/all_to_all | solution.py:136
  82.9 1.0 convolution_bitcast_fusion
  83.9 1.7 copy-done.8
  85.6 3.8 %collective-permute-start.1 = (f32[1,1,512]{2,1,0:T(1,128)S(1)}, f32[1,1,512]{2,1,0:T(1,128)S(1)}, u32[]{:S(2)}, u32[]{:S(2)}) collective-permute-start(f32[1,1,512]{2,1,0:T(1,128)S(1)} %slice.56), channel_id=1, source_target_pairs={{0,1},{1,2},{2,3},{3,4},{4,5},{5,6},{6,7},{8,9},{9,10},{10,11},{11... | collective-permute-start | bytes 6152 | tf_op jit(solution)/shard_map/ppermute | solution.py:20
  89.4 1.3 slice.57
  90.7 1.3 slice.63
  92.0 26.2 %all-to-all-done = bf16[16,256,120]{1,2,0:T(8,128)(2,1)} async-done(((bf16[16,256,120]{1,2,0:T(8,128)(2,1)}), bf16[16,256,120]{1,2,0:T(8,128)(2,1)}, u32[]{:S(2)}, u32[]{:S(2)}) %all-to-all-start) | async-done | bytes 983072 | tf_op jit(solution)/shard_map/all_to_all | solution.py:136
  118.3 2.3 copy.29
  120.5 0.0 collective-permute-done.1
  120.5 1.5 fusion.9
  122.0 0.1 pad_maximum_fusion
  122.2 1.2 convert_element_type.75
  123.3 116.7 %all-reduce.5.cloned.1.call-done = (f32[786432]{0:T(1024)}, f32[524288]{0:T(1024)}) async-done(((f32[786432]{0:T(1024)}, f32[524288]{0:T(1024)}), (f32[786432]{0:T(1024)}, f32[524288]{0:T(1024)})) %all-reduce.5.cloned.1.call-update) | async-done | bytes 5242896
  240.0 1.5 dynamic-slice
  241.6 1.5 dynamic-slice.1
  (47 shorter events, 0.1 us)
Async XLA Ops:
  7.2 24.6 %copy-start = (bf16[1536,512]{1,0:T(8,128)(2,1)S(1)}, bf16[1536,512]{1,0:T(8,128)(2,1)}, u32[]{:S(2)}) copy-start(bf16[1536,512]{1,0:T(8,128)(2,1)} %param.11) | copy-start | bytes 4718596
  8.6 14.2 %copy-start.20 = (f32[2,512]{1,0:T(2,128)S(1)}, f32[2,512]{1,0:T(2,128)}, u32[]{:S(2)}) copy-start(f32[2,512]{1,0:T(2,128)} %param.13) | copy-start | bytes 12292
  8.6 14.8 %copy-start.21 = (f32[2,512]{1,0:T(2,128)S(1)}, f32[2,512]{1,0:T(2,128)}, u32[]{:S(2)}) copy-start(f32[2,512]{1,0:T(2,128)} %param.14) | copy-start | bytes 12292
  8.6 15.4 %copy-start.22 = (f32[2,512]{1,0:T(2,128)S(1)}, f32[2,512]{1,0:T(2,128)}, u32[]{:S(2)}) copy-start(f32[2,512]{1,0:T(2,128)} %param.15) | copy-start | bytes 12292
  8.6 23.2 %collective-permute-start = (bf16[1,1,512]{2,1,0:T(2,128)(2,1)}, bf16[1,1,512]{2,1,0:T(2,128)(2,1)}, u32[]{:S(2)}, u32[]{:S(2)}) collective-permute-start(bf16[1,1,512]{2,1,0:T(2,128)(2,1)} %slice.43), channel_id=1, source_target_pairs={{1,0},{2,1},{3,2},{4,3},{5,4},{6,5},{7,6},{9,8},{10,9},{11,10},{12... | collective-permute-start | bytes 3080 | tf_op jit(solution)/shard_map/ppermute | solution.py:20
  13.7 34.7 %all-to-all-start.1 = ((bf16[2,2048,120]{2,0,1:T(2,128)(2,1)}), bf16[2,2048,120]{2,0,1:T(2,128)(2,1)}, u32[]{:S(2)}, u32[]{:S(2)}) async-start(bf16[2,2048,120]{2,0,1:T(2,128)(2,1)} %copy.26), calls=%async_computation.1 | async-start | bytes 2097152 | tf_op jit(solution)/shard_map/all_to_all | solution.py:118
  22.7 6.0 %copy-start.2 = (bf16[512,1920]{1,0:T(8,128)(2,1)S(1)}, bf16[512,1920]{1,0:T(8,128)(2,1)}, u32[]{:S(2)}) copy-start(bf16[512,1920]{1,0:T(8,128)(2,1)} %param.17) | copy-start | bytes 5898244
  22.7 217.3 %all-reduce.5.cloned.1.call-start = ((), (), s32[]{:S(2)}) async-start(), calls=%async_computation.2 | async-start | bytes 10485760
  23.9 10.5 %copy-start.13 = (f32[1,512]{1,0:T(1,128)}, f32[1,512]{1,0:T(1,128)S(1)}, u32[]{:S(2)}) copy-start(f32[1,512]{1,0:T(1,128)S(1)} %get-tuple-element.18) | copy-start | bytes 6148
  24.5 10.0 %copy-start.15 = (f32[1,512]{1,0:T(1,128)}, f32[1,512]{1,0:T(1,128)S(1)}, u32[]{:S(2)}) copy-start(f32[1,512]{1,0:T(1,128)S(1)} %get-tuple-element.20) | copy-start | bytes 6148
  34.5 3.5 %copy-start.19 = (f32[1,512]{1,0:T(1,128)S(1)}, f32[1,512]{1,0:T(1,128)}, u32[]{:S(2)}) copy-start(f32[1,512]{1,0:T(1,128)} %get-tuple-element.16) | copy-start | bytes 6148
  35.9 4.2 %copy-start.17 = (f32[1,512]{1,0:T(1,128)S(1)}, f32[1,512]{1,0:T(1,128)}, u32[]{:S(2)}) copy-start(f32[1,512]{1,0:T(1,128)} %get-tuple-element.19) | copy-start | bytes 6148
  35.9 4.2 %copy-start.18 = (f32[1,512]{1,0:T(1,128)S(1)}, f32[1,512]{1,0:T(1,128)}, u32[]{:S(2)}) copy-start(f32[1,512]{1,0:T(1,128)} %get-tuple-element.21) | copy-start | bytes 6148
  39.8 12.2 %copy-start.12 = (f32[512]{0:T(512)S(1)}, f32[512]{0:T(512)}, u32[]{:S(2)}) copy-start(f32[512]{0:T(512)} %param.16) | copy-start | bytes 6148
  40.4 14.3 %copy-start.4 = (bf16[256,512]{1,0:T(8,128)(2,1)}, bf16[256,512]{1,0:T(8,128)(2,1)S(1)}, u32[]{:S(2)}) copy-start(bf16[256,512]{1,0:T(8,128)(2,1)S(1)} %get-tuple-element.15) | copy-start | bytes 786436
  54.7 1.2 copy-start.6
  55.4 2.0 copy-start.5
  59.2 4.9 %copy-start.14 = (f32[1,512]{1,0:T(1,128)S(1)}, f32[1,512]{1,0:T(1,128)}, u32[]{:S(2)}) copy-start(f32[1,512]{1,0:T(1,128)} %copy-done.13) | copy-start | bytes 6148
  59.2 4.9 %copy-start.16 = (f32[1,512]{1,0:T(1,128)S(1)}, f32[1,512]{1,0:T(1,128)}, u32[]{:S(2)}) copy-start(f32[1,512]{1,0:T(1,128)} %copy-done.15) | copy-start | bytes 6148
  66.1 1.2 copy-start.7
  66.1 1.5 copy-start.11
  66.5 0.8 copy-start.9
  69.4 2.5 %copy-start.1 = (f32[128,4,8,128]{3,2,1,0:T(8,128)S(1)}, f32[128,4,8,128]{3,2,1,0:T(8,128)}, u32[]{:S(2)}) copy-start(f32[128,4,8,128]{3,2,1,0:T(8,128)} %multiply_bitcast_fusion) | copy-start | bytes 6291460
  73.9 1.5 copy-start.3
  77.4 5.5 %copy-start.10 = (bf16[512,512]{0,1:T(8,128)(2,1)S(1)}, bf16[512,512]{0,1:T(8,128)(2,1)}, u32[]{:S(2)}) copy-start(bf16[512,512]{0,1:T(8,128)(2,1)} %copy-done.9) | copy-start | bytes 1572868
  78.6 39.6 %all-to-all-start = ((bf16[16,256,120]{1,2,0:T(8,128)(2,1)}), bf16[16,256,120]{1,2,0:T(8,128)(2,1)}, u32[]{:S(2)}, u32[]{:S(2)}) async-start(bf16[16,256,120]{1,2,0:T(8,128)(2,1)} %fusion.10), calls=%async_computation | async-start | bytes 1966080 | tf_op jit(solution)/shard_map/all_to_all | solution.py:136
  83.9 1.7 copy-start.8
  85.6 34.9 %collective-permute-start.1 = (f32[1,1,512]{2,1,0:T(1,128)S(1)}, f32[1,1,512]{2,1,0:T(1,128)S(1)}, u32[]{:S(2)}, u32[]{:S(2)}) collective-permute-start(f32[1,1,512]{2,1,0:T(1,128)S(1)} %slice.56), channel_id=1, source_target_pairs={{0,1},{1,2},{2,3},{3,4},{4,5},{5,6},{6,7},{8,9},{9,10},{10,11},{11... | collective-permute-start | bytes 6152 | tf_op jit(solution)/shard_map/ppermute | solution.py:20
Sparse Core Ops, SparseCore 0:
  74.0 165.9 all-reduce.4
where the time goes:
time: 251 us; the launch traced here: 250 us
  waiting for transfers between devices  151 us (60%)
  local copies, waits for them, and re-layouts  44 us (18%)
  starting transfers between devices  18.4 us (7%)
  matrix products  15 us (6%)
  between operations  14.4 us (6%)
  other arithmetic  7.35 us (3%)
    unnamed x2, waiting for transfers between devices  117 us
    all_to_all x1, waiting for transfers between devices, shards(): lax.all_to_all(heads_local, 'tm', split_axis=0, concat_axis=1, tiled=True)  26.2 us
    unnamed x52, local copies, waits for them, and re-layouts  18.3 us
    all_to_all x1, starting transfers between devices, shards(): lax.all_to_all(upstream, 'tm', split_axis=1, concat_axis=0, tiled=True)  8.97 us
    all_to_all x1, waiting for transfers between devices, shards(): lax.all_to_all(upstream, 'tm', split_axis=1, concat_axis=0, tiled=True)  7.76 us
    ppermute x2, starting transfers between devices, passed_along(): lax.ppermute(value, axis, [(source, source + steps) for source in range(l...  5.19 us
  transfers between devices with their start and end apart: 5, of which 3 were waited for; matrix products, arithmetic and copies ran while one was open for 13% of the time, Pallas kernels for 0%

commit v1 on v0

--- a/solution.py
+++ b/solution.py
@@ -3,6 +3,8 @@
 import jax
 import jax.numpy as jnp
 from jax import lax
+from jax.experimental import pallas as pl
+from jax.experimental.pallas import tpu as pltpu
 from jax.sharding import PartitionSpec as P
 
 HEADS = 16
@@ -98,7 +100,7 @@
     return result
 
 
-def shards(
+def generic_shards(
     features,
     conv_wide,
     conv_narrow,
@@ -156,6 +158,396 @@
     return (attn_input, feature_grad, grad_conv_wide, grad_conv_narrow)
 
 
+F32 = jnp.float32
+BF16 = jnp.bfloat16
+NT = (((1,), (1,)), ((), ()))
+
+
+def dot(a, b):
+    return jnp.dot(a, b, preferred_element_type=F32)
+
+
+def dot_nt(a, b):
+    return lax.dot_general(a, b, NT, preferred_element_type=F32)
+
+
+def row_mean(values):
+    return jnp.mean(values, axis=1, keepdims=True)
+
+
+def normalized(values):
+    centered = values - row_mean(values)
+    inverse = lax.rsqrt(row_mean(centered * centered) + EPSILON)
+    return centered * inverse, inverse
+
+
+def gelu_parts(preact):
+    cumulative = 0.5 * (1.0 + lax.erf(preact * SQRT_HALF))
+    slope = cumulative + preact * (jnp.exp(-0.5 * preact * preact) * INV_ROOT_TAU)
+    return preact * cumulative, slope
+
+
+def params(limit=58):
+    return pltpu.CompilerParams(vmem_limit_bytes=limit << 20)
+
+
+def shaped(*shapes):
+    return [jax.ShapeDtypeStruct(shape, dtype) for shape, dtype in shapes]
+
+
+def move_slices(source, shape, slices, views):
+    def kernel(src, dst, sems):
+        copies = []
+        for k in range(slices):
+            from_at, to_at = views(k)
+            copies.append(pltpu.make_async_copy(src.at[from_at], dst.at[to_at], sems.at[k]))
+        for copy in copies:
+            copy.start()
+        for copy in copies:
+            copy.wait()
+
+    return pl.pallas_call(
+        kernel,
+        out_shape=jax.ShapeDtypeStruct(shape, source.dtype),
+        in_specs=[pl.BlockSpec(memory_space=pl.ANY)],
+        out_specs=pl.BlockSpec(memory_space=pl.ANY),
+        scratch_shapes=[pltpu.SemaphoreType.DMA((slices,))],
+        name="move_slices",
+    )(source)
+
+
+def spread_rows(spread, first, count):
+    lanes = [spread[lane, pl.ds(first, count, stride=4), :] for lane in range(spread.shape[0])]
+    return jnp.concatenate(lanes, axis=1)
+
+
+def put_rows(spread, first, value):
+    for lane in range(spread.shape[0]):
+        spread[lane, pl.ds(first, value.shape[0], stride=4), :] = value[:, lane * 128 : (lane + 1) * 128]
+
+
+def forward_kernel(
+    feat,
+    halo,
+    conv_wide,
+    conv_narrow,
+    conv_bias,
+    norm_gain,
+    norm_bias,
+    proj_gain,
+    proj_weight,
+    proj_bias,
+    proj_t,
+    patch_t,
+    act_t,
+    normed_w,
+    slope_w,
+    inv_w,
+    normed_n,
+    slope_n,
+    inv_n,
+    unit_out,
+    row_inv,
+    spread,
+    patches,
+):
+    frames = feat.shape[0] // 4
+    channels = feat.shape[1]
+    for lane in range(channels // 128):
+        spread[lane] = feat[:, lane * 128 : (lane + 1) * 128].astype(F32)
+    rows = [spread_rows(spread, j, frames) for j in range(4)]
+    following = pltpu.roll(rows[0], frames - 1, axis=0)
+    at_end = lax.broadcasted_iota(jnp.int32, (frames, 1), 0) == frames - 1
+    rows.append(jnp.where(at_end, halo[0:1, :].astype(F32), following))
+    rows = [row.astype(BF16) for row in rows]
+    for parity in range(2):
+        for tap in range(3):
+            piece = rows[2 * parity + tap]
+            patches[parity * frames : (parity + 1) * frames, tap * channels : (tap + 1) * channels] = piece
+            patch_t[tap * channels : (tap + 1) * channels, parity * frames : (parity + 1) * frames] = piece.T
+    conv = dot(patches[...], conv_wide[...]) + conv_bias[0:1, :]
+    normed, inverse = normalized(conv)
+    normed_w[...] = normed
+    inv_w[...] = jnp.broadcast_to(inverse, inv_w.shape)
+    act, slope = gelu_parts(normed * norm_gain[0:1, :] + norm_bias[0:1, :])
+    slope_w[...] = slope * norm_gain[0:1, :]
+    act = act.astype(BF16)
+    even, odd = act[:frames], act[frames:]
+    act_t[0:channels, :] = even.T
+    act_t[channels:, :] = odd.T
+    conv = dot(even, conv_narrow[0:channels, :]) + dot(odd, conv_narrow[channels:, :]) + conv_bias[1:2, :]
+    normed, inverse = normalized(conv)
+    normed_n[...] = normed
+    inv_n[...] = jnp.broadcast_to(inverse, inv_n.shape)
+    act, slope = gelu_parts(normed * norm_gain[1:2, :] + norm_bias[1:2, :])
+    slope_n[...] = slope * norm_gain[1:2, :]
+    unit, inverse = normalized(act.astype(BF16).astype(F32))
+    unit_out[...] = unit
+    row_inv[...] = jnp.broadcast_to(inverse, row_inv.shape)
+    normed_in = (unit * proj_gain[...]).astype(BF16)
+    projected = dot(normed_in, proj_weight[...]) + proj_bias[...]
+    proj_t[...] = projected.astype(BF16).T
+
+
+def backward_kernel(
+    factor,
+    grad_t,
+    proj_weight,
+    proj_gain,
+    conv_narrow,
+    last_tap,
+    patch_t,
+    act_t,
+    normed_w,
+    slope_w,
+    inv_w,
+    normed_n,
+    slope_n,
+    inv_n,
+    unit_in,
+    row_inv,
+    send,
+    keep,
+    grad_conv,
+    tail,
+):
+    frames, channels = unit_in.shape
+    core = lax.axis_index("dp") % 2
+    unit = unit_in[...]
+    grad_unit = dot(proj_weight[...], grad_t[...]).T * proj_gain[...]
+    grad_last = row_inv[:, 0:1] * (grad_unit - row_mean(grad_unit) - unit * row_mean(grad_unit * unit))
+    grad_normed = grad_last.astype(BF16).astype(F32) * slope_n[...]
+    normed = normed_n[...]
+    grad_narrow = (
+        inv_n[:, 0:1] * (grad_normed - row_mean(grad_normed) - normed * row_mean(grad_normed * normed))
+    ).astype(BF16)
+    grad_even = dot_nt(grad_narrow, conv_narrow[0:channels, :])
+    grad_odd = dot_nt(grad_narrow, conv_narrow[channels:, :])
+    grad_first = jnp.concatenate([grad_even, grad_odd], axis=0).astype(BF16)
+    grad_normed = grad_first.astype(F32) * slope_w[...]
+    normed = normed_w[...]
+    grad_wide = (
+        inv_w[:, 0:1] * (grad_normed - row_mean(grad_normed) - normed * row_mean(grad_normed * normed))
+    ).astype(BF16)
+    grad_conv[...] = grad_wide
+    tail[...] = dot_nt(grad_wide[2 * frames - 8 :, :], last_tap[...])
+    outer = send.shape[0]
+    inner = send.shape[1]
+    for target, owner in ((send, 1 - core), (keep, core)):
+        for block in range(outer):
+            row = 0
+            for lhs, rhs in ((patch_t, grad_wide), (act_t, grad_narrow)):
+                part = lhs.shape[0] // (2 * outer)
+                start = pl.multiple_of((2 * block + owner) * part, part)
+                value = (dot(lhs[pl.ds(start, part), :], rhs) * factor).astype(BF16)
+                each = part // inner
+                for k in range(inner):
+                    target[block, k, row : row + each, :] = value[k * each : (k + 1) * each]
+                row += each
+
+
+def input_grad_kernel(grad_conv, conv_wide, incoming, out, spread):
+    frames = grad_conv.shape[0] // 2
+    channels = grad_conv.shape[1]
+    even, odd = grad_conv[:frames, :], grad_conv[frames:, :]
+    taps = [conv_wide[tap * channels : (tap + 1) * channels, :] for tap in range(3)]
+    shifted = pltpu.roll(dot_nt(odd, taps[2]), 1, axis=0)
+    at_start = lax.broadcasted_iota(jnp.int32, (frames, 1), 0) == 0
+    shifted = jnp.where(at_start, incoming[7:8, :], shifted)
+    put_rows(spread, 0, dot_nt(even, taps[0]) + shifted)
+    put_rows(spread, 1, dot_nt(even, taps[1]))
+    put_rows(spread, 2, dot_nt(even, taps[2]) + dot_nt(odd, taps[0]))
+    put_rows(spread, 3, dot_nt(odd, taps[1]))
+    for lane in range(channels // 128):
+        out[:, lane * 128 : (lane + 1) * 128] = spread[lane].astype(BF16)
+
+
+def first_sum_kernel(keep, received, *outs):
+    y = lax.axis_index("dp") // 2
+    x = lax.axis_index("tm") % 2
+    inner = keep.shape[1] // 2
+    for flip, out in enumerate(outs):
+        block = y ^ (flip // 2)
+        lane = x ^ (flip % 2)
+        for z in range(inner):
+            at = 2 * z + lane
+            out[z] = (keep[block, at].astype(F32) + received[block, at].astype(F32)).astype(BF16)
+
+
+def second_sum_kernel(a, b, c, d, *outs):
+    z = lax.axis_index("tm") // 2
+    for flip, out in enumerate(outs):
+        at = z ^ flip
+        total = (a[at].astype(F32) + b[at].astype(F32)) + (c[at].astype(F32) + d[at].astype(F32))
+        out[...] = total.astype(BF16)
+
+
+def last_sum_kernel(wide_rows, a, b, c, d, wide, narrow):
+    total = (a[...].astype(F32) + b[...].astype(F32)) + (c[...].astype(F32) + d[...].astype(F32))
+    rows, channels = total.shape
+    pieces = channels // 128
+    for p in range(pieces):
+        lanes = total[:, p * 128 : (p + 1) * 128]
+        wide[pl.ds(p, wide_rows, stride=pieces), :] = lanes[:wide_rows]
+        narrow[pl.ds(p, rows - wide_rows, stride=pieces), :] = lanes[wide_rows:]
+
+
+def flipped(dy, dc, dz, dx):
+    dp, tm = lax.axis_size("dp"), lax.axis_size("tm")
+    change_dp, change_tm = 2 * dy + dc, 2 * dz + dx
+    return [
+        (p * tm + t, (p ^ change_dp) * tm + (t ^ change_tm)) for p in range(dp) for t in range(tm)
+    ]
+
+
+def swap(value, dy, dc, dz, dx):
+    return lax.ppermute(value, ("dp", "tm"), flipped(dy, dc, dz, dx))
+
+
+def shards(
+    features,
+    conv_wide,
+    conv_narrow,
+    conv_bias,
+    norm_gain,
+    norm_bias,
+    proj_gain,
+    proj_weight,
+    proj_bias,
+    upstream,
+):
+    dp, tm = lax.axis_size("dp"), lax.axis_size("tm")
+    recs_local, length, channels = features.shape
+    pairs, frames_total, depth = upstream.shape
+    frames = frames_total // tm
+    if not (dp == 4 and tm == 8 and recs_local == 1 and frames % 128 == 0 and pairs * tm == HEADS):
+        return generic_shards(
+            features,
+            conv_wide,
+            conv_narrow,
+            conv_bias,
+            norm_gain,
+            norm_bias,
+            proj_gain,
+            proj_weight,
+            proj_bias,
+            upstream,
+        )
+    width = HEADS * depth
+    factor = 1.0 / math.sqrt(recs_local * dp * frames_total)
+    ups = upstream.transpose(0, 2, 1)
+    packed = move_slices(
+        ups,
+        (tm, pairs, depth, frames),
+        tm,
+        lambda k: ((slice(None), slice(None), pl.ds(k * frames, frames)), k),
+    )
+    grad_t = lax.all_to_all(
+        packed.reshape(tm, pairs * depth, frames), "tm", split_axis=0, concat_axis=0, tiled=True
+    ).reshape(width, frames)
+    signal = features.reshape(length, channels)
+    halo = passed_along(signal[:8], "tm", -1)
+    wide_rows = 2 * frames
+    saved = shaped(
+        ((3 * channels, wide_rows), BF16),
+        ((2 * channels, frames), BF16),
+        ((wide_rows, channels), F32),
+        ((wide_rows, channels), F32),
+        ((wide_rows, 128), F32),
+        ((frames, channels), F32),
+        ((frames, channels), F32),
+        ((frames, 128), F32),
+        ((frames, channels), F32),
+        ((frames, 128), F32),
+    )
+    proj_t, *stored = pl.pallas_call(
+        forward_kernel,
+        out_shape=shaped(((width, frames), BF16)) + saved,
+        scratch_shapes=[pltpu.VMEM((channels // 128, length, 128), F32), pltpu.VMEM((wide_rows, 3 * channels), BF16)],
+        compiler_params=params(),
+        name="forward",
+    )(
+        signal,
+        halo,
+        conv_wide,
+        conv_narrow,
+        conv_bias,
+        norm_gain,
+        norm_bias,
+        proj_gain.reshape(1, channels),
+        proj_weight,
+        proj_bias.reshape(1, width),
+    )
+    proj_t, grad_t = lax.optimization_barrier((proj_t, grad_t))
+    outer, inner = dp // 2, tm
+    part_rows = 5 * channels // (dp * tm)
+    part = ((outer, inner, part_rows, channels), BF16)
+    send, keep, grad_conv, tail = pl.pallas_call(
+        lambda *refs: backward_kernel(factor, *refs),
+        out_shape=shaped(part, part, ((wide_rows, channels), BF16), ((8, channels), F32)),
+        compiler_params=params(),
+        name="backward",
+    )(
+        grad_t,
+        proj_weight,
+        proj_gain.reshape(1, channels),
+        conv_narrow,
+        conv_wide[2 * channels :],
+        *stored,
+    )
+    received = swap(send, 0, 1, 0, 0)
+    heads = lax.all_to_all(
+        proj_t.reshape(tm, pairs * depth, frames), "tm", split_axis=0, concat_axis=0, tiled=True
+    )
+    attn_t = move_slices(
+        heads.reshape(tm, pairs, depth, frames),
+        (pairs, depth, frames_total),
+        tm,
+        lambda k: (k, (slice(None), slice(None), pl.ds(k * frames, frames))),
+    )
+    attn_input = attn_t.transpose(0, 2, 1)
+    incoming = passed_along(tail, "tm", 1)
+    feature_grad = pl.pallas_call(
+        input_grad_kernel,
+        out_shape=jax.ShapeDtypeStruct((length, channels), BF16),
+        scratch_shapes=[pltpu.VMEM((channels // 128, length, 128), F32)],
+        compiler_params=params(),
+        name="input_grad",
+    )(grad_conv, conv_wide, incoming)
+    plane = ((tm // 2, part_rows, channels), BF16)
+    own, *outgoing = pl.pallas_call(
+        first_sum_kernel,
+        out_shape=shaped(plane, plane, plane, plane),
+        compiler_params=params(),
+        name="first_sum",
+    )(keep, received)
+    arrived = [swap(value, k // 2, 0, 0, k % 2) for k, value in enumerate(outgoing, 1)]
+    piece = ((part_rows, channels), BF16)
+    own, *outgoing = pl.pallas_call(
+        second_sum_kernel,
+        out_shape=shaped(piece, piece, piece, piece),
+        compiler_params=params(),
+        name="second_sum",
+    )(own, *arrived)
+    arrived = [swap(value, 0, 0, k, 0) for k, value in enumerate(outgoing, 1)]
+    own_wide = 3 * channels // (dp * tm)
+    wide, narrow = pl.pallas_call(
+        lambda *refs: last_sum_kernel(own_wide, *refs),
+        out_shape=shaped(
+            ((own_wide * channels // 128, 128), F32),
+            (((part_rows - own_wide) * channels // 128, 128), F32),
+        ),
+        compiler_params=params(),
+        name="last_sum",
+    )(own, *arrived)
+    return (
+        attn_input,
+        feature_grad.reshape(recs_local, length, channels),
+        wide.reshape(-1),
+        narrow.reshape(-1),
+    )
+
+
 def solution(mesh):
     in_specs = (
         P("dp", "tm", None),

time: 251 us -> 166 us (0.66)
  waiting for transfers between devices: 151 us -> 34.2 us
  Pallas kernels: 0 us -> 89.5 us
  local copies, waits for them, and re-layouts: 44 us -> 8.79 us
  matrix products: 15 us -> 0 us
  between operations: 14.4 us -> 0.77 us
  starting transfers between devices: 18.4 us -> 29.6 us
  other arithmetic: 7.35 us -> 0 us
    unnamed x2 -> x0, waiting for transfers between devices: 117 us -> none
    pallas_call x0 -> x8, Pallas kernels: none -> 89.5 us  [the longest x2 61.9 us: move_slices(): pl.pallas_call(kernel, out_shape=jax.ShapeDtypeStruct(shape, source.dtype...]
    all_to_all x2, waiting for transfers between devices: 34 us -> 9.26 us  [the longest x1 9.26 us: shards(): lax.all_to_all(packed.reshape(tm, pairs * depth, frames), 'tm', split_axi...]
    ppermute x0 -> x7, waiting for transfers between devices: none -> 21.2 us  [swap(): return lax.ppermute(value, ('dp', 'tm'), flipped(dy, dc, dz, dx))]
    dot_general x7 -> x0, matrix products: 13 us -> none  [the longest x2 4.34 us: conv_forward(): jnp.dot(patches.reshape(recs_local * out_rows, patch_width), weight, pref...]
    unnamed x52 -> x26, local copies, waits for them, and re-layouts: 18.3 us -> 5.62 us
    ppermute x0 -> x7, starting transfers between devices: none -> 8.35 us  [swap(): return lax.ppermute(value, ('dp', 'tm'), flipped(dy, dc, dz, dx))]
    convert_element_type x4 -> x0, local copies, waits for them, and re-layouts: 7.12 us -> none  [the longest x2 4.94 us: conv_backward(): grad_normed = grad_act.astype(jnp.float32) * gelu_slope(preact) * gain_row]
  transfers between devices with their start and end apart: 5 -> 11, of which waited for: 3 -> 5; matrix products, arithmetic and copies ran while one was open for 13% -> 2% of each run, Pallas kernels for 0% -> 29%
where the time goes in v1:
time: 166 us; the launch traced here: 163 us
  Pallas kernels  89.5 us (54%)
  waiting for transfers between devices  34.2 us (21%)
  starting transfers between devices  29.6 us (18%)
  local copies, waits for them, and re-layouts  8.79 us (5%)
    pallas_call x2, Pallas kernels, move_slices(): pl.pallas_call(kernel, out_shape=jax.ShapeDtypeStruct(shape, source.dtype...  61.9 us
    ppermute x7, waiting for transfers between devices, swap(): return lax.ppermute(value, ('dp', 'tm'), flipped(dy, dc, dz, dx))  21.2 us
    all_to_all x1, starting transfers between devices, shards(): lax.all_to_all(proj_t.reshape(tm, pairs * depth, frames), 'tm', split_axi...  11.3 us
    pallas_call x1, Pallas kernels, shards(): pl.pallas_call(lambda *refs: backward_kernel(factor, *refs), out_shape=sh...  9.33 us
    all_to_all x1, waiting for transfers between devices, shards(): lax.all_to_all(packed.reshape(tm, pairs * depth, frames), 'tm', split_axi...  9.26 us
    ppermute x7, starting transfers between devices, swap(): return lax.ppermute(value, ('dp', 'tm'), flipped(dy, dc, dz, dx))  8.35 us
    pallas_call x1, Pallas kernels, shards(): pl.pallas_call(forward_kernel, out_shape=shaped(((width, frames), BF16))...  7.84 us
    all_to_all x1, starting transfers between devices, shards(): lax.all_to_all(packed.reshape(tm, pairs * depth, frames), 'tm', split_axi...  7.26 us
  transfers between devices with their start and end apart: 11, of which 5 were waited for; matrix products, arithmetic and copies ran while one was open for 2% of the time, Pallas kernels for 29%

profile of v1, /device:TPU:0, one launch (start us, length us, event | category | flops | bytes accessed | tf_op | source)
XLA Modules:
  0.0 162.9 jit_solution(9056376934363998950)
XLA Ops:
  0.6 0.0 copy-start.11
  0.6 31.0 %move_slices.2 = bf16[8,2,120,256]{3,2,1,0:T(8,128)(2,1)} custom-call(bf16[2,120,2048]{2,1,0:T(8,128)(2,1)} %bitcast.18), custom_call_target="tpu_custom_call" | custom-call | tf_op jit(solution)/shard_map/move_slices/pallas_call | solution.py:209
  31.6 7.3 %all-to-all-start = ((bf16[8,240,256]{2,1,0:T(8,128)(2,1)}), bf16[8,240,256]{2,1,0:T(8,128)(2,1)S(1)}, u32[]{:S(2)}, u32[]{:S(2)}) async-start(bf16[8,240,256]{2,1,0:T(8,128)(2,1)} %bitcast.15), calls=%async_computation | async-start | bytes 1966080 | tf_op jit(solution)/shard_map/all_to_all | solution.py:445
  38.9 0.7 slice_bitcast_fusion
  39.6 1.3 collective-permute-start
  40.9 0.0 copy-done.11
  40.9 0.6 reshape.42.proj_bias
  41.5 1.9 %slice.11.refs_4_ = bf16[512,512]{1,0:T(8,128)(2,1)} slice(bf16[1536,512]{1,0:T(8,128)(2,1)} %conv_wide.3), slice={[1024:1536], [0:512]} | slice | bytes 1048576 | tf_op jit(solution)/shard_map/slice | solution.py:495
  43.3 2.3 %collective-permute-done.halo = bf16[8,512]{1,0:T(8,128)(2,1)S(1)} collective-permute-done((bf16[8,512]{1,0:T(8,128)(2,1)S(1)}, bf16[8,512]{1,0:T(8,128)(2,1)S(1)}, u32[]{:S(2)}, u32[]{:S(2)}) %collective-permute-start) | collective-permute-done | bytes 8224 | tf_op jit(solution)/shard_map/ppermute | solution.py:22
  45.6 0.0 copy-start.10
  45.6 0.6 copy-done.10
  46.2 7.8 %forward.1 = (bf16[1920,256]{1,0:T(8,128)(2,1)}, bf16[1536,512]{1,0:T(8,128)(2,1)}, bf16[1024,256]{1,0:T(8,128)(2,1)}, f32[512,512]{1,0:T(8,128)}, f32[512,512]{...) custom-call(bf16[1024,512]{1,0:T(8,128)(2,1)} %bitcast.16, ...), custom_call_target="tpu_custom_call" | custom-call | tf_op jit(solution)/shard_map/forward/pallas_call | solution.py:463
  54.1 9.3 %all-to-all-done = bf16[8,240,256]{2,1,0:T(8,128)(2,1)S(1)} async-done(((bf16[8,240,256]{2,1,0:T(8,128)(2,1)}), bf16[8,240,256]{2,1,0:T(8,128)(2,1)S(1)}, u32[]{:S(2)}, u32[]{:S(2)}) %all-to-all-start) | async-done | bytes 983072 | tf_op jit(solution)/shard_map/all_to_all | solution.py:445
  63.3 0.0 copy-start.1
  63.3 1.0 copy-done.1
  64.3 9.3 %backward.1 = (bf16[2,8,80,512]{3,2,1,0:T(8,128)(2,1)}, bf16[2,8,80,512]{3,2,1,0:T(8,128)(2,1)}, bf16[512,512]{1,0:T(8,128)(2,1)}, f32[8,512]{1,0:T(8,128)}) custom-call(bf16[1920,256]{1,0:T(8,128)(2,1)} %bitcast.14, bf16[512,1920]{1,0:T(8,128)(2,1)} %refs_1_.1, f32[1,512]{1,0:T(1,128)} %bitcast.21, bf16[1024,512]{1,0:T(8,128)(2,1)} %refs_3_.1, ...), custom_call_target="tpu_custom_call" | custom-call | tf_op jit(solution)/shard_map/backward/pallas_call | solution.py:485
  73.6 0.0 collective-permute-start.2
  73.6 11.3 %all-to-all-start.1 = ((bf16[8,240,256]{2,1,0:T(8,128)(2,1)}), bf16[8,240,256]{2,1,0:T(8,128)(2,1)S(1)}, u32[]{:S(2)}, u32[]{:S(2)}) async-start(bf16[8,240,256]{2,1,0:T(8,128)(2,1)} %bitcast.6), calls=%async_computation.1 | async-start | bytes 1966080 | tf_op jit(solution)/shard_map/all_to_all | solution.py:499
  84.9 0.0 collective-permute-done.2.received
  84.9 0.0 copy-start.2
  84.9 1.1 copy-done.2
  86.0 0.0 copy-start.12
  86.0 3.0 %first_sum.1 = (bf16[4,80,512]{2,1,0:T(8,128)(2,1)}, bf16[4,80,512]{2,1,0:T(8,128)(2,1)}, bf16[4,80,512]{2,1,0:T(8,128)(2,1)}, bf16[4,80,512]{2,1,0:T(8,128)(2,1)}) custom-call(bf16[2,8,80,512]{3,2,1,0:T(8,128)(2,1)} %get-tuple-element.46.keep, bf16[2,8,80,512]{3,2,1,0:T(8,128)(2,1)} %copy-done.2), custom_call_target="tpu_custom_call" | custom-call | tf_op jit(solution)/shard_map/first_sum/pallas_call | solution.py:518
  89.0 2.0 %collective-permute-start.3 = (bf16[4,80,512]{2,1,0:T(8,128)(2,1)}, bf16[4,80,512]{2,1,0:T(8,128)(2,1)S(1)}, u32[]{:S(2)}, u32[]{:S(2)}) collective-permute-start(bf16[4,80,512]{2,1,0:T(8,128)(2,1)} %get-tuple-element.49), channel_id=1, source_target_pairs={{0,1},{1,0},{2,3},{3,2},{4,5},{5,4},{6,7},{7,6},{8,9},{9,8},{10,11... | collective-permute-start | bytes 983048 | tf_op jit(solution)/shard_map/ppermute | solution.py:404
  91.0 1.5 collective-permute-start.4
  92.6 0.0 collective-permute-start.5
  92.6 13.6 %collective-permute-done.3.b = bf16[4,80,512]{2,1,0:T(8,128)(2,1)S(1)} collective-permute-done((bf16[4,80,512]{2,1,0:T(8,128)(2,1)}, bf16[4,80,512]{2,1,0:T(8,128)(2,1)S(1)}, u32[]{:S(2)}, u32[]{:S(2)}) %collective-permute-start.3) | collective-permute-done | bytes 327712 | tf_op jit(solution)/shard_map/ppermute | solution.py:404
  106.2 0.0 copy-start.3
  106.2 0.0 collective-permute-done.4.c
  106.2 0.0 copy-start.4
  106.2 7.6 %collective-permute-done.5.d = bf16[4,80,512]{2,1,0:T(8,128)(2,1)S(1)} collective-permute-done((bf16[4,80,512]{2,1,0:T(8,128)(2,1)}, bf16[4,80,512]{2,1,0:T(8,128)(2,1)S(1)}, u32[]{:S(2)}, u32[]{:S(2)}) %collective-permute-start.5) | collective-permute-done | bytes 327712 | tf_op jit(solution)/shard_map/ppermute | solution.py:404
  113.8 0.0 copy-start.5
  113.8 0.0 copy-done.3
  113.8 0.0 copy-done.4
  113.8 0.7 copy-done.5
  114.5 2.1 %second_sum.1 = (bf16[80,512]{1,0:T(8,128)(2,1)}, bf16[80,512]{1,0:T(8,128)(2,1)}, bf16[80,512]{1,0:T(8,128)(2,1)}, bf16[80,512]{1,0:T(8,128)(2,1)}) custom-call(bf16[4,80,512]{2,1,0:T(8,128)(2,1)} %get-tuple-element.48.a, bf16[4,80,512]{2,1,0:T(8,128)(2,1)} %copy-done.3, bf16[4,80,512]{2,1,0:T(8,128)(2,1)} %copy-done.4, bf16[4,80,512]{2,1,0:T(8,128)(2,1)} %copy-done.5), custom_call_target="tpu_custom_call" | custom-call | tf_op jit(solution)/shard_map/second_sum/pallas_call | solution.py:526
  116.6 1.1 collective-permute-start.6
  117.7 3.6 %collective-permute-start.7 = (bf16[80,512]{1,0:T(8,128)(2,1)}, bf16[80,512]{1,0:T(8,128)(2,1)S(1)}, u32[]{:S(2)}, u32[]{:S(2)}) collective-permute-start(bf16[80,512]{1,0:T(8,128)(2,1)} %get-tuple-element.54), channel_id=1, source_target_pairs={{0,4},{1,5},{2,6},{3,7},{4,0},{5,1},{6,2},{7,3},{8,12},{9,13},{10,... | collective-permute-start | bytes 245768 | tf_op jit(solution)/shard_map/ppermute | solution.py:404
  121.4 0.0 collective-permute-start.8
  121.4 0.0 copy-done.12
  121.4 1.5 collective-permute-start.1
  122.9 1.4 collective-permute-done.1.incoming
  124.3 0.0 copy-start.9
  124.3 0.6 copy-done.9
  124.9 3.7 %input_grad.1 = bf16[1024,512]{1,0:T(8,128)(2,1)} custom-call(bf16[512,512]{1,0:T(8,128)(2,1)} %get-tuple-element.44.grad_conv, bf16[1536,512]{1,0:T(8,128)(2,1)} %conv_wide.3, f32[8,512]{1,0:T(8,128)} %copy-done.9), custom_call_target="tpu_custom_call" | custom-call | tf_op jit(solution)/shard_map/input_grad/pallas_call | solution.py:510
  128.6 0.0 all-to-all-done.1
  128.6 0.0 copy-start
  128.6 1.0 copy-done
  129.6 31.0 %move_slices.3 = bf16[2,120,2048]{2,1,0:T(8,128)(2,1)} custom-call(bf16[8,2,120,256]{3,2,1,0:T(8,128)(2,1)} %bitcast.13), custom_call_target="tpu_custom_call" | custom-call | tf_op jit(solution)/shard_map/move_slices/pallas_call | solution.py:209
  160.5 0.0 collective-permute-done.6.refs_1_
  160.5 0.0 copy-start.6
  160.5 0.0 collective-permute-done.7.refs_2_
  160.5 0.0 copy-start.7
  160.6 0.0 collective-permute-done.8.refs_3_
  160.6 0.0 copy-start.8
  160.6 0.6 copy-done.6
  161.2 0.0 copy-done.7
  161.2 0.0 copy-done.8
  161.2 1.7 %last_sum.1 = (f32[192,128]{1,0:T(8,128)}, f32[128,128]{1,0:T(8,128)}) custom-call(bf16[80,512]{1,0:T(8,128)(2,1)} %get-tuple-element.52.refs_0_, bf16[80,512]{1,0:T(8,128)(2,1)} %copy-done.6, bf16[80,512]{1,0:T(8,128)(2,1)} %copy-done.7, bf16[80,512]{1,0:T(8,128)(2,1)} %copy-done.8), custom_call_target="tpu_custom_call" | custom-call | tf_op jit(solution)/shard_map/last_sum/pallas_call | solution.py:534
Async XLA Ops:
  0.6 40.2 %copy-start.11 = (f32[1920]{0:T(1024)S(1)}, f32[1920]{0:T(1024)}, u32[]{:S(2)}) copy-start(f32[1920]{0:T(1024)} %param.18) | copy-start | bytes 23044
  31.6 31.7 %all-to-all-start = ((bf16[8,240,256]{2,1,0:T(8,128)(2,1)}), bf16[8,240,256]{2,1,0:T(8,128)(2,1)S(1)}, u32[]{:S(2)}, u32[]{:S(2)}) async-start(bf16[8,240,256]{2,1,0:T(8,128)(2,1)} %bitcast.15), calls=%async_computation | async-start | bytes 1966080 | tf_op jit(solution)/shard_map/all_to_all | solution.py:445
  39.6 6.1 %collective-permute-start = (bf16[8,512]{1,0:T(8,128)(2,1)S(1)}, bf16[8,512]{1,0:T(8,128)(2,1)S(1)}, u32[]{:S(2)}, u32[]{:S(2)}) collective-permute-start(bf16[8,512]{1,0:T(8,128)(2,1)S(1)} %slice_bitcast_fusion), channel_id=1, source_target_pairs={{1,0},{2,1},{3,2},{4,3},{5,4},{6,5},{7,6},{9,8},{10,9},{11,10},{12... | collective-permute-start | bytes 24584 | tf_op jit(solution)/shard_map/ppermute | solution.py:22
  45.6 0.6 copy-start.10
  63.3 1.0 copy-start.1
  73.6 11.3 %collective-permute-start.2 = (bf16[2,8,80,512]{3,2,1,0:T(8,128)(2,1)}, bf16[2,8,80,512]{3,2,1,0:T(8,128)(2,1)S(1)}, u32[]{:S(2)}, u32[]{:S(2)}) collective-permute-start(bf16[2,8,80,512]{3,2,1,0:T(8,128)(2,1)} %get-tuple-element.47), channel_id=1, source_target_pairs={{0,8},{1,9},{2,10},{3,11},{4,12},{5,13},{6,14},{7,15},{8,0},{9,1},... | collective-permute-start | bytes 3932168 | tf_op jit(solution)/shard_map/ppermute | solution.py:404
  73.6 54.9 %all-to-all-start.1 = ((bf16[8,240,256]{2,1,0:T(8,128)(2,1)}), bf16[8,240,256]{2,1,0:T(8,128)(2,1)S(1)}, u32[]{:S(2)}, u32[]{:S(2)}) async-start(bf16[8,240,256]{2,1,0:T(8,128)(2,1)} %bitcast.6), calls=%async_computation.1 | async-start | bytes 1966080 | tf_op jit(solution)/shard_map/all_to_all | solution.py:499
  84.9 1.1 copy-start.2
  86.0 35.4 %copy-start.12 = (f32[8,512]{1,0:T(8,128)S(1)}, f32[8,512]{1,0:T(8,128)}, u32[]{:S(2)}) copy-start(f32[8,512]{1,0:T(8,128)} %get-tuple-element.45) | copy-start | bytes 49156
  89.0 17.2 %collective-permute-start.3 = (bf16[4,80,512]{2,1,0:T(8,128)(2,1)}, bf16[4,80,512]{2,1,0:T(8,128)(2,1)S(1)}, u32[]{:S(2)}, u32[]{:S(2)}) collective-permute-start(bf16[4,80,512]{2,1,0:T(8,128)(2,1)} %get-tuple-element.49), channel_id=1, source_target_pairs={{0,1},{1,0},{2,3},{3,2},{4,5},{5,4},{6,7},{7,6},{8,9},{9,8},{10,11... | collective-permute-start | bytes 983048 | tf_op jit(solution)/shard_map/ppermute | solution.py:404
  91.0 15.1 %collective-permute-start.4 = (bf16[4,80,512]{2,1,0:T(8,128)(2,1)}, bf16[4,80,512]{2,1,0:T(8,128)(2,1)S(1)}, u32[]{:S(2)}, u32[]{:S(2)}) collective-permute-start(bf16[4,80,512]{2,1,0:T(8,128)(2,1)} %get-tuple-element.50), channel_id=1, source_target_pairs={{0,16},{1,17},{2,18},{3,19},{4,20},{5,21},{6,22},{7,23},{8,24},{9,... | collective-permute-start | bytes 983048 | tf_op jit(solution)/shard_map/ppermute | solution.py:404
  92.6 21.2 %collective-permute-start.5 = (bf16[4,80,512]{2,1,0:T(8,128)(2,1)}, bf16[4,80,512]{2,1,0:T(8,128)(2,1)S(1)}, u32[]{:S(2)}, u32[]{:S(2)}) collective-permute-start(bf16[4,80,512]{2,1,0:T(8,128)(2,1)} %get-tuple-element.51), channel_id=1, source_target_pairs={{0,17},{1,16},{2,19},{3,18},{4,21},{5,20},{6,23},{7,22},{8,25},{9,... | collective-permute-start | bytes 983048 | tf_op jit(solution)/shard_map/ppermute | solution.py:404
  106.2 7.6 %copy-start.3 = (bf16[4,80,512]{2,1,0:T(8,128)(2,1)}, bf16[4,80,512]{2,1,0:T(8,128)(2,1)S(1)}, u32[]{:S(2)}) copy-start(bf16[4,80,512]{2,1,0:T(8,128)(2,1)S(1)} %collective-permute-done.3.b) | copy-start | bytes 983044
  106.2 7.6 %copy-start.4 = (bf16[4,80,512]{2,1,0:T(8,128)(2,1)}, bf16[4,80,512]{2,1,0:T(8,128)(2,1)S(1)}, u32[]{:S(2)}) copy-start(bf16[4,80,512]{2,1,0:T(8,128)(2,1)S(1)} %collective-permute-done.4.c) | copy-start | bytes 983044
  113.8 0.7 copy-start.5
  116.6 43.9 %collective-permute-start.6 = (bf16[80,512]{1,0:T(8,128)(2,1)}, bf16[80,512]{1,0:T(8,128)(2,1)S(1)}, u32[]{:S(2)}, u32[]{:S(2)}) collective-permute-start(bf16[80,512]{1,0:T(8,128)(2,1)} %get-tuple-element.53), channel_id=1, source_target_pairs={{0,2},{1,3},{2,0},{3,1},{4,6},{5,7},{6,4},{7,5},{8,10},{9,11},{10,... | collective-permute-start | bytes 245768 | tf_op jit(solution)/shard_map/ppermute | solution.py:404
  117.7 42.8 %collective-permute-start.7 = (bf16[80,512]{1,0:T(8,128)(2,1)}, bf16[80,512]{1,0:T(8,128)(2,1)S(1)}, u32[]{:S(2)}, u32[]{:S(2)}) collective-permute-start(bf16[80,512]{1,0:T(8,128)(2,1)} %get-tuple-element.54), channel_id=1, source_target_pairs={{0,4},{1,5},{2,6},{3,7},{4,0},{5,1},{6,2},{7,3},{8,12},{9,13},{10,... | collective-permute-start | bytes 245768 | tf_op jit(solution)/shard_map/ppermute | solution.py:404
  121.4 39.2 %collective-permute-start.8 = (bf16[80,512]{1,0:T(8,128)(2,1)}, bf16[80,512]{1,0:T(8,128)(2,1)S(1)}, u32[]{:S(2)}, u32[]{:S(2)}) collective-permute-start(bf16[80,512]{1,0:T(8,128)(2,1)} %get-tuple-element.55), channel_id=1, source_target_pairs={{0,6},{1,7},{2,4},{3,5},{4,2},{5,3},{6,0},{7,1},{8,14},{9,15},{10,... | collective-permute-start | bytes 245768 | tf_op jit(solution)/shard_map/ppermute | solution.py:404
  121.4 2.9 %collective-permute-start.1 = (f32[8,512]{1,0:T(8,128)S(1)}, f32[8,512]{1,0:T(8,128)S(1)}, u32[]{:S(2)}, u32[]{:S(2)}) collective-permute-start(f32[8,512]{1,0:T(8,128)S(1)} %copy-done.12), channel_id=1, source_target_pairs={{0,1},{1,2},{2,3},{3,4},{4,5},{5,6},{6,7},{8,9},{9,10},{10,11},{11... | collective-permute-start | bytes 49160 | tf_op jit(solution)/shard_map/ppermute | solution.py:22
  124.3 0.6 copy-start.9
  128.6 1.0 copy-start
  160.5 0.6 copy-start.6
  160.5 0.7 copy-start.7
  160.6 0.6 copy-start.8

commit v2 on v0

--- a/solution.py
+++ b/solution.py
@@ -3,6 +3,8 @@
 import jax
 import jax.numpy as jnp
 from jax import lax
+from jax.experimental import pallas as pl
+from jax.experimental.pallas import tpu as pltpu
 from jax.sharding import PartitionSpec as P
 
 HEADS = 16
@@ -98,7 +100,7 @@
     return result
 
 
-def shards(
+def generic_shards(
     features,
     conv_wide,
     conv_narrow,
@@ -156,6 +158,490 @@
     return (attn_input, feature_grad, grad_conv_wide, grad_conv_narrow)
 
 
+F32 = jnp.float32
+BF16 = jnp.bfloat16
+NT = (((1,), (1,)), ((), ()))
+
+
+def dot(a, b):
+    return jnp.dot(a, b, preferred_element_type=F32)
+
+
+def dot_nt(a, b):
+    return lax.dot_general(a, b, NT, preferred_element_type=F32)
+
+
+def row_mean(values):
+    return jnp.mean(values, axis=1, keepdims=True)
+
+
+def normalized(values):
+    centered = values - row_mean(values)
+    inverse = lax.rsqrt(row_mean(centered * centered) + EPSILON)
+    return centered * inverse, inverse
+
+
+def gelu_parts(preact):
+    cumulative = 0.5 * (1.0 + lax.erf(preact * SQRT_HALF))
+    slope = cumulative + preact * (jnp.exp(-0.5 * preact * preact) * INV_ROOT_TAU)
+    return preact * cumulative, slope
+
+
+def local(kernel, operands, outs, name, limit=16, scratch=(), raw=(), raw_out=(), aliases=None, cost=1000):
+    out_shape, out_specs = [], []
+    for number, (shape, dtype, stays) in enumerate(outs):
+        out_shape.append((pltpu.VMEM if stays else pltpu.HBM)(shape, dtype))
+        out_specs.append(pl.BlockSpec(memory_space=pltpu.HBM if number in raw_out else pltpu.VMEM))
+    held = [
+        pltpu.with_memory_space_constraint(x, pltpu.HBM if k in raw else pltpu.VMEM)
+        for k, x in enumerate(operands)
+    ]
+    return pl.pallas_call(
+        kernel,
+        out_shape=out_shape,
+        in_specs=[
+            pl.BlockSpec(memory_space=pltpu.HBM if k in raw else pltpu.VMEM) for k in range(len(operands))
+        ],
+        out_specs=out_specs,
+        scratch_shapes=list(scratch),
+        input_output_aliases=aliases or {},
+        compiler_params=pltpu.CompilerParams(vmem_limit_bytes=limit << 20),
+        cost_estimate=pl.CostEstimate(flops=cost, bytes_accessed=0, transcendentals=0),
+        name=name,
+    )(*held)
+
+
+def run_copies(pairs, sems):
+    copies = [pltpu.make_async_copy(src, dst, sems.at[k]) for k, (src, dst) in enumerate(pairs)]
+    for copy in copies:
+        copy.start()
+    for copy in copies:
+        copy.wait()
+
+
+def cut_kernel(whole, *refs):
+    *parts, held, sems, out_sems = refs
+    count, width = held.shape[0], held.shape[3]
+    own = lax.axis_index("tm")
+    reads, writes = [], []
+    for k in range(count):
+        start = pl.multiple_of((own ^ k) * width, width)
+        reads.append(pltpu.make_async_copy(whole.at[:, :, pl.ds(start, width)], held.at[k], sems.at[k]))
+        writes.append(pltpu.make_async_copy(held.at[k], parts[k], out_sems.at[k]))
+    for read in reads:
+        read.start()
+    for read, write in zip(reads, writes):
+        read.wait()
+        write.start()
+    for write in writes:
+        write.wait()
+
+
+def join_kernel(parts, whole, sems):
+    width = parts.shape[3]
+    run_copies([(parts.at[k], whole.at[:, :, pl.ds(k * width, width)]) for k in range(parts.shape[0])], sems)
+
+
+class Loads:
+    def __init__(self, sources, held, sems):
+        self.pairs = [
+            (pltpu.make_async_copy(src, buf, sems.at[k]), buf) for k, (src, buf) in enumerate(zip(sources, held))
+        ]
+        for read, _ in self.pairs:
+            read.start()
+
+    def take(self, count):
+        taken, self.pairs = self.pairs[:count], self.pairs[count:]
+        for read, _ in taken:
+            read.wait()
+        return [buf for _, buf in taken]
+
+
+def spread_rows(spread, first, count):
+    lanes = [spread[lane, pl.ds(first, count, stride=4), :] for lane in range(spread.shape[0])]
+    return jnp.concatenate(lanes, axis=1)
+
+
+def put_rows(spread, first, value):
+    for lane in range(spread.shape[0]):
+        spread[lane, pl.ds(first, value.shape[0], stride=4), :] = value[:, lane * 128 : (lane + 1) * 128]
+
+
+def forward_kernel(*refs):
+    sources, outs, rest = refs[:10], refs[10:21], refs[21:]
+    *held, sems, spread, patches = rest
+    (
+        proj_t,
+        patch_t,
+        act_t,
+        normed_w,
+        slope_w,
+        inv_w,
+        normed_n,
+        slope_n,
+        inv_n,
+        unit_out,
+        row_inv,
+    ) = outs
+    loads = Loads(sources, held, sems)
+    feat, halo, conv_bias, norm_gain, norm_bias = loads.take(5)
+    frames = feat.shape[0] // 4
+    channels = feat.shape[1]
+    for lane in range(channels // 128):
+        spread[lane] = feat[:, lane * 128 : (lane + 1) * 128].astype(F32)
+    rows = [spread_rows(spread, j, frames) for j in range(4)]
+    following = pltpu.roll(rows[0], frames - 1, axis=0)
+    at_end = lax.broadcasted_iota(jnp.int32, (frames, 1), 0) == frames - 1
+    rows.append(jnp.where(at_end, halo[0:1, :].astype(F32), following))
+    rows = [row.astype(BF16) for row in rows]
+    for parity in range(2):
+        for tap in range(3):
+            piece = rows[2 * parity + tap]
+            patches[parity * frames : (parity + 1) * frames, tap * channels : (tap + 1) * channels] = piece
+            patch_t[tap * channels : (tap + 1) * channels, parity * frames : (parity + 1) * frames] = piece.T
+    (conv_wide,) = loads.take(1)
+    conv = dot(patches[...], conv_wide[...]) + conv_bias[0:1, :]
+    normed, inverse = normalized(conv)
+    normed_w[...] = normed
+    inv_w[...] = jnp.broadcast_to(inverse, inv_w.shape)
+    act, slope = gelu_parts(normed * norm_gain[0:1, :] + norm_bias[0:1, :])
+    slope_w[...] = slope * norm_gain[0:1, :]
+    act = act.astype(BF16)
+    even, odd = act[:frames], act[frames:]
+    act_t[0:channels, :] = even.T
+    act_t[channels:, :] = odd.T
+    (conv_narrow,) = loads.take(1)
+    conv = dot(even, conv_narrow[0:channels, :]) + dot(odd, conv_narrow[channels:, :]) + conv_bias[1:2, :]
+    normed, inverse = normalized(conv)
+    normed_n[...] = normed
+    inv_n[...] = jnp.broadcast_to(inverse, inv_n.shape)
+    act, slope = gelu_parts(normed * norm_gain[1:2, :] + norm_bias[1:2, :])
+    slope_n[...] = slope * norm_gain[1:2, :]
+    unit, inverse = normalized(act.astype(BF16).astype(F32))
+    unit_out[...] = unit
+    row_inv[...] = jnp.broadcast_to(inverse, row_inv.shape)
+    proj_gain, proj_bias, proj_weight = loads.take(3)
+    normed_in = (unit * proj_gain[...]).astype(BF16)
+    projected = dot(normed_in, proj_weight[...]) + proj_bias[...]
+    proj_t[...] = projected.astype(BF16).T
+
+
+def owned_rows(left, owner, outer):
+    part = left.shape[0] // (2 * outer)
+    return [left.at[pl.ds(pl.multiple_of((2 * block + owner) * part, part), part), :] for block in range(outer)]
+
+
+def weight_grad(loads, grads, factor, target):
+    outer, inner = target.shape[0], target.shape[1]
+    row = 0
+    for grad in grads:
+        for block, left in enumerate(loads.take(outer)):
+            value = (dot(left[...], grad) * factor).astype(BF16)
+            each = left.shape[0] // inner
+            for k in range(inner):
+                target[block, k, row : row + each, :] = value[k * each : (k + 1) * each]
+        row += each
+
+
+def backward_kernel(factor, *refs):
+    tm = lax.axis_size("tm")
+    count = 13 + tm
+    sources, (send, grad_conv, grad_low), rest = refs[:count], refs[count : count + 3], refs[count + 3 :]
+    *held, grad_t, sems = rest
+    outer = send.shape[0]
+    own = lax.axis_index("tm")
+    rows = sources[1].shape[0]
+    places = [grad_t.at[pl.ds(pl.multiple_of((own ^ k) * rows, rows), rows), :] for k in range(tm)]
+    other = 1 - lax.axis_index("dp") % 2
+    lefts = [rows for left in sources[-2:] for rows in owned_rows(left, other, outer)]
+    loads = Loads([*sources[:-2], *lefts], [held[0], *places, *held[1:]], sems)
+    proj_weight, *_, proj_gain = loads.take(2 + tm)
+    grad_unit = dot(proj_weight[...], grad_t[...]).T * proj_gain[...]
+    unit_in, row_inv = loads.take(2)
+    frames, channels = unit_in.shape
+    unit = unit_in[...]
+    grad_last = row_inv[:, 0:1] * (grad_unit - row_mean(grad_unit) - unit * row_mean(grad_unit * unit))
+    normed_n, slope_n, inv_n, conv_narrow = loads.take(4)
+    grad_normed = grad_last.astype(BF16).astype(F32) * slope_n[...]
+    normed = normed_n[...]
+    grad_narrow = (
+        inv_n[:, 0:1] * (grad_normed - row_mean(grad_normed) - normed * row_mean(grad_normed * normed))
+    ).astype(BF16)
+    grad_low[...] = grad_narrow
+    normed_w, slope_w, inv_w = loads.take(3)
+    for parity in range(2):
+        at = pl.ds(parity * frames, frames)
+        grad_first = dot_nt(grad_narrow, conv_narrow[parity * channels : (parity + 1) * channels, :]).astype(BF16)
+        grad_normed = grad_first.astype(F32) * slope_w[at, :]
+        normed = normed_w[at, :]
+        grad_conv[at, :] = (
+            inv_w[at, 0:1] * (grad_normed - row_mean(grad_normed) - normed * row_mean(grad_normed * normed))
+        ).astype(BF16)
+    weight_grad(loads, (grad_conv[...], grad_narrow), factor, send)
+
+
+def own_grad_kernel(factor, patch_t, act_t, conv_wide, grad_conv, grad_low, keep, tail, *rest):
+    held, sems = rest[:-1], rest[-1]
+    outer = keep.shape[0]
+    core = lax.axis_index("dp") % 2
+    lefts = [rows for left in (patch_t, act_t) for rows in owned_rows(left, core, outer)]
+    last_tap = held[-1].shape[0]
+    loads = Loads([*lefts, conv_wide.at[pl.ds(2 * last_tap, last_tap), :]], held, sems)
+    grad_wide = grad_conv[...]
+    weight_grad(loads, (grad_wide, grad_low[...]), factor, keep)
+    (tap,) = loads.take(1)
+    tail[...] = dot_nt(grad_wide[grad_wide.shape[0] - 8 :, :], tap[...])
+
+
+def input_grad_kernel(grad_conv, conv_wide, out, first_rows, spread):
+    frames = grad_conv.shape[0] // 2
+    channels = grad_conv.shape[1]
+    even, odd = grad_conv[:frames, :], grad_conv[frames:, :]
+    taps = [conv_wide[tap * channels : (tap + 1) * channels, :] for tap in range(3)]
+    shifted = pltpu.roll(dot_nt(odd, taps[2]), 1, axis=0)
+    at_start = lax.broadcasted_iota(jnp.int32, (frames, 1), 0) == 0
+    shifted = jnp.where(at_start, 0.0, shifted)
+    put_rows(spread, 0, dot_nt(even, taps[0]) + shifted)
+    put_rows(spread, 1, dot_nt(even, taps[1]))
+    put_rows(spread, 2, dot_nt(even, taps[2]) + dot_nt(odd, taps[0]))
+    put_rows(spread, 3, dot_nt(odd, taps[1]))
+    for lane in range(channels // 128):
+        out[:, lane * 128 : (lane + 1) * 128] = spread[lane].astype(BF16)
+        first_rows[:, lane * 128 : (lane + 1) * 128] = spread[lane, 0:8, :]
+
+
+def first_sum_kernel(keep, received, *outs):
+    y = lax.axis_index("dp") // 2
+    x = lax.axis_index("tm") % 2
+    inner = keep.shape[1] // 2
+    for flip, out in enumerate(outs):
+        block = y ^ (flip // 2)
+        lane = x ^ (flip % 2)
+        for z in range(inner):
+            at = 2 * z + lane
+            out[z] = (keep[block, at].astype(F32) + received[block, at].astype(F32)).astype(BF16)
+
+
+def second_sum_kernel(a, b, c, d, *outs):
+    z = lax.axis_index("tm") // 2
+    for flip, out in enumerate(outs):
+        at = z ^ flip
+        total = (a[at].astype(F32) + b[at].astype(F32)) + (c[at].astype(F32) + d[at].astype(F32))
+        out[...] = total.astype(BF16)
+
+
+def last_sum_kernel(wide_rows, a, b, c, d, incoming, first_rows, grad_in, wide, narrow, grad_out, rows_buf, sem):
+    at_start = lax.broadcasted_iota(jnp.int32, (8, 1), 0) == 0
+    rows_buf[...] = (first_rows[...] + jnp.where(at_start, incoming[7:8, :], 0.0)).astype(BF16)
+    put = pltpu.make_async_copy(rows_buf, grad_out.at[pl.ds(0, 8), :], sem)
+    put.start()
+    total = (a[...].astype(F32) + b[...].astype(F32)) + (c[...].astype(F32) + d[...].astype(F32))
+    rows, channels = total.shape
+    pieces = channels // 128
+    for p in range(pieces):
+        lanes = total[:, p * 128 : (p + 1) * 128]
+        wide[pl.ds(p, wide_rows, stride=pieces), :] = lanes[:wide_rows]
+        narrow[pl.ds(p, rows - wide_rows, stride=pieces), :] = lanes[wide_rows:]
+    put.wait()
+
+
+def flipped(dy, dc, dz, dx):
+    dp, tm = lax.axis_size("dp"), lax.axis_size("tm")
+    change_dp, change_tm = 2 * dy + dc, 2 * dz + dx
+    return [
+        (p * tm + t, (p ^ change_dp) * tm + (t ^ change_tm)) for p in range(dp) for t in range(tm)
+    ]
+
+
+def swap(value, dy, dc, dz, dx):
+    return lax.ppermute(value, ("dp", "tm"), flipped(dy, dc, dz, dx))
+
+
+def shards(
+    features,
+    conv_wide,
+    conv_narrow,
+    conv_bias,
+    norm_gain,
+    norm_bias,
+    proj_gain,
+    proj_weight,
+    proj_bias,
+    upstream,
+):
+    dp, tm = lax.axis_size("dp"), lax.axis_size("tm")
+    recs_local, length, channels = features.shape
+    pairs, frames_total, depth = upstream.shape
+    frames = frames_total // tm
+    if not (dp == 4 and tm == 8 and recs_local == 1 and frames % 128 == 0 and pairs * tm == HEADS):
+        return generic_shards(
+            features,
+            conv_wide,
+            conv_narrow,
+            conv_bias,
+            norm_gain,
+            norm_bias,
+            proj_gain,
+            proj_weight,
+            proj_bias,
+            upstream,
+        )
+    width = HEADS * depth
+    factor = 1.0 / math.sqrt(recs_local * dp * frames_total)
+    sems = [pltpu.SemaphoreType.DMA((tm,))]
+    cuts = local(
+        cut_kernel,
+        [upstream.transpose(0, 2, 1)],
+        [((pairs, depth, frames), BF16, False)] * tm,
+        "cut",
+        scratch=[pltpu.VMEM((tm, pairs, depth, frames), BF16)] + sems * 2,
+        raw=(0,),
+        raw_out=range(tm),
+    )
+    cuts = [cut.reshape(pairs * depth, frames) for cut in cuts]
+    heads_in = {0: cuts[0]}
+    for k in (6, 7, 4, 5, 2, 3, 1):
+        heads_in[k] = swap(cuts[k], 0, 0, k // 2, k % 2)
+    signal = features.reshape(length, channels)
+    halo = passed_along(signal[:8], "tm", -1)
+    wide_rows = 2 * frames
+    spread = pltpu.VMEM((channels // 128, length, 128), F32)
+    gain = proj_gain.reshape(1, channels)
+    forward_in = [
+        signal,
+        halo,
+        conv_bias,
+        norm_gain,
+        norm_bias,
+        conv_wide,
+        conv_narrow,
+        gain,
+        proj_bias.reshape(1, width),
+        proj_weight,
+    ]
+    proj_t, *stored = local(
+        forward_kernel,
+        forward_in,
+        [
+            ((width, frames), BF16, False),
+            ((3 * channels, wide_rows), BF16, False),
+            ((2 * channels, frames), BF16, False),
+            ((wide_rows, channels), F32, False),
+            ((wide_rows, channels), F32, False),
+            ((wide_rows, 128), F32, False),
+            ((frames, channels), F32, False),
+            ((frames, channels), F32, False),
+            ((frames, 128), F32, False),
+            ((frames, channels), F32, False),
+            ((frames, 128), F32, False),
+        ],
+        "forward",
+        limit=32,
+        scratch=[pltpu.VMEM(x.shape, x.dtype) for x in forward_in]
+        + [
+            pltpu.SemaphoreType.DMA((len(forward_in),)),
+            spread,
+            pltpu.VMEM((wide_rows, 3 * channels), BF16),
+        ],
+        raw=range(len(forward_in)),
+    )
+    proj_t, heads_in[4] = lax.optimization_barrier((proj_t, heads_in[4]))
+    heads = lax.all_to_all(
+        proj_t.reshape(tm, pairs * depth, frames), "tm", split_axis=0, concat_axis=0, tiled=True
+    )
+    outer, inner = dp // 2, tm
+    part_rows = 5 * channels // (dp * tm)
+    part = ((outer, inner, part_rows, channels), BF16, True)
+    patch_t, act_t, normed_w, slope_w, inv_w, normed_n, slope_n, inv_n, unit, row_inv = stored
+    inputs = [
+        proj_weight,
+        *[heads_in[k] for k in range(tm)],
+        gain,
+        unit,
+        row_inv,
+        normed_n,
+        slope_n,
+        inv_n,
+        conv_narrow,
+        normed_w,
+        slope_w,
+        inv_w,
+        patch_t,
+        act_t,
+    ]
+    lefts = [
+        pltpu.VMEM((x.shape[0] // (2 * outer), x.shape[1]), BF16)
+        for x in (patch_t, act_t)
+        for _ in range(outer)
+    ]
+    held = [pltpu.VMEM(x.shape, x.dtype) for x in inputs[:1] + inputs[tm + 1 : -2]] + lefts
+    grad_buf = pltpu.VMEM((width, frames), BF16)
+    send, grad_conv, grad_low = local(
+        lambda *refs: backward_kernel(factor, *refs),
+        inputs,
+        [part, ((wide_rows, channels), BF16, True), ((frames, channels), BF16, True)],
+        "backward",
+        limit=24,
+        scratch=held + [grad_buf, pltpu.SemaphoreType.DMA((len(held) + tm,))],
+        raw=range(len(inputs)),
+    )
+    received = swap(send, 0, 1, 0, 0)
+    held = lefts + [pltpu.VMEM((channels, channels), BF16)]
+    keep, tail = local(
+        lambda *refs: own_grad_kernel(factor, *refs),
+        [patch_t, act_t, conv_wide, grad_conv, grad_low],
+        [part, ((8, channels), F32, True)],
+        "own_grad",
+        scratch=held + [pltpu.SemaphoreType.DMA((len(held),))],
+        raw=(0, 1, 2),
+    )
+    plane = ((tm // 2, part_rows, channels), BF16, True)
+    own, *outgoing = local(first_sum_kernel, [keep, received], [plane] * 4, "first_sum")
+    arrived = [swap(value, k // 2, 0, 0, k % 2) for k, value in enumerate(outgoing, 1)]
+    tail, grad_conv, own = lax.optimization_barrier((tail, grad_conv, own))
+    incoming = passed_along(tail, "tm", 1)
+    feature_grad, first_rows = local(
+        input_grad_kernel,
+        [grad_conv, conv_wide],
+        [((length, channels), BF16, False), ((8, channels), F32, True)],
+        "input_grad",
+        scratch=[spread],
+    )
+    piece = ((part_rows, channels), BF16, True)
+    (attn_t,) = local(
+        join_kernel,
+        [heads.reshape(tm, pairs, depth, frames)],
+        [((pairs, depth, frames_total), BF16, False)],
+        "join",
+        scratch=sems,
+        raw_out=(0,),
+    )
+    attn_t, first_rows, own = lax.optimization_barrier((attn_t, first_rows, own))
+    own, *outgoing = local(second_sum_kernel, [own, *arrived], [piece] * 4, "second_sum")
+    arrived = [swap(value, 0, 0, k, 0) for k, value in enumerate(outgoing, 1)]
+    own_wide = 3 * channels // (dp * tm)
+    wide, narrow, feature_grad = local(
+        lambda *refs: last_sum_kernel(own_wide, *refs),
+        [own, *arrived, incoming, first_rows, feature_grad],
+        [
+            ((own_wide * channels // 128, 128), F32, False),
+            (((part_rows - own_wide) * channels // 128, 128), F32, False),
+            ((length, channels), BF16, False),
+        ],
+        "last_sum",
+        scratch=[pltpu.VMEM((8, channels), BF16), pltpu.SemaphoreType.DMA(())],
+        raw=(6,),
+        raw_out=(2,),
+        aliases={6: 2},
+    )
+    return (
+        attn_t.transpose(0, 2, 1),
+        feature_grad.reshape(recs_local, length, channels),
+        wide.reshape(-1),
+        narrow.reshape(-1),
+    )
+
+
 def solution(mesh):
     in_specs = (
         P("dp", "tm", None),

time: 251 us -> 78.1 us (0.31)
  waiting for transfers between devices: 151 us -> 17.8 us
  local copies, waits for them, and re-layouts: 44 us -> 2.79 us
  Pallas kernels: 0 us -> 22.7 us
  starting transfers between devices: 18.4 us -> 33.6 us
  matrix products: 15 us -> 0 us
  between operations: 14.4 us -> 0.83 us
  other arithmetic: 7.35 us -> 0 us
    unnamed x2 -> x0, waiting for transfers between devices: 117 us -> none
    all_to_all x2 -> x1, waiting for transfers between devices: 34 us -> 6.24 us  [shards(): lax.all_to_all(proj_t.reshape(tm, pairs * depth, frames), 'tm', split_axi...]
    ppermute x0 -> x14, starting transfers between devices: none -> 24.8 us  [swap(): return lax.ppermute(value, ('dp', 'tm'), flipped(dy, dc, dz, dx))]
    pallas_call x0 -> x9, Pallas kernels: none -> 22.7 us  [local(): pl.pallas_call(kernel, out_shape=out_shape, in_specs=[pl.BlockSpec(memory...]
    unnamed x52 -> x18, local copies, waits for them, and re-layouts: 18.3 us -> 0.8 us
    dot_general x7 -> x0, matrix products: 13 us -> none  [the longest x2 4.34 us: conv_forward(): jnp.dot(patches.reshape(recs_local * out_rows, patch_width), weight, pref...]
    ppermute x0 -> x14, waiting for transfers between devices: none -> 10.1 us  [swap(): return lax.ppermute(value, ('dp', 'tm'), flipped(dy, dc, dz, dx))]
    all_to_all x2 -> x1, starting transfers between devices: 13.2 us -> 5.37 us  [shards(): lax.all_to_all(proj_t.reshape(tm, pairs * depth, frames), 'tm', split_axi...]
  transfers between devices with their start and end apart: 5 -> 17, of which waited for: 3 -> 6; matrix products, arithmetic and copies ran while one was open for 13% -> 3% of each run, Pallas kernels for 0% -> 25%
where the time goes in v2:
time: 78.1 us; the launch traced here: 77.7 us
  starting transfers between devices  33.6 us (43%)
  Pallas kernels  22.7 us (29%)
  waiting for transfers between devices  17.8 us (23%)
  local copies, waits for them, and re-layouts  2.79 us (4%)
  between operations  0.83 us (1%)
    ppermute x14, starting transfers between devices, swap(): return lax.ppermute(value, ('dp', 'tm'), flipped(dy, dc, dz, dx))  24.8 us
    pallas_call x9, Pallas kernels, local(): pl.pallas_call(kernel, out_shape=out_shape, in_specs=[pl.BlockSpec(memory...  22.7 us
    ppermute x14, waiting for transfers between devices, swap(): return lax.ppermute(value, ('dp', 'tm'), flipped(dy, dc, dz, dx))  10.1 us
    all_to_all x1, waiting for transfers between devices, shards(): lax.all_to_all(proj_t.reshape(tm, pairs * depth, frames), 'tm', split_axi...  6.24 us
    all_to_all x1, starting transfers between devices, shards(): lax.all_to_all(proj_t.reshape(tm, pairs * depth, frames), 'tm', split_axi...  5.37 us
    ppermute x2, starting transfers between devices, passed_along(): lax.ppermute(value, axis, [(source, source + steps) for source in range(l...  3.36 us
  transfers between devices with their start and end apart: 17, of which 6 were waited for; matrix products, arithmetic and copies ran while one was open for 3% of the time, Pallas kernels for 25%

profile of v2, /device:TPU:0, one launch (start us, length us, event | category | flops | bytes accessed | tf_op | source)
XLA Modules:
  0.0 77.7 jit_solution(13904885453521852904)
XLA Ops:
  0.6 2.1 %cut.1 = (bf16[2,120,256]{2,1,0:T(8,128)(2,1)}, bf16[2,120,256]{2,1,0:T(8,128)(2,1)}, bf16[2,120,256]{2,1,0:T(8,128)(2,1)}, bf16[2,120,256]{2,1,0:T(8,128)(2,1)}...) custom-call(bf16[2,120,2048]{2,1,0:T(8,128)(2,1)} %bitcast.22), custom_call_target="tpu_custom_call" | custom-call | flops 1000 | tf_op jit(solution)/shard_map/cut/pallas_call | solution.py:199
  2.7 4.1 %collective-permute-start.1 = (bf16[240,256]{1,0:T(8,128)(2,1)}, bf16[240,256]{1,0:T(8,128)(2,1)S(1)}, u32[]{:S(2)}, u32[]{:S(2)}) collective-permute-start(bf16[240,256]{1,0:T(8,128)(2,1)} %bitcast.34), channel_id=1, source_target_pairs={{0,4},{1,5},{2,6},{3,7},{4,0},{5,1},{6,2},{7,3},{8,12},{9,13},{10,... | collective-permute-start | bytes 368648 | tf_op jit(solution)/shard_map/ppermute | solution.py:457
  6.8 1.5 %collective-permute-start.2 = (bf16[240,256]{1,0:T(8,128)(2,1)}, bf16[240,256]{1,0:T(8,128)(2,1)S(1)}, u32[]{:S(2)}, u32[]{:S(2)}) collective-permute-start(bf16[240,256]{1,0:T(8,128)(2,1)} %bitcast.33), channel_id=1, source_target_pairs={{0,1},{1,0},{2,3},{3,2},{4,5},{5,4},{6,7},{7,6},{8,9},{9,8},{10,11... | collective-permute-start | bytes 368648 | tf_op jit(solution)/shard_map/ppermute | solution.py:457
  8.3 0.7 slice_bitcast_fusion
  9.0 1.3 %collective-permute-start = (bf16[8,512]{1,0:T(8,128)(2,1)S(1)}, bf16[8,512]{1,0:T(8,128)(2,1)S(1)}, u32[]{:S(2)}, u32[]{:S(2)}) collective-permute-start(bf16[8,512]{1,0:T(8,128)(2,1)S(1)} %slice_bitcast_fusion), channel_id=1, source_target_pairs={{1,0},{2,1},{3,2},{4,3},{5,4},{6,5},{7,6},{9,8},{10,9},{11,10},{12... | collective-permute-start | bytes 24584 | tf_op jit(solution)/shard_map/ppermute | solution.py:22
  10.3 2.7 %collective-permute-start.3 = (bf16[240,256]{1,0:T(8,128)(2,1)}, bf16[240,256]{1,0:T(8,128)(2,1)S(1)}, u32[]{:S(2)}, u32[]{:S(2)}) collective-permute-start(bf16[240,256]{1,0:T(8,128)(2,1)} %bitcast.32), channel_id=1, source_target_pairs={{0,2},{1,3},{2,0},{3,1},{4,6},{5,7},{6,4},{7,5},{8,10},{9,11},{10,... | collective-permute-start | bytes 368648 | tf_op jit(solution)/shard_map/ppermute | solution.py:457
  13.0 1.5 %collective-permute-start.4 = (bf16[240,256]{1,0:T(8,128)(2,1)}, bf16[240,256]{1,0:T(8,128)(2,1)S(1)}, u32[]{:S(2)}, u32[]{:S(2)}) collective-permute-start(bf16[240,256]{1,0:T(8,128)(2,1)} %bitcast.31), channel_id=1, source_target_pairs={{0,3},{1,2},{2,1},{3,0},{4,7},{5,6},{6,5},{7,4},{8,11},{9,10},{10,... | collective-permute-start | bytes 368648 | tf_op jit(solution)/shard_map/ppermute | solution.py:457
  14.5 0.1 collective-permute-done.refs_1_
  14.5 0.0 copy-start.8
  14.6 2.4 %collective-permute-start.5 = (bf16[240,256]{1,0:T(8,128)(2,1)}, bf16[240,256]{1,0:T(8,128)(2,1)S(1)}, u32[]{:S(2)}, u32[]{:S(2)}) collective-permute-start(bf16[240,256]{1,0:T(8,128)(2,1)} %bitcast.30), channel_id=1, source_target_pairs={{0,5},{1,4},{2,7},{3,6},{4,1},{5,0},{6,3},{7,2},{8,13},{9,12},{10,... | collective-permute-start | bytes 368648 | tf_op jit(solution)/shard_map/ppermute | solution.py:457
  16.9 0.0 collective-permute-done.1.refs_5_
  16.9 0.0 copy-start.1
  16.9 2.4 %collective-permute-start.6 = (bf16[240,256]{1,0:T(8,128)(2,1)}, bf16[240,256]{1,0:T(8,128)(2,1)S(1)}, u32[]{:S(2)}, u32[]{:S(2)}) collective-permute-start(bf16[240,256]{1,0:T(8,128)(2,1)} %bitcast.29), channel_id=1, source_target_pairs={{0,6},{1,7},{2,4},{3,5},{4,2},{5,3},{6,0},{7,1},{8,14},{9,15},{10,... | collective-permute-start | bytes 368648 | tf_op jit(solution)/shard_map/ppermute | solution.py:457
  19.4 0.0 collective-permute-done.2.refs_2_
  19.4 0.0 copy-start.2
  19.4 0.6 collective-permute-start.7
  20.0 1.3 %reshape.59.refs_8_ = f32[1,1920]{1,0:T(1,128)} reshape(f32[1920]{0:T(1024)} %param.18) | data formatting | bytes 15360 | tf_op jit(solution)/shard_map/reshape | solution.py:519
  21.3 0.0 copy-done.8
  21.3 7.7 %forward.1 = (bf16[1920,256]{1,0:T(8,128)(2,1)}, bf16[1536,512]{1,0:T(8,128)(2,1)}, bf16[1024,256]{1,0:T(8,128)(2,1)}, f32[512,512]{1,0:T(8,128)}, f32[512,512]{...) custom-call(bf16[1024,512]{1,0:T(8,128)(2,1)} %bitcast.20, ...), custom_call_target="tpu_custom_call" | custom-call | flops 1000 | tf_op jit(solution)/shard_map/forward/pallas_call | solution.py:199
  29.0 0.0 copy-done.1
  29.0 0.0 copy-done.2
  29.0 5.4 %all-to-all-start = ((bf16[8,240,256]{2,1,0:T(8,128)(2,1)}), bf16[8,240,256]{2,1,0:T(8,128)(2,1)S(1)}, u32[]{:S(2)}, u32[]{:S(2)}) async-start(bf16[8,240,256]{2,1,0:T(8,128)(2,1)} %bitcast.23), calls=%async_computation | async-start | bytes 1966080 | tf_op jit(solution)/shard_map/all_to_all | solution.py:549
  34.4 0.0 collective-permute-done.3.refs_3_
  34.4 0.0 copy-start.3
  34.4 0.0 collective-permute-done.4.refs_4_
  34.4 0.0 copy-start.4
  34.4 0.0 collective-permute-done.5.refs_6_
  34.4 0.0 copy-start.5
  34.4 0.0 collective-permute-done.6.refs_7_
  34.5 0.0 copy-start.6
  34.5 0.0 collective-permute-done.7.refs_8_
  34.5 0.0 copy-start.7
  34.5 0.5 copy-done.3
  35.0 0.1 copy-done.4
  35.1 0.1 copy-done.5
  35.1 0.1 copy-done.6
  35.2 0.1 copy-done.7
  35.3 5.8 %backward.1 = (bf16[2,8,80,512]{3,2,1,0:T(8,128)(2,1)S(1)}, bf16[512,512]{1,0:T(8,128)(2,1)S(1)}, bf16[256,512]{1,0:T(8,128)(2,1)S(1)}) custom-call(bf16[512,1920]{1,0:T(8,128)(2,1)} %refs_0_.1, bf16[240,256]{1,0:T(8,128)(2,1)} %bitcast.25, bf16[240,256]{1,0:T(8,128)(2,1)} %copy-done.2, bf16[240,256]{1,0:T(8,128)(2,1)} %copy-done.3, ...), custom_call_target="tpu_custom_call" | custom-call | flops 1000 | tf_op jit(solution)/shard_map/backward/pallas_call | solution.py:199
  41.0 0.1 collective-permute-start.8
  41.1 2.3 %own_grad.1 = (bf16[2,8,80,512]{3,2,1,0:T(8,128)(2,1)S(1)}, f32[8,512]{1,0:T(8,128)S(1)}) custom-call(bf16[1536,512]{1,0:T(8,128)(2,1)} %get-tuple-element.52.refs_19_.refs_0_, bf16[1024,256]{1,0:T(8,128)(2,1)} %get-tuple-element.53.refs_20_.refs_1_, bf16[1536,512]{1,0:T(8,128)(2,1)} %conv_wide.1, bf16[512,512]{1,0:T(8,128)(2,1)S(1)} %get-tuple-element.76.refs_3_.grad_conv, ...), custom_call_target="tpu_custom_call" | custom-call | flops 1000 | tf_op jit(solution)/shard_map/own_grad/pallas_call | solution.py:199
  43.4 0.0 copy-start
  43.4 0.7 collective-permute-done.8.received
  44.1 0.3 first_sum.1
  44.4 2.1 %collective-permute-start.9 = (bf16[4,80,512]{2,1,0:T(8,128)(2,1)S(1)}, bf16[4,80,512]{2,1,0:T(8,128)(2,1)S(1)}, u32[]{:S(2)}, u32[]{:S(2)}) collective-permute-start(bf16[4,80,512]{2,1,0:T(8,128)(2,1)S(1)} %get-tuple-element.81), channel_id=1, source_target_pairs={{0,1},{1,0},{2,3},{3,2},{4,5},{5,4},{6,7},{7,6},{8,9},{9,8},{10,11... | collective-permute-start | bytes 983048 | tf_op jit(solution)/shard_map/ppermute | solution.py:457
  46.5 1.5 %collective-permute-start.10 = (bf16[4,80,512]{2,1,0:T(8,128)(2,1)S(1)}, bf16[4,80,512]{2,1,0:T(8,128)(2,1)S(1)}, u32[]{:S(2)}, u32[]{:S(2)}) collective-permute-start(bf16[4,80,512]{2,1,0:T(8,128)(2,1)S(1)} %get-tuple-element.82), channel_id=1, source_target_pairs={{0,16},{1,17},{2,18},{3,19},{4,20},{5,21},{6,22},{7,23},{8,24},{9,... | collective-permute-start | bytes 983048 | tf_op jit(solution)/shard_map/ppermute | solution.py:457
  48.0 0.0 collective-permute-start.11
  48.1 0.0 copy-done
  48.1 2.2 %input_grad.1 = (bf16[1024,512]{1,0:T(8,128)(2,1)}, f32[8,512]{1,0:T(8,128)S(1)}) custom-call(bf16[512,512]{1,0:T(8,128)(2,1)S(1)} %get-tuple-element.76.refs_3_.grad_conv, bf16[1536,512]{1,0:T(8,128)(2,1)S(1)} %copy-done), custom_call_target="tpu_custom_call" | custom-call | flops 1000 | tf_op jit(solution)/shard_map/input_grad/pallas_call | solution.py:199
  50.2 6.2 %all-to-all-done = bf16[8,240,256]{2,1,0:T(8,128)(2,1)S(1)} async-done(((bf16[8,240,256]{2,1,0:T(8,128)(2,1)}), bf16[8,240,256]{2,1,0:T(8,128)(2,1)S(1)}, u32[]{:S(2)}, u32[]{:S(2)}) %all-to-all-start) | async-done | bytes 983072 | tf_op jit(solution)/shard_map/all_to_all | solution.py:549
  56.5 1.0 %join.1 = bf16[2,120,2048]{2,1,0:T(8,128)(2,1)} custom-call(bf16[8,2,120,256]{3,2,1,0:T(8,128)(2,1)S(1)} %bitcast.19), custom_call_target="tpu_custom_call" | custom-call | flops 1000 | tf_op jit(solution)/shard_map/join/pallas_call | solution.py:199
  57.5 0.0 collective-permute-done.9.b
  57.5 0.0 collective-permute-done.10.c
  57.5 6.4 %collective-permute-done.11.d = bf16[4,80,512]{2,1,0:T(8,128)(2,1)S(1)} collective-permute-done((bf16[4,80,512]{2,1,0:T(8,128)(2,1)S(1)}, bf16[4,80,512]{2,1,0:T(8,128)(2,1)S(1)}, u32[]{:S(2)}, u32[]{:S(2)}) %collective-permute-start.11) | collective-permute-done | bytes 327712 | tf_op jit(solution)/shard_map/ppermute | solution.py:457
  63.9 0.2 second_sum.1
  64.1 3.0 %collective-permute-start.12 = (bf16[80,512]{1,0:T(8,128)(2,1)S(1)}, bf16[80,512]{1,0:T(8,128)(2,1)S(1)}, u32[]{:S(2)}, u32[]{:S(2)}) collective-permute-start(bf16[80,512]{1,0:T(8,128)(2,1)S(1)} %get-tuple-element.85), channel_id=1, source_target_pairs={{0,2},{1,3},{2,0},{3,1},{4,6},{5,7},{6,4},{7,5},{8,10},{9,11},{10,... | collective-permute-start | bytes 245768 | tf_op jit(solution)/shard_map/ppermute | solution.py:457
  67.0 1.6 %collective-permute-start.13 = (bf16[80,512]{1,0:T(8,128)(2,1)S(1)}, bf16[80,512]{1,0:T(8,128)(2,1)S(1)}, u32[]{:S(2)}, u32[]{:S(2)}) collective-permute-start(bf16[80,512]{1,0:T(8,128)(2,1)S(1)} %get-tuple-element.86), channel_id=1, source_target_pairs={{0,4},{1,5},{2,6},{3,7},{4,0},{5,1},{6,2},{7,3},{8,12},{9,13},{10,... | collective-permute-start | bytes 245768 | tf_op jit(solution)/shard_map/ppermute | solution.py:457
  68.6 1.4 %collective-permute-start.14 = (bf16[80,512]{1,0:T(8,128)(2,1)S(1)}, bf16[80,512]{1,0:T(8,128)(2,1)S(1)}, u32[]{:S(2)}, u32[]{:S(2)}) collective-permute-start(bf16[80,512]{1,0:T(8,128)(2,1)S(1)} %get-tuple-element.87), channel_id=1, source_target_pairs={{0,6},{1,7},{2,4},{3,5},{4,2},{5,3},{6,0},{7,1},{8,14},{9,15},{10,... | collective-permute-start | bytes 245768 | tf_op jit(solution)/shard_map/ppermute | solution.py:457
  70.0 2.1 %collective-permute-start.15 = (f32[8,512]{1,0:T(8,128)S(1)}, f32[8,512]{1,0:T(8,128)S(1)}, u32[]{:S(2)}, u32[]{:S(2)}) collective-permute-start(f32[8,512]{1,0:T(8,128)S(1)} %get-tuple-element.88), channel_id=1, source_target_pairs={{0,1},{1,2},{2,3},{3,4},{4,5},{5,6},{6,7},{8,9},{9,10},{10,11},{11... | collective-permute-start | bytes 49160 | tf_op jit(solution)/shard_map/ppermute | solution.py:22
  72.1 1.4 %collective-permute-done.15.refs_4_ = f32[8,512]{1,0:T(8,128)S(1)} collective-permute-done((f32[8,512]{1,0:T(8,128)S(1)}, f32[8,512]{1,0:T(8,128)S(1)}, u32[]{:S(2)}, u32[]{:S(2)}) %collective-permute-start.15) | collective-permute-done | bytes 16416 | tf_op jit(solution)/shard_map/ppermute | solution.py:22
  73.5 0.0 collective-permute-done.12.refs_1_
  73.5 2.9 %collective-permute-done.13.refs_2_ = bf16[80,512]{1,0:T(8,128)(2,1)S(1)} collective-permute-done((bf16[80,512]{1,0:T(8,128)(2,1)S(1)}, bf16[80,512]{1,0:T(8,128)(2,1)S(1)}, u32[]{:S(2)}, u32[]{:S(2)}) %collective-permute-start.13) | collective-permute-done | bytes 81952 | tf_op jit(solution)/shard_map/ppermute | solution.py:457
  76.5 0.0 collective-permute-done.14.refs_3_
  76.5 1.3 %last_sum.1 = (f32[192,128]{1,0:T(8,128)}, f32[128,128]{1,0:T(8,128)}, bf16[1024,512]{1,0:T(8,128)(2,1)}) custom-call(bf16[80,512]{1,0:T(8,128)(2,1)S(1)} %get-tuple-element.84.refs_0_, bf16[80,512]{1,0:T(8,128)(2,1)S(1)} %collective-permute-done.12.refs_1_, bf16[80,512]{1,0:T(8,128)(2,1)S(1)} %collective-permute-done.13.refs_2_, ...), custom_call_target="tpu_custom_call", output_to_operand_aliasing={{2}: (6, {})} | custom-call | flops 1000 | tf_op jit(solution)/shard_map/last_sum/pallas_call | solution.py:199
Async XLA Ops:
  2.7 14.2 %collective-permute-start.1 = (bf16[240,256]{1,0:T(8,128)(2,1)}, bf16[240,256]{1,0:T(8,128)(2,1)S(1)}, u32[]{:S(2)}, u32[]{:S(2)}) collective-permute-start(bf16[240,256]{1,0:T(8,128)(2,1)} %bitcast.34), channel_id=1, source_target_pairs={{0,4},{1,5},{2,6},{3,7},{4,0},{5,1},{6,2},{7,3},{8,12},{9,13},{10,... | collective-permute-start | bytes 368648 | tf_op jit(solution)/shard_map/ppermute | solution.py:457
  6.8 12.5 %collective-permute-start.2 = (bf16[240,256]{1,0:T(8,128)(2,1)}, bf16[240,256]{1,0:T(8,128)(2,1)S(1)}, u32[]{:S(2)}, u32[]{:S(2)}) collective-permute-start(bf16[240,256]{1,0:T(8,128)(2,1)} %bitcast.33), channel_id=1, source_target_pairs={{0,1},{1,0},{2,3},{3,2},{4,5},{5,4},{6,7},{7,6},{8,9},{9,8},{10,11... | collective-permute-start | bytes 368648 | tf_op jit(solution)/shard_map/ppermute | solution.py:457
  9.0 5.5 %collective-permute-start = (bf16[8,512]{1,0:T(8,128)(2,1)S(1)}, bf16[8,512]{1,0:T(8,128)(2,1)S(1)}, u32[]{:S(2)}, u32[]{:S(2)}) collective-permute-start(bf16[8,512]{1,0:T(8,128)(2,1)S(1)} %slice_bitcast_fusion), channel_id=1, source_target_pairs={{1,0},{2,1},{3,2},{4,3},{5,4},{6,5},{7,6},{9,8},{10,9},{11,10},{12... | collective-permute-start | bytes 24584 | tf_op jit(solution)/shard_map/ppermute | solution.py:22
  10.3 24.1 %collective-permute-start.3 = (bf16[240,256]{1,0:T(8,128)(2,1)}, bf16[240,256]{1,0:T(8,128)(2,1)S(1)}, u32[]{:S(2)}, u32[]{:S(2)}) collective-permute-start(bf16[240,256]{1,0:T(8,128)(2,1)} %bitcast.32), channel_id=1, source_target_pairs={{0,2},{1,3},{2,0},{3,1},{4,6},{5,7},{6,4},{7,5},{8,10},{9,11},{10,... | collective-permute-start | bytes 368648 | tf_op jit(solution)/shard_map/ppermute | solution.py:457
  13.0 21.4 %collective-permute-start.4 = (bf16[240,256]{1,0:T(8,128)(2,1)}, bf16[240,256]{1,0:T(8,128)(2,1)S(1)}, u32[]{:S(2)}, u32[]{:S(2)}) collective-permute-start(bf16[240,256]{1,0:T(8,128)(2,1)} %bitcast.31), channel_id=1, source_target_pairs={{0,3},{1,2},{2,1},{3,0},{4,7},{5,6},{6,5},{7,4},{8,11},{9,10},{10,... | collective-permute-start | bytes 368648 | tf_op jit(solution)/shard_map/ppermute | solution.py:457
  14.5 6.8 %copy-start.8 = (bf16[8,512]{1,0:T(8,128)(2,1)}, bf16[8,512]{1,0:T(8,128)(2,1)S(1)}, u32[]{:S(2)}) copy-start(bf16[8,512]{1,0:T(8,128)(2,1)S(1)} %collective-permute-done.refs_1_) | copy-start | bytes 24580
  14.6 19.9 %collective-permute-start.5 = (bf16[240,256]{1,0:T(8,128)(2,1)}, bf16[240,256]{1,0:T(8,128)(2,1)S(1)}, u32[]{:S(2)}, u32[]{:S(2)}) collective-permute-start(bf16[240,256]{1,0:T(8,128)(2,1)} %bitcast.30), channel_id=1, source_target_pairs={{0,5},{1,4},{2,7},{3,6},{4,1},{5,0},{6,3},{7,2},{8,13},{9,12},{10,... | collective-permute-start | bytes 368648 | tf_op jit(solution)/shard_map/ppermute | solution.py:457
  16.9 12.1 %copy-start.1 = (bf16[240,256]{1,0:T(8,128)(2,1)}, bf16[240,256]{1,0:T(8,128)(2,1)S(1)}, u32[]{:S(2)}) copy-start(bf16[240,256]{1,0:T(8,128)(2,1)S(1)} %collective-permute-done.1.refs_5_) | copy-start | bytes 368644
  16.9 17.5 %collective-permute-start.6 = (bf16[240,256]{1,0:T(8,128)(2,1)}, bf16[240,256]{1,0:T(8,128)(2,1)S(1)}, u32[]{:S(2)}, u32[]{:S(2)}) collective-permute-start(bf16[240,256]{1,0:T(8,128)(2,1)} %bitcast.29), channel_id=1, source_target_pairs={{0,6},{1,7},{2,4},{3,5},{4,2},{5,3},{6,0},{7,1},{8,14},{9,15},{10,... | collective-permute-start | bytes 368648 | tf_op jit(solution)/shard_map/ppermute | solution.py:457
  19.4 9.6 %copy-start.2 = (bf16[240,256]{1,0:T(8,128)(2,1)}, bf16[240,256]{1,0:T(8,128)(2,1)S(1)}, u32[]{:S(2)}) copy-start(bf16[240,256]{1,0:T(8,128)(2,1)S(1)} %collective-permute-done.2.refs_2_) | copy-start | bytes 368644
  19.4 15.1 %collective-permute-start.7 = (bf16[240,256]{1,0:T(8,128)(2,1)}, bf16[240,256]{1,0:T(8,128)(2,1)S(1)}, u32[]{:S(2)}, u32[]{:S(2)}) collective-permute-start(bf16[240,256]{1,0:T(8,128)(2,1)} %bitcast.28), channel_id=1, source_target_pairs={{0,7},{1,6},{2,5},{3,4},{4,3},{5,2},{6,1},{7,0},{8,15},{9,14},{10,... | collective-permute-start | bytes 368648 | tf_op jit(solution)/shard_map/ppermute | solution.py:457
  29.0 27.4 %all-to-all-start = ((bf16[8,240,256]{2,1,0:T(8,128)(2,1)}), bf16[8,240,256]{2,1,0:T(8,128)(2,1)S(1)}, u32[]{:S(2)}, u32[]{:S(2)}) async-start(bf16[8,240,256]{2,1,0:T(8,128)(2,1)} %bitcast.23), calls=%async_computation | async-start | bytes 1966080 | tf_op jit(solution)/shard_map/all_to_all | solution.py:549
  34.4 0.6 copy-start.3
  34.4 0.7 copy-start.4
  34.4 0.7 copy-start.5
  34.5 0.8 copy-start.6
  34.5 0.8 %copy-start.7 = (bf16[240,256]{1,0:T(8,128)(2,1)}, bf16[240,256]{1,0:T(8,128)(2,1)S(1)}, u32[]{:S(2)}) copy-start(bf16[240,256]{1,0:T(8,128)(2,1)S(1)} %collective-permute-done.7.refs_8_) | copy-start | bytes 368644
  41.0 3.1 %collective-permute-start.8 = (bf16[2,8,80,512]{3,2,1,0:T(8,128)(2,1)S(1)}, bf16[2,8,80,512]{3,2,1,0:T(8,128)(2,1)S(1)}, u32[]{:S(2)}, u32[]{:S(2)}) collective-permute-start(bf16[2,8,80,512]{3,2,1,0:T(8,128)(2,1)S(1)} %get-tuple-element.74), channel_id=1, source_target_pairs={{0,8},{1,9},{2,10},{3,11},{4,12},{5,13},{6,14},{7,15},{8,0},{9,1},... | collective-permute-start | bytes 3932168 | tf_op jit(solution)/shard_map/ppermute | solution.py:457
  43.4 4.6 %copy-start = (bf16[1536,512]{1,0:T(8,128)(2,1)S(1)}, bf16[1536,512]{1,0:T(8,128)(2,1)}, u32[]{:S(2)}) copy-start(bf16[1536,512]{1,0:T(8,128)(2,1)} %conv_wide.1) | copy-start | bytes 4718596
  44.4 13.0 %collective-permute-start.9 = (bf16[4,80,512]{2,1,0:T(8,128)(2,1)S(1)}, bf16[4,80,512]{2,1,0:T(8,128)(2,1)S(1)}, u32[]{:S(2)}, u32[]{:S(2)}) collective-permute-start(bf16[4,80,512]{2,1,0:T(8,128)(2,1)S(1)} %get-tuple-element.81), channel_id=1, source_target_pairs={{0,1},{1,0},{2,3},{3,2},{4,5},{5,4},{6,7},{7,6},{8,9},{9,8},{10,11... | collective-permute-start | bytes 983048 | tf_op jit(solution)/shard_map/ppermute | solution.py:457
  46.5 11.0 %collective-permute-start.10 = (bf16[4,80,512]{2,1,0:T(8,128)(2,1)S(1)}, bf16[4,80,512]{2,1,0:T(8,128)(2,1)S(1)}, u32[]{:S(2)}, u32[]{:S(2)}) collective-permute-start(bf16[4,80,512]{2,1,0:T(8,128)(2,1)S(1)} %get-tuple-element.82), channel_id=1, source_target_pairs={{0,16},{1,17},{2,18},{3,19},{4,20},{5,21},{6,22},{7,23},{8,24},{9,... | collective-permute-start | bytes 983048 | tf_op jit(solution)/shard_map/ppermute | solution.py:457
  48.0 15.8 %collective-permute-start.11 = (bf16[4,80,512]{2,1,0:T(8,128)(2,1)S(1)}, bf16[4,80,512]{2,1,0:T(8,128)(2,1)S(1)}, u32[]{:S(2)}, u32[]{:S(2)}) collective-permute-start(bf16[4,80,512]{2,1,0:T(8,128)(2,1)S(1)} %get-tuple-element.83), channel_id=1, source_target_pairs={{0,17},{1,16},{2,19},{3,18},{4,21},{5,20},{6,23},{7,22},{8,25},{9,... | collective-permute-start | bytes 983048 | tf_op jit(solution)/shard_map/ppermute | solution.py:457
  64.1 9.5 %collective-permute-start.12 = (bf16[80,512]{1,0:T(8,128)(2,1)S(1)}, bf16[80,512]{1,0:T(8,128)(2,1)S(1)}, u32[]{:S(2)}, u32[]{:S(2)}) collective-permute-start(bf16[80,512]{1,0:T(8,128)(2,1)S(1)} %get-tuple-element.85), channel_id=1, source_target_pairs={{0,2},{1,3},{2,0},{3,1},{4,6},{5,7},{6,4},{7,5},{8,10},{9,11},{10,... | collective-permute-start | bytes 245768 | tf_op jit(solution)/shard_map/ppermute | solution.py:457
  67.0 9.4 %collective-permute-start.13 = (bf16[80,512]{1,0:T(8,128)(2,1)S(1)}, bf16[80,512]{1,0:T(8,128)(2,1)S(1)}, u32[]{:S(2)}, u32[]{:S(2)}) collective-permute-start(bf16[80,512]{1,0:T(8,128)(2,1)S(1)} %get-tuple-element.86), channel_id=1, source_target_pairs={{0,4},{1,5},{2,6},{3,7},{4,0},{5,1},{6,2},{7,3},{8,12},{9,13},{10,... | collective-permute-start | bytes 245768 | tf_op jit(solution)/shard_map/ppermute | solution.py:457
  68.6 7.9 %collective-permute-start.14 = (bf16[80,512]{1,0:T(8,128)(2,1)S(1)}, bf16[80,512]{1,0:T(8,128)(2,1)S(1)}, u32[]{:S(2)}, u32[]{:S(2)}) collective-permute-start(bf16[80,512]{1,0:T(8,128)(2,1)S(1)} %get-tuple-element.87), channel_id=1, source_target_pairs={{0,6},{1,7},{2,4},{3,5},{4,2},{5,3},{6,0},{7,1},{8,14},{9,15},{10,... | collective-permute-start | bytes 245768 | tf_op jit(solution)/shard_map/ppermute | solution.py:457
  70.0 3.5 %collective-permute-start.15 = (f32[8,512]{1,0:T(8,128)S(1)}, f32[8,512]{1,0:T(8,128)S(1)}, u32[]{:S(2)}, u32[]{:S(2)}) collective-permute-start(f32[8,512]{1,0:T(8,128)S(1)} %get-tuple-element.88), channel_id=1, source_target_pairs={{0,1},{1,2},{2,3},{3,4},{4,5},{5,6},{6,7},{8,9},{9,10},{10,11},{11... | collective-permute-start | bytes 49160 | tf_op jit(solution)/shard_map/ppermute | solution.py:22

commit v3 on v2

--- a/solution.py
+++ b/solution.py
@@ -159,6 +159,7 @@
 
 
 F32 = jnp.float32
+ORDER = (0, 6, 7, 4, 5, 2, 3, 1)
 BF16 = jnp.bfloat16
 NT = (((1,), (1,)), ((), ()))
 
@@ -187,20 +188,21 @@
     return preact * cumulative, slope
 
 
-def local(kernel, operands, outs, name, limit=16, scratch=(), raw=(), raw_out=(), aliases=None, cost=1000):
+def local(kernel, operands, outs, name, limit=16, scratch=(), raw=(), raw_out=(), free=(), aliases=None, cost=1000):
     out_shape, out_specs = [], []
     for number, (shape, dtype, stays) in enumerate(outs):
         out_shape.append((pltpu.VMEM if stays else pltpu.HBM)(shape, dtype))
         out_specs.append(pl.BlockSpec(memory_space=pltpu.HBM if number in raw_out else pltpu.VMEM))
     held = [
-        pltpu.with_memory_space_constraint(x, pltpu.HBM if k in raw else pltpu.VMEM)
+        x if k in free else pltpu.with_memory_space_constraint(x, pltpu.HBM if k in raw else pltpu.VMEM)
         for k, x in enumerate(operands)
     ]
     return pl.pallas_call(
         kernel,
         out_shape=out_shape,
         in_specs=[
-            pl.BlockSpec(memory_space=pltpu.HBM if k in raw else pltpu.VMEM) for k in range(len(operands))
+            pl.BlockSpec(memory_space=pl.ANY if k in free else pltpu.HBM if k in raw else pltpu.VMEM)
+            for k in range(len(operands))
         ],
         out_specs=out_specs,
         scratch_shapes=list(scratch),
@@ -219,13 +221,22 @@
         copy.wait()
 
 
-def cut_kernel(whole, *refs):
+def first_cut_kernel(flips, whole, signal, *refs):
+    *parts, first_rows, sems = refs
+    width = parts[0].shape[2]
+    own = lax.axis_index("tm")
+    starts = [pl.multiple_of((own ^ flip) * width, width) for flip in flips]
+    pairs = [(whole.at[:, :, pl.ds(start, width)], part) for start, part in zip(starts, parts)]
+    run_copies([*pairs, (signal.at[pl.ds(0, 8), :], first_rows)], sems)
+
+
+def rest_cut_kernel(flips, whole, *refs):
     *parts, held, sems, out_sems = refs
-    count, width = held.shape[0], held.shape[3]
+    width = held.shape[3]
     own = lax.axis_index("tm")
     reads, writes = [], []
-    for k in range(count):
-        start = pl.multiple_of((own ^ k) * width, width)
+    for k, flip in enumerate(flips):
+        start = pl.multiple_of((own ^ flip) * width, width)
         reads.append(pltpu.make_async_copy(whole.at[:, :, pl.ds(start, width)], held.at[k], sems.at[k]))
         writes.append(pltpu.make_async_copy(held.at[k], parts[k], out_sems.at[k]))
     for read in reads:
@@ -269,7 +280,15 @@
 
 def forward_kernel(*refs):
     sources, outs, rest = refs[:10], refs[10:21], refs[21:]
-    *held, sems, spread, patches = rest
+    *held, sems, out_sems, spread, patches = rest
+    held, bufs = held[:10], held[10:]
+    writes = []
+
+    def put(number):
+        write = pltpu.make_async_copy(bufs[number], outs[number], out_sems.at[number])
+        write.start()
+        writes.append(write)
+
     (
         proj_t,
         patch_t,
@@ -282,7 +301,7 @@
         inv_n,
         unit_out,
         row_inv,
-    ) = outs
+    ) = bufs
     loads = Loads(sources, held, sems)
     feat, halo, conv_bias, norm_gain, norm_bias = loads.take(5)
     frames = feat.shape[0] // 4
@@ -299,31 +318,45 @@
             piece = rows[2 * parity + tap]
             patches[parity * frames : (parity + 1) * frames, tap * channels : (tap + 1) * channels] = piece
             patch_t[tap * channels : (tap + 1) * channels, parity * frames : (parity + 1) * frames] = piece.T
+    put(1)
     (conv_wide,) = loads.take(1)
     conv = dot(patches[...], conv_wide[...]) + conv_bias[0:1, :]
     normed, inverse = normalized(conv)
     normed_w[...] = normed
     inv_w[...] = jnp.broadcast_to(inverse, inv_w.shape)
+    put(3)
+    put(5)
     act, slope = gelu_parts(normed * norm_gain[0:1, :] + norm_bias[0:1, :])
     slope_w[...] = slope * norm_gain[0:1, :]
+    put(4)
     act = act.astype(BF16)
     even, odd = act[:frames], act[frames:]
     act_t[0:channels, :] = even.T
     act_t[channels:, :] = odd.T
+    put(2)
     (conv_narrow,) = loads.take(1)
     conv = dot(even, conv_narrow[0:channels, :]) + dot(odd, conv_narrow[channels:, :]) + conv_bias[1:2, :]
     normed, inverse = normalized(conv)
     normed_n[...] = normed
     inv_n[...] = jnp.broadcast_to(inverse, inv_n.shape)
+    put(6)
+    put(8)
     act, slope = gelu_parts(normed * norm_gain[1:2, :] + norm_bias[1:2, :])
     slope_n[...] = slope * norm_gain[1:2, :]
+    put(7)
     unit, inverse = normalized(act.astype(BF16).astype(F32))
     unit_out[...] = unit
     row_inv[...] = jnp.broadcast_to(inverse, row_inv.shape)
+    put(9)
+    put(10)
     proj_gain, proj_bias, proj_weight = loads.take(3)
     normed_in = (unit * proj_gain[...]).astype(BF16)
-    projected = dot(normed_in, proj_weight[...]) + proj_bias[...]
+    bias = jnp.concatenate([proj_bias[k : k + 1, :] for k in range(proj_bias.shape[0])], axis=1)
+    projected = dot(normed_in, proj_weight[...]) + bias
     proj_t[...] = projected.astype(BF16).T
+    put(0)
+    for write in writes:
+        write.wait()
 
 
 def owned_rows(left, owner, outer):
@@ -351,7 +384,7 @@
     outer = send.shape[0]
     own = lax.axis_index("tm")
     rows = sources[1].shape[0]
-    places = [grad_t.at[pl.ds(pl.multiple_of((own ^ k) * rows, rows), rows), :] for k in range(tm)]
+    places = [grad_t.at[pl.ds(pl.multiple_of((own ^ k) * rows, rows), rows), :] for k in ORDER]
     other = 1 - lax.axis_index("dp") % 2
     lefts = [rows for left in sources[-2:] for rows in owned_rows(left, other, outer)]
     loads = Loads([*sources[:-2], *lefts], [held[0], *places, *held[1:]], sems)
@@ -473,7 +506,7 @@
     recs_local, length, channels = features.shape
     pairs, frames_total, depth = upstream.shape
     frames = frames_total // tm
-    if not (dp == 4 and tm == 8 and recs_local == 1 and frames % 128 == 0 and pairs * tm == HEADS):
+    if not (dp == 4 and tm == 8 and recs_local == 1 and frames % 128 == 0 and HEADS * depth % 128 == 0 and pairs * tm == HEADS):
         return generic_shards(
             features,
             conv_wide,
@@ -489,21 +522,32 @@
     width = HEADS * depth
     factor = 1.0 / math.sqrt(recs_local * dp * frames_total)
     sems = [pltpu.SemaphoreType.DMA((tm,))]
-    cuts = local(
-        cut_kernel,
+    signal = features.reshape(length, channels)
+    frames_cut = (pairs, depth, frames)
+    early = (1, 6)
+    late = [k for k in range(tm) if k not in early]
+    *cuts, first_rows = local(
+        lambda *refs: first_cut_kernel(early, *refs),
+        [upstream.transpose(0, 2, 1), signal],
+        [(frames_cut, BF16, True)] * len(early) + [((8, channels), BF16, True)],
+        "cut",
+        scratch=[pltpu.SemaphoreType.DMA((len(early) + 1,))],
+        raw=(0, 1),
+    )
+    cuts += local(
+        lambda *refs: rest_cut_kernel(late, *refs),
         [upstream.transpose(0, 2, 1)],
-        [((pairs, depth, frames), BF16, False)] * tm,
-        "cut",
-        scratch=[pltpu.VMEM((tm, pairs, depth, frames), BF16)] + sems * 2,
+        [(frames_cut, BF16, False)] * len(late),
+        "rest_cut",
+        scratch=[pltpu.VMEM((len(late), *frames_cut), BF16)] + [pltpu.SemaphoreType.DMA((len(late),))] * 2,
         raw=(0,),
-        raw_out=range(tm),
-    )
-    cuts = [cut.reshape(pairs * depth, frames) for cut in cuts]
+        raw_out=range(len(late)),
+    )
+    cuts = {k: cut.reshape(pairs * depth, frames) for k, cut in zip([*early, *late], cuts)}
     heads_in = {0: cuts[0]}
-    for k in (6, 7, 4, 5, 2, 3, 1):
+    for k in ORDER[1:]:
         heads_in[k] = swap(cuts[k], 0, 0, k // 2, k % 2)
-    signal = features.reshape(length, channels)
-    halo = passed_along(signal[:8], "tm", -1)
+    halo = passed_along(first_rows, "tm", -1)
     wide_rows = 2 * frames
     spread = pltpu.VMEM((channels // 128, length, 128), F32)
     gain = proj_gain.reshape(1, channels)
@@ -516,36 +560,40 @@
         conv_wide,
         conv_narrow,
         gain,
-        proj_bias.reshape(1, width),
+        proj_bias.reshape(width // 128, 128),
         proj_weight,
+    ]
+    forward_out = [
+        ((width, frames), BF16, False),
+        ((3 * channels, wide_rows), BF16, False),
+        ((2 * channels, frames), BF16, False),
+        ((wide_rows, channels), F32, False),
+        ((wide_rows, channels), F32, False),
+        ((wide_rows, 128), F32, False),
+        ((frames, channels), F32, False),
+        ((frames, channels), F32, False),
+        ((frames, 128), F32, False),
+        ((frames, channels), F32, False),
+        ((frames, 128), F32, False),
     ]
     proj_t, *stored = local(
         forward_kernel,
         forward_in,
-        [
-            ((width, frames), BF16, False),
-            ((3 * channels, wide_rows), BF16, False),
-            ((2 * channels, frames), BF16, False),
-            ((wide_rows, channels), F32, False),
-            ((wide_rows, channels), F32, False),
-            ((wide_rows, 128), F32, False),
-            ((frames, channels), F32, False),
-            ((frames, channels), F32, False),
-            ((frames, 128), F32, False),
-            ((frames, channels), F32, False),
-            ((frames, 128), F32, False),
-        ],
+        forward_out,
         "forward",
-        limit=32,
+        limit=40,
         scratch=[pltpu.VMEM(x.shape, x.dtype) for x in forward_in]
+        + [pltpu.VMEM(shape, dtype) for shape, dtype, _ in forward_out]
         + [
             pltpu.SemaphoreType.DMA((len(forward_in),)),
+            pltpu.SemaphoreType.DMA((len(forward_out),)),
             spread,
             pltpu.VMEM((wide_rows, 3 * channels), BF16),
         ],
         raw=range(len(forward_in)),
-    )
-    proj_t, heads_in[4] = lax.optimization_barrier((proj_t, heads_in[4]))
+        raw_out=range(len(forward_out)),
+    )
+    proj_t, heads_in[1] = lax.optimization_barrier((proj_t, heads_in[1]))
     heads = lax.all_to_all(
         proj_t.reshape(tm, pairs * depth, frames), "tm", split_axis=0, concat_axis=0, tiled=True
     )
@@ -555,7 +603,7 @@
     patch_t, act_t, normed_w, slope_w, inv_w, normed_n, slope_n, inv_n, unit, row_inv = stored
     inputs = [
         proj_weight,
-        *[heads_in[k] for k in range(tm)],
+        *[heads_in[k] for k in ORDER],
         gain,
         unit,
         row_inv,
@@ -584,6 +632,7 @@
         limit=24,
         scratch=held + [grad_buf, pltpu.SemaphoreType.DMA((len(held) + tm,))],
         raw=range(len(inputs)),
+        free=range(1, tm + 1),
     )
     received = swap(send, 0, 1, 0, 0)
     held = lefts + [pltpu.VMEM((channels, channels), BF16)]
@@ -597,7 +646,7 @@
     )
     plane = ((tm // 2, part_rows, channels), BF16, True)
     own, *outgoing = local(first_sum_kernel, [keep, received], [plane] * 4, "first_sum")
-    arrived = [swap(value, k // 2, 0, 0, k % 2) for k, value in enumerate(outgoing, 1)]
+    arrived = [swap(outgoing[k - 1], k // 2, 0, 0, k % 2) for k in (3, 1, 2)]
     tail, grad_conv, own = lax.optimization_barrier((tail, grad_conv, own))
     incoming = passed_along(tail, "tm", 1)
     feature_grad, first_rows = local(
@@ -616,9 +665,9 @@
         scratch=sems,
         raw_out=(0,),
     )
-    attn_t, first_rows, own = lax.optimization_barrier((attn_t, first_rows, own))
+    attn_t, first_rows, incoming, own = lax.optimization_barrier((attn_t, first_rows, incoming, own))
     own, *outgoing = local(second_sum_kernel, [own, *arrived], [piece] * 4, "second_sum")
-    arrived = [swap(value, 0, 0, k, 0) for k, value in enumerate(outgoing, 1)]
+    arrived = [swap(outgoing[k - 1], 0, 0, k, 0) for k in (2, 3, 1)]
     own_wide = 3 * channels // (dp * tm)
     wide, narrow, feature_grad = local(
         lambda *refs: last_sum_kernel(own_wide, *refs),

time: 78.1 us -> 74.4 us (0.953)
  local copies, waits for them, and re-layouts: 2.79 us -> 0.01 us
  starting transfers between devices: 33.6 us -> 32.2 us
    ppermute x2, waiting for transfers between devices: 1.5 us -> 5.32 us  [passed_along(): lax.ppermute(value, axis, [(source, source + steps) for source in range(l...]
    all_to_all x1, waiting for transfers between devices: 6.24 us -> 3.07 us  [shards(): lax.all_to_all(proj_t.reshape(tm, pairs * depth, frames), 'tm', split_axi...]
    ppermute x14, starting transfers between devices: 24.8 us -> 23.1 us  [swap(): return lax.ppermute(value, ('dp', 'tm'), flipped(dy, dc, dz, dx))]
    reshape x1 -> x0, local copies, waits for them, and re-layouts: 1.3 us -> none  [shards(): proj_bias.reshape(1, width)]
    unnamed x18 -> x6, local copies, waits for them, and re-layouts: 0.8 us -> 0.01 us
    pallas_call x9 -> x10, Pallas kernels: 22.7 us -> 22.9 us  [local(): pl.pallas_call(kernel, out_shape=out_shape, in_specs=[pl.BlockSpec(memory...]
  transfers between devices with their start and end apart: 17 -> 17, of which waited for: 6 -> 8; matrix products, arithmetic and copies ran while one was open for 3% -> 0% of each run, Pallas kernels for 25% -> 28%
where the time goes in v3:
time: 74.4 us; the launch traced here: 74.1 us
  starting transfers between devices  32.2 us (43%)
  Pallas kernels  22.9 us (31%)
  waiting for transfers between devices  18.2 us (24%)
  between operations  0.76 us (1%)
    ppermute x14, starting transfers between devices, swap(): return lax.ppermute(value, ('dp', 'tm'), flipped(dy, dc, dz, dx))  23.1 us
    pallas_call x10, Pallas kernels, local(): pl.pallas_call(kernel, out_shape=out_shape, in_specs=[pl.BlockSpec(memory...  22.9 us
    ppermute x14, waiting for transfers between devices, swap(): return lax.ppermute(value, ('dp', 'tm'), flipped(dy, dc, dz, dx))  9.79 us
    ppermute x2, waiting for transfers between devices, passed_along(): lax.ppermute(value, axis, [(source, source + steps) for source in range(l...  5.32 us
    all_to_all x1, starting transfers between devices, shards(): lax.all_to_all(proj_t.reshape(tm, pairs * depth, frames), 'tm', split_axi...  5.03 us
    ppermute x2, starting transfers between devices, passed_along(): lax.ppermute(value, axis, [(source, source + steps) for source in range(l...  4.06 us
    all_to_all x1, waiting for transfers between devices, shards(): lax.all_to_all(proj_t.reshape(tm, pairs * depth, frames), 'tm', split_axi...  3.07 us
  transfers between devices with their start and end apart: 17, of which 8 were waited for; matrix products, arithmetic and copies ran while one was open for 0% of the time, Pallas kernels for 28%

profile of v3, /device:TPU:0, one launch (start us, length us, event | category | flops | bytes accessed | tf_op | source)
XLA Modules:
  0.0 74.1 jit_solution(7564502477763290163)
XLA Ops:
  0.6 1.0 %cut.1 = (bf16[2,120,256]{2,1,0:T(8,128)(2,1)S(1)}, bf16[2,120,256]{2,1,0:T(8,128)(2,1)S(1)}, bf16[8,512]{1,0:T(8,128)(2,1)S(1)}) custom-call(bf16[2,120,2048]{2,1,0:T(8,128)(2,1)} %bitcast.24, bf16[1024,512]{1,0:T(8,128)(2,1)} %bitcast.22), custom_call_target="tpu_custom_call" | custom-call | flops 1000 | tf_op jit(solution)/shard_map/cut/pallas_call | solution.py:200
  1.6 3.0 %collective-permute-start.1 = (bf16[240,256]{1,0:T(8,128)(2,1)S(1)}, bf16[240,256]{1,0:T(8,128)(2,1)S(1)}, u32[]{:S(2)}, u32[]{:S(2)}) collective-permute-start(bf16[240,256]{1,0:T(8,128)(2,1)S(1)} %bitcast.21), channel_id=1, source_target_pairs={{0,1},{1,0},{2,3},{3,2},{4,5},{5,4},{6,7},{7,6},{8,9},{9,8},{10,11... | collective-permute-start | bytes 368648 | tf_op jit(solution)/shard_map/ppermute | solution.py:490
  4.6 3.6 %collective-permute-start.2 = (bf16[240,256]{1,0:T(8,128)(2,1)S(1)}, bf16[240,256]{1,0:T(8,128)(2,1)S(1)}, u32[]{:S(2)}, u32[]{:S(2)}) collective-permute-start(bf16[240,256]{1,0:T(8,128)(2,1)S(1)} %bitcast.20), channel_id=1, source_target_pairs={{0,6},{1,7},{2,4},{3,5},{4,2},{5,3},{6,0},{7,1},{8,14},{9,15},{10,... | collective-permute-start | bytes 368648 | tf_op jit(solution)/shard_map/ppermute | solution.py:490
  8.2 1.3 %collective-permute-start = (bf16[8,512]{1,0:T(8,128)(2,1)S(1)}, bf16[8,512]{1,0:T(8,128)(2,1)S(1)}, u32[]{:S(2)}, u32[]{:S(2)}) collective-permute-start(bf16[8,512]{1,0:T(8,128)(2,1)S(1)} %get-tuple-element.51), channel_id=1, source_target_pairs={{1,0},{2,1},{3,2},{4,3},{5,4},{6,5},{7,6},{9,8},{10,9},{11,10},{12... | collective-permute-start | bytes 24584 | tf_op jit(solution)/shard_map/ppermute | solution.py:22
  9.5 2.0 %rest_cut.1 = (bf16[2,120,256]{2,1,0:T(8,128)(2,1)}, bf16[2,120,256]{2,1,0:T(8,128)(2,1)}, bf16[2,120,256]{2,1,0:T(8,128)(2,1)}, bf16[2,120,256]{2,1,0:T(8,128)(...) custom-call(bf16[2,120,2048]{2,1,0:T(8,128)(2,1)} %bitcast.25), custom_call_target="tpu_custom_call" | custom-call | flops 1000 | tf_op jit(solution)/shard_map/rest_cut/pallas_call | solution.py:200
  11.5 2.4 %collective-permute-start.3 = (bf16[240,256]{1,0:T(8,128)(2,1)}, bf16[240,256]{1,0:T(8,128)(2,1)S(1)}, u32[]{:S(2)}, u32[]{:S(2)}) collective-permute-start(bf16[240,256]{1,0:T(8,128)(2,1)} %bitcast.36), channel_id=1, source_target_pairs={{0,7},{1,6},{2,5},{3,4},{4,3},{5,2},{6,1},{7,0},{8,15},{9,14},{10,... | collective-permute-start | bytes 368648 | tf_op jit(solution)/shard_map/ppermute | solution.py:490
  13.9 0.8 %collective-permute-start.4 = (bf16[240,256]{1,0:T(8,128)(2,1)}, bf16[240,256]{1,0:T(8,128)(2,1)S(1)}, u32[]{:S(2)}, u32[]{:S(2)}) collective-permute-start(bf16[240,256]{1,0:T(8,128)(2,1)} %bitcast.35), channel_id=1, source_target_pairs={{0,4},{1,5},{2,6},{3,7},{4,0},{5,1},{6,2},{7,3},{8,12},{9,13},{10,... | collective-permute-start | bytes 368648 | tf_op jit(solution)/shard_map/ppermute | solution.py:490
  14.7 0.0 collective-permute-done.refs_1_
  14.7 0.0 copy-start.2
  14.7 2.2 %collective-permute-start.5 = (bf16[240,256]{1,0:T(8,128)(2,1)}, bf16[240,256]{1,0:T(8,128)(2,1)S(1)}, u32[]{:S(2)}, u32[]{:S(2)}) collective-permute-start(bf16[240,256]{1,0:T(8,128)(2,1)} %bitcast.34), channel_id=1, source_target_pairs={{0,5},{1,4},{2,7},{3,6},{4,1},{5,0},{6,3},{7,2},{8,13},{9,12},{10,... | collective-permute-start | bytes 368648 | tf_op jit(solution)/shard_map/ppermute | solution.py:490
  16.9 0.0 collective-permute-done.1.refs_8_
  16.9 1.2 %collective-permute-start.6 = (bf16[240,256]{1,0:T(8,128)(2,1)}, bf16[240,256]{1,0:T(8,128)(2,1)S(1)}, u32[]{:S(2)}, u32[]{:S(2)}) collective-permute-start(bf16[240,256]{1,0:T(8,128)(2,1)} %bitcast.33), channel_id=1, source_target_pairs={{0,2},{1,3},{2,0},{3,1},{4,6},{5,7},{6,4},{7,5},{8,10},{9,11},{10,... | collective-permute-start | bytes 368648 | tf_op jit(solution)/shard_map/ppermute | solution.py:490
  18.1 0.0 collective-permute-done.2.refs_2_
  18.1 1.6 %collective-permute-start.7 = (bf16[240,256]{1,0:T(8,128)(2,1)}, bf16[240,256]{1,0:T(8,128)(2,1)S(1)}, u32[]{:S(2)}, u32[]{:S(2)}) collective-permute-start(bf16[240,256]{1,0:T(8,128)(2,1)} %bitcast.32), channel_id=1, source_target_pairs={{0,3},{1,2},{2,1},{3,0},{4,7},{5,6},{6,5},{7,4},{8,11},{9,10},{10,... | collective-permute-start | bytes 368648 | tf_op jit(solution)/shard_map/ppermute | solution.py:490
  19.7 0.0 copy-done.2
  19.7 6.5 %forward.1 = (bf16[1920,256]{1,0:T(8,128)(2,1)}, bf16[1536,512]{1,0:T(8,128)(2,1)}, bf16[1024,256]{1,0:T(8,128)(2,1)}, f32[512,512]{1,0:T(8,128)}, f32[512,512]{...) custom-call(bf16[1024,512]{1,0:T(8,128)(2,1)} %bitcast.23, ...), custom_call_target="tpu_custom_call" | custom-call | flops 1000 | tf_op jit(solution)/shard_map/forward/pallas_call | solution.py:200
  26.3 0.0 copy-start.1
  26.3 5.0 %all-to-all-start = ((bf16[8,240,256]{2,1,0:T(8,128)(2,1)}), bf16[8,240,256]{2,1,0:T(8,128)(2,1)S(1)}, u32[]{:S(2)}, u32[]{:S(2)}) async-start(bf16[8,240,256]{2,1,0:T(8,128)(2,1)} %bitcast.27), calls=%async_computation | async-start | bytes 1966080 | tf_op jit(solution)/shard_map/all_to_all | solution.py:597
  31.3 0.0 collective-permute-done.3.refs_3_
  31.3 0.0 collective-permute-done.4.refs_4_
  31.3 1.2 %collective-permute-done.5.refs_5_ = bf16[240,256]{1,0:T(8,128)(2,1)S(1)} collective-permute-done((bf16[240,256]{1,0:T(8,128)(2,1)}, bf16[240,256]{1,0:T(8,128)(2,1)S(1)}, u32[]{:S(2)}, u32[]{:S(2)}) %collective-permute-start.5) | collective-permute-done | bytes 122912 | tf_op jit(solution)/shard_map/ppermute | solution.py:490
  32.5 0.0 collective-permute-done.6.refs_6_
  32.5 0.0 collective-permute-done.7.refs_7_
  32.5 0.0 copy-done.1
  32.5 6.2 %backward.1 = (bf16[2,8,80,512]{3,2,1,0:T(8,128)(2,1)S(1)}, bf16[512,512]{1,0:T(8,128)(2,1)S(1)}, bf16[256,512]{1,0:T(8,128)(2,1)S(1)}) custom-call(bf16[512,1920]{1,0:T(8,128)(2,1)} %refs_0_.1, bf16[240,256]{1,0:T(8,128)(2,1)S(1)} %bitcast.19, bf16[240,256]{1,0:T(8,128)(2,1)S(1)} %collective-permute-done.2.refs_2_, ...), custom_call_target="tpu_custom_call" | custom-call | flops 1000 | tf_op jit(solution)/shard_map/backward/pallas_call | solution.py:200
  38.7 0.1 collective-permute-start.8
  38.8 2.3 %own_grad.1 = (bf16[2,8,80,512]{3,2,1,0:T(8,128)(2,1)S(1)}, f32[8,512]{1,0:T(8,128)S(1)}) custom-call(bf16[1536,512]{1,0:T(8,128)(2,1)} %get-tuple-element.55.refs_19_.refs_0_, bf16[1024,256]{1,0:T(8,128)(2,1)} %get-tuple-element.56.refs_20_.refs_1_, bf16[1536,512]{1,0:T(8,128)(2,1)} %conv_wide.1, bf16[512,512]{1,0:T(8,128)(2,1)S(1)} %get-tuple-element.79.refs_3_.grad_conv, ...), custom_call_target="tpu_custom_call" | custom-call | flops 1000 | tf_op jit(solution)/shard_map/own_grad/pallas_call | solution.py:200
  41.1 0.0 copy-start
  41.1 0.7 collective-permute-done.8.received
  41.8 0.3 first_sum.1
  42.1 1.9 %collective-permute-start.10 = (bf16[4,80,512]{2,1,0:T(8,128)(2,1)S(1)}, bf16[4,80,512]{2,1,0:T(8,128)(2,1)S(1)}, u32[]{:S(2)}, u32[]{:S(2)}) collective-permute-start(bf16[4,80,512]{2,1,0:T(8,128)(2,1)S(1)} %get-tuple-element.85), channel_id=1, source_target_pairs={{0,17},{1,16},{2,19},{3,18},{4,21},{5,20},{6,23},{7,22},{8,25},{9,... | collective-permute-start | bytes 983048 | tf_op jit(solution)/shard_map/ppermute | solution.py:490
  44.0 1.1 %collective-permute-start.11 = (bf16[4,80,512]{2,1,0:T(8,128)(2,1)S(1)}, bf16[4,80,512]{2,1,0:T(8,128)(2,1)S(1)}, u32[]{:S(2)}, u32[]{:S(2)}) collective-permute-start(bf16[4,80,512]{2,1,0:T(8,128)(2,1)S(1)} %get-tuple-element.86), channel_id=1, source_target_pairs={{0,1},{1,0},{2,3},{3,2},{4,5},{5,4},{6,7},{7,6},{8,9},{9,8},{10,11... | collective-permute-start | bytes 983048 | tf_op jit(solution)/shard_map/ppermute | solution.py:490
  45.2 0.5 collective-permute-start.12
  45.7 2.8 %collective-permute-start.9 = (f32[8,512]{1,0:T(8,128)S(1)}, f32[8,512]{1,0:T(8,128)S(1)}, u32[]{:S(2)}, u32[]{:S(2)}) collective-permute-start(f32[8,512]{1,0:T(8,128)S(1)} %get-tuple-element.81), channel_id=1, source_target_pairs={{0,1},{1,2},{2,3},{3,4},{4,5},{5,6},{6,7},{8,9},{9,10},{10,11},{11... | collective-permute-start | bytes 49160 | tf_op jit(solution)/shard_map/ppermute | solution.py:22
  48.5 0.0 copy-done
  48.5 2.2 %input_grad.1 = (bf16[1024,512]{1,0:T(8,128)(2,1)}, f32[8,512]{1,0:T(8,128)S(1)}) custom-call(bf16[512,512]{1,0:T(8,128)(2,1)S(1)} %get-tuple-element.79.refs_3_.grad_conv, bf16[1536,512]{1,0:T(8,128)(2,1)S(1)} %copy-done), custom_call_target="tpu_custom_call" | custom-call | flops 1000 | tf_op jit(solution)/shard_map/input_grad/pallas_call | solution.py:200
  50.6 3.1 %all-to-all-done = bf16[8,240,256]{2,1,0:T(8,128)(2,1)S(1)} async-done(((bf16[8,240,256]{2,1,0:T(8,128)(2,1)}), bf16[8,240,256]{2,1,0:T(8,128)(2,1)S(1)}, u32[]{:S(2)}, u32[]{:S(2)}) %all-to-all-start) | async-done | bytes 983072 | tf_op jit(solution)/shard_map/all_to_all | solution.py:597
  53.7 1.0 %join.1 = bf16[2,120,2048]{2,1,0:T(8,128)(2,1)} custom-call(bf16[8,2,120,256]{3,2,1,0:T(8,128)(2,1)S(1)} %bitcast.18), custom_call_target="tpu_custom_call" | custom-call | flops 1000 | tf_op jit(solution)/shard_map/join/pallas_call | solution.py:200
  54.7 5.3 %collective-permute-done.9.refs_4_ = f32[8,512]{1,0:T(8,128)S(1)} collective-permute-done((f32[8,512]{1,0:T(8,128)S(1)}, f32[8,512]{1,0:T(8,128)S(1)}, u32[]{:S(2)}, u32[]{:S(2)}) %collective-permute-start.9) | collective-permute-done | bytes 16416 | tf_op jit(solution)/shard_map/ppermute | solution.py:22
  60.0 0.0 collective-permute-done.10.b
  60.0 1.2 %collective-permute-done.11.c = bf16[4,80,512]{2,1,0:T(8,128)(2,1)S(1)} collective-permute-done((bf16[4,80,512]{2,1,0:T(8,128)(2,1)S(1)}, bf16[4,80,512]{2,1,0:T(8,128)(2,1)S(1)}, u32[]{:S(2)}, u32[]{:S(2)}) %collective-permute-start.11) | collective-permute-done | bytes 327712 | tf_op jit(solution)/shard_map/ppermute | solution.py:490
  61.3 0.0 collective-permute-done.12.d
  61.3 0.2 second_sum.1
  61.4 3.9 %collective-permute-start.13 = (bf16[80,512]{1,0:T(8,128)(2,1)S(1)}, bf16[80,512]{1,0:T(8,128)(2,1)S(1)}, u32[]{:S(2)}, u32[]{:S(2)}) collective-permute-start(bf16[80,512]{1,0:T(8,128)(2,1)S(1)} %get-tuple-element.89), channel_id=1, source_target_pairs={{0,4},{1,5},{2,6},{3,7},{4,0},{5,1},{6,2},{7,3},{8,12},{9,13},{10,... | collective-permute-start | bytes 245768 | tf_op jit(solution)/shard_map/ppermute | solution.py:490
  65.3 0.8 %collective-permute-start.14 = (bf16[80,512]{1,0:T(8,128)(2,1)S(1)}, bf16[80,512]{1,0:T(8,128)(2,1)S(1)}, u32[]{:S(2)}, u32[]{:S(2)}) collective-permute-start(bf16[80,512]{1,0:T(8,128)(2,1)S(1)} %get-tuple-element.90), channel_id=1, source_target_pairs={{0,6},{1,7},{2,4},{3,5},{4,2},{5,3},{6,0},{7,1},{8,14},{9,15},{10,... | collective-permute-start | bytes 245768 | tf_op jit(solution)/shard_map/ppermute | solution.py:490
  66.1 0.0 collective-permute-start.15
  66.1 5.5 %collective-permute-done.13.refs_1_ = bf16[80,512]{1,0:T(8,128)(2,1)S(1)} collective-permute-done((bf16[80,512]{1,0:T(8,128)(2,1)S(1)}, bf16[80,512]{1,0:T(8,128)(2,1)S(1)}, u32[]{:S(2)}, u32[]{:S(2)}) %collective-permute-start.13) | collective-permute-done | bytes 81952 | tf_op jit(solution)/shard_map/ppermute | solution.py:490
  71.7 0.5 collective-permute-done.14.refs_2_
  72.1 0.7 collective-permute-done.15.refs_3_
  72.8 1.3 %last_sum.1 = (f32[192,128]{1,0:T(8,128)}, f32[128,128]{1,0:T(8,128)}, bf16[1024,512]{1,0:T(8,128)(2,1)}) custom-call(bf16[80,512]{1,0:T(8,128)(2,1)S(1)} %get-tuple-element.88.refs_0_, bf16[80,512]{1,0:T(8,128)(2,1)S(1)} %collective-permute-done.13.refs_1_, bf16[80,512]{1,0:T(8,128)(2,1)S(1)} %collective-permute-done.14.refs_2_, ...), custom_call_target="tpu_custom_call", output_to_operand_aliasing={{2}: (6, {})} | custom-call | flops 1000 | tf_op jit(solution)/shard_map/last_sum/pallas_call | solution.py:200
Async XLA Ops:
  1.6 15.3 %collective-permute-start.1 = (bf16[240,256]{1,0:T(8,128)(2,1)S(1)}, bf16[240,256]{1,0:T(8,128)(2,1)S(1)}, u32[]{:S(2)}, u32[]{:S(2)}) collective-permute-start(bf16[240,256]{1,0:T(8,128)(2,1)S(1)} %bitcast.21), channel_id=1, source_target_pairs={{0,1},{1,0},{2,3},{3,2},{4,5},{5,4},{6,7},{7,6},{8,9},{9,8},{10,11... | collective-permute-start | bytes 368648 | tf_op jit(solution)/shard_map/ppermute | solution.py:490
  4.6 13.5 %collective-permute-start.2 = (bf16[240,256]{1,0:T(8,128)(2,1)S(1)}, bf16[240,256]{1,0:T(8,128)(2,1)S(1)}, u32[]{:S(2)}, u32[]{:S(2)}) collective-permute-start(bf16[240,256]{1,0:T(8,128)(2,1)S(1)} %bitcast.20), channel_id=1, source_target_pairs={{0,6},{1,7},{2,4},{3,5},{4,2},{5,3},{6,0},{7,1},{8,14},{9,15},{10,... | collective-permute-start | bytes 368648 | tf_op jit(solution)/shard_map/ppermute | solution.py:490
  8.2 6.4 %collective-permute-start = (bf16[8,512]{1,0:T(8,128)(2,1)S(1)}, bf16[8,512]{1,0:T(8,128)(2,1)S(1)}, u32[]{:S(2)}, u32[]{:S(2)}) collective-permute-start(bf16[8,512]{1,0:T(8,128)(2,1)S(1)} %get-tuple-element.51), channel_id=1, source_target_pairs={{1,0},{2,1},{3,2},{4,3},{5,4},{6,5},{7,6},{9,8},{10,9},{11,10},{12... | collective-permute-start | bytes 24584 | tf_op jit(solution)/shard_map/ppermute | solution.py:22
  11.5 19.8 %collective-permute-start.3 = (bf16[240,256]{1,0:T(8,128)(2,1)}, bf16[240,256]{1,0:T(8,128)(2,1)S(1)}, u32[]{:S(2)}, u32[]{:S(2)}) collective-permute-start(bf16[240,256]{1,0:T(8,128)(2,1)} %bitcast.36), channel_id=1, source_target_pairs={{0,7},{1,6},{2,5},{3,4},{4,3},{5,2},{6,1},{7,0},{8,15},{9,14},{10,... | collective-permute-start | bytes 368648 | tf_op jit(solution)/shard_map/ppermute | solution.py:490
  13.9 17.4 %collective-permute-start.4 = (bf16[240,256]{1,0:T(8,128)(2,1)}, bf16[240,256]{1,0:T(8,128)(2,1)S(1)}, u32[]{:S(2)}, u32[]{:S(2)}) collective-permute-start(bf16[240,256]{1,0:T(8,128)(2,1)} %bitcast.35), channel_id=1, source_target_pairs={{0,4},{1,5},{2,6},{3,7},{4,0},{5,1},{6,2},{7,3},{8,12},{9,13},{10,... | collective-permute-start | bytes 368648 | tf_op jit(solution)/shard_map/ppermute | solution.py:490
  14.7 5.1 %copy-start.2 = (bf16[8,512]{1,0:T(8,128)(2,1)}, bf16[8,512]{1,0:T(8,128)(2,1)S(1)}, u32[]{:S(2)}) copy-start(bf16[8,512]{1,0:T(8,128)(2,1)S(1)} %collective-permute-done.refs_1_) | copy-start | bytes 24580
  14.7 17.8 %collective-permute-start.5 = (bf16[240,256]{1,0:T(8,128)(2,1)}, bf16[240,256]{1,0:T(8,128)(2,1)S(1)}, u32[]{:S(2)}, u32[]{:S(2)}) collective-permute-start(bf16[240,256]{1,0:T(8,128)(2,1)} %bitcast.34), channel_id=1, source_target_pairs={{0,5},{1,4},{2,7},{3,6},{4,1},{5,0},{6,3},{7,2},{8,13},{9,12},{10,... | collective-permute-start | bytes 368648 | tf_op jit(solution)/shard_map/ppermute | solution.py:490
  16.9 15.6 %collective-permute-start.6 = (bf16[240,256]{1,0:T(8,128)(2,1)}, bf16[240,256]{1,0:T(8,128)(2,1)S(1)}, u32[]{:S(2)}, u32[]{:S(2)}) collective-permute-start(bf16[240,256]{1,0:T(8,128)(2,1)} %bitcast.33), channel_id=1, source_target_pairs={{0,2},{1,3},{2,0},{3,1},{4,6},{5,7},{6,4},{7,5},{8,10},{9,11},{10,... | collective-permute-start | bytes 368648 | tf_op jit(solution)/shard_map/ppermute | solution.py:490
  18.1 14.4 %collective-permute-start.7 = (bf16[240,256]{1,0:T(8,128)(2,1)}, bf16[240,256]{1,0:T(8,128)(2,1)S(1)}, u32[]{:S(2)}, u32[]{:S(2)}) collective-permute-start(bf16[240,256]{1,0:T(8,128)(2,1)} %bitcast.32), channel_id=1, source_target_pairs={{0,3},{1,2},{2,1},{3,0},{4,7},{5,6},{6,5},{7,4},{8,11},{9,10},{10,... | collective-permute-start | bytes 368648 | tf_op jit(solution)/shard_map/ppermute | solution.py:490
  26.3 6.2 %copy-start.1 = (bf16[2,120,256]{2,1,0:T(8,128)(2,1)S(1)}, bf16[2,120,256]{2,1,0:T(8,128)(2,1)}, u32[]{:S(2)}) copy-start(bf16[2,120,256]{2,1,0:T(8,128)(2,1)} %get-tuple-element.57) | copy-start | bytes 368644
  26.3 27.4 %all-to-all-start = ((bf16[8,240,256]{2,1,0:T(8,128)(2,1)}), bf16[8,240,256]{2,1,0:T(8,128)(2,1)S(1)}, u32[]{:S(2)}, u32[]{:S(2)}) async-start(bf16[8,240,256]{2,1,0:T(8,128)(2,1)} %bitcast.27), calls=%async_computation | async-start | bytes 1966080 | tf_op jit(solution)/shard_map/all_to_all | solution.py:597
  38.7 3.1 %collective-permute-start.8 = (bf16[2,8,80,512]{3,2,1,0:T(8,128)(2,1)S(1)}, bf16[2,8,80,512]{3,2,1,0:T(8,128)(2,1)S(1)}, u32[]{:S(2)}, u32[]{:S(2)}) collective-permute-start(bf16[2,8,80,512]{3,2,1,0:T(8,128)(2,1)S(1)} %get-tuple-element.77), channel_id=1, source_target_pairs={{0,8},{1,9},{2,10},{3,11},{4,12},{5,13},{6,14},{7,15},{8,0},{9,1},... | collective-permute-start | bytes 3932168 | tf_op jit(solution)/shard_map/ppermute | solution.py:490
  41.1 7.4 %copy-start = (bf16[1536,512]{1,0:T(8,128)(2,1)S(1)}, bf16[1536,512]{1,0:T(8,128)(2,1)}, u32[]{:S(2)}) copy-start(bf16[1536,512]{1,0:T(8,128)(2,1)} %conv_wide.1) | copy-start | bytes 4718596
  42.1 17.9 %collective-permute-start.10 = (bf16[4,80,512]{2,1,0:T(8,128)(2,1)S(1)}, bf16[4,80,512]{2,1,0:T(8,128)(2,1)S(1)}, u32[]{:S(2)}, u32[]{:S(2)}) collective-permute-start(bf16[4,80,512]{2,1,0:T(8,128)(2,1)S(1)} %get-tuple-element.85), channel_id=1, source_target_pairs={{0,17},{1,16},{2,19},{3,18},{4,21},{5,20},{6,23},{7,22},{8,25},{9,... | collective-permute-start | bytes 983048 | tf_op jit(solution)/shard_map/ppermute | solution.py:490
  44.0 17.2 %collective-permute-start.11 = (bf16[4,80,512]{2,1,0:T(8,128)(2,1)S(1)}, bf16[4,80,512]{2,1,0:T(8,128)(2,1)S(1)}, u32[]{:S(2)}, u32[]{:S(2)}) collective-permute-start(bf16[4,80,512]{2,1,0:T(8,128)(2,1)S(1)} %get-tuple-element.86), channel_id=1, source_target_pairs={{0,1},{1,0},{2,3},{3,2},{4,5},{5,4},{6,7},{7,6},{8,9},{9,8},{10,11... | collective-permute-start | bytes 983048 | tf_op jit(solution)/shard_map/ppermute | solution.py:490
  45.2 16.1 %collective-permute-start.12 = (bf16[4,80,512]{2,1,0:T(8,128)(2,1)S(1)}, bf16[4,80,512]{2,1,0:T(8,128)(2,1)S(1)}, u32[]{:S(2)}, u32[]{:S(2)}) collective-permute-start(bf16[4,80,512]{2,1,0:T(8,128)(2,1)S(1)} %get-tuple-element.87), channel_id=1, source_target_pairs={{0,16},{1,17},{2,18},{3,19},{4,20},{5,21},{6,22},{7,23},{8,24},{9,... | collective-permute-start | bytes 983048 | tf_op jit(solution)/shard_map/ppermute | solution.py:490
  45.7 14.4 %collective-permute-start.9 = (f32[8,512]{1,0:T(8,128)S(1)}, f32[8,512]{1,0:T(8,128)S(1)}, u32[]{:S(2)}, u32[]{:S(2)}) collective-permute-start(f32[8,512]{1,0:T(8,128)S(1)} %get-tuple-element.81), channel_id=1, source_target_pairs={{0,1},{1,2},{2,3},{3,4},{4,5},{5,6},{6,7},{8,9},{9,10},{10,11},{11... | collective-permute-start | bytes 49160 | tf_op jit(solution)/shard_map/ppermute | solution.py:22
  61.4 10.2 %collective-permute-start.13 = (bf16[80,512]{1,0:T(8,128)(2,1)S(1)}, bf16[80,512]{1,0:T(8,128)(2,1)S(1)}, u32[]{:S(2)}, u32[]{:S(2)}) collective-permute-start(bf16[80,512]{1,0:T(8,128)(2,1)S(1)} %get-tuple-element.89), channel_id=1, source_target_pairs={{0,4},{1,5},{2,6},{3,7},{4,0},{5,1},{6,2},{7,3},{8,12},{9,13},{10,... | collective-permute-start | bytes 245768 | tf_op jit(solution)/shard_map/ppermute | solution.py:490
  65.3 6.8 %collective-permute-start.14 = (bf16[80,512]{1,0:T(8,128)(2,1)S(1)}, bf16[80,512]{1,0:T(8,128)(2,1)S(1)}, u32[]{:S(2)}, u32[]{:S(2)}) collective-permute-start(bf16[80,512]{1,0:T(8,128)(2,1)S(1)} %get-tuple-element.90), channel_id=1, source_target_pairs={{0,6},{1,7},{2,4},{3,5},{4,2},{5,3},{6,0},{7,1},{8,14},{9,15},{10,... | collective-permute-start | bytes 245768 | tf_op jit(solution)/shard_map/ppermute | solution.py:490
  66.1 6.7 %collective-permute-start.15 = (bf16[80,512]{1,0:T(8,128)(2,1)S(1)}, bf16[80,512]{1,0:T(8,128)(2,1)S(1)}, u32[]{:S(2)}, u32[]{:S(2)}) collective-permute-start(bf16[80,512]{1,0:T(8,128)(2,1)S(1)} %get-tuple-element.91), channel_id=1, source_target_pairs={{0,2},{1,3},{2,0},{3,1},{4,6},{5,7},{6,4},{7,5},{8,10},{9,11},{10,... | collective-permute-start | bytes 245768 | tf_op jit(solution)/shard_map/ppermute | solution.py:490

commit v4 on v3

--- a/solution.py
+++ b/solution.py
@@ -159,7 +159,7 @@
 
 
 F32 = jnp.float32
-ORDER = (0, 6, 7, 4, 5, 2, 3, 1)
+ORDER = (0, 7, 6, 4, 5, 3, 2, 1)
 BF16 = jnp.bfloat16
 NT = (((1,), (1,)), ((), ()))
 
@@ -364,16 +364,14 @@
     return [left.at[pl.ds(pl.multiple_of((2 * block + owner) * part, part), part), :] for block in range(outer)]
 
 
-def weight_grad(loads, grads, factor, target):
-    outer, inner = target.shape[0], target.shape[1]
-    row = 0
-    for grad in grads:
-        for block, left in enumerate(loads.take(outer)):
-            value = (dot(left[...], grad) * factor).astype(BF16)
-            each = left.shape[0] // inner
-            for k in range(inner):
-                target[block, k, row : row + each, :] = value[k * each : (k + 1) * each]
-        row += each
+def weight_grad(loads, grad, factor, target, low):
+    outer, inner, height = target.shape[0], target.shape[1], target.shape[2]
+    for block, left in enumerate(loads.take(outer)):
+        value = (dot(left[...], grad) * factor).astype(BF16)
+        each = left.shape[0] // inner
+        row = height - each if low else 0
+        for k in range(inner):
+            target[block, k, row : row + each, :] = value[k * each : (k + 1) * each]
 
 
 def backward_kernel(factor, *refs):
@@ -386,10 +384,14 @@
     rows = sources[1].shape[0]
     places = [grad_t.at[pl.ds(pl.multiple_of((own ^ k) * rows, rows), rows), :] for k in ORDER]
     other = 1 - lax.axis_index("dp") % 2
-    lefts = [rows for left in sources[-2:] for rows in owned_rows(left, other, outer)]
-    loads = Loads([*sources[:-2], *lefts], [held[0], *places, *held[1:]], sems)
-    proj_weight, *_, proj_gain = loads.take(2 + tm)
-    grad_unit = dot(proj_weight[...], grad_t[...]).T * proj_gain[...]
+    wide_left, low_left = (owned_rows(left, other, outer) for left in sources[-2:])
+    cut = held[0].shape[1] * 8 // 15
+    halves = [pl.ds(0, cut), pl.ds(cut, held[0].shape[1] - cut)]
+    loads = Loads([*sources[1 : 1 + tm], *(sources[0].at[:, at] for at in halves), *sources[1 + tm : -5], *low_left, *sources[-5:-2], *wide_left], [*places, *(held[0].at[:, at] for at in halves), *held[1:]], sems)
+    loads.take(tm)
+    product = dot(loads.take(1)[0][...], grad_t[0:cut, :])
+    right, proj_gain = loads.take(2)
+    grad_unit = (product + dot(right[...], grad_t[cut:, :])).T * proj_gain[...]
     unit_in, row_inv = loads.take(2)
     frames, channels = unit_in.shape
     unit = unit_in[...]
@@ -401,6 +403,7 @@
         inv_n[:, 0:1] * (grad_normed - row_mean(grad_normed) - normed * row_mean(grad_normed * normed))
     ).astype(BF16)
     grad_low[...] = grad_narrow
+    weight_grad(loads, grad_narrow, factor, send, True)
     normed_w, slope_w, inv_w = loads.take(3)
     for parity in range(2):
         at = pl.ds(parity * frames, frames)
@@ -410,7 +413,7 @@
         grad_conv[at, :] = (
             inv_w[at, 0:1] * (grad_normed - row_mean(grad_normed) - normed * row_mean(grad_normed * normed))
         ).astype(BF16)
-    weight_grad(loads, (grad_conv[...], grad_narrow), factor, send)
+    weight_grad(loads, grad_conv[...], factor, send, False)
 
 
 def own_grad_kernel(factor, patch_t, act_t, conv_wide, grad_conv, grad_low, keep, tail, *rest):
@@ -421,7 +424,8 @@
     last_tap = held[-1].shape[0]
     loads = Loads([*lefts, conv_wide.at[pl.ds(2 * last_tap, last_tap), :]], held, sems)
     grad_wide = grad_conv[...]
-    weight_grad(loads, (grad_wide, grad_low[...]), factor, keep)
+    weight_grad(loads, grad_wide, factor, keep, False)
+    weight_grad(loads, grad_low[...], factor, keep, True)
     (tap,) = loads.take(1)
     tail[...] = dot_nt(grad_wide[grad_wide.shape[0] - 8 :, :], tap[...])
 
@@ -524,7 +528,7 @@
     sems = [pltpu.SemaphoreType.DMA((tm,))]
     signal = features.reshape(length, channels)
     frames_cut = (pairs, depth, frames)
-    early = (1, 6)
+    early = (1, 7)
     late = [k for k in range(tm) if k not in early]
     *cuts, first_rows = local(
         lambda *refs: first_cut_kernel(early, *refs),
@@ -622,7 +626,8 @@
         for x in (patch_t, act_t)
         for _ in range(outer)
     ]
-    held = [pltpu.VMEM(x.shape, x.dtype) for x in inputs[:1] + inputs[tm + 1 : -2]] + lefts
+    held = [pltpu.VMEM(x.shape, x.dtype) for x in inputs[:1] + inputs[tm + 1 : -2]]
+    held = held[:-3] + lefts[outer:] + held[-3:] + lefts[:outer]
     grad_buf = pltpu.VMEM((width, frames), BF16)
     send, grad_conv, grad_low = local(
         lambda *refs: backward_kernel(factor, *refs),
@@ -630,7 +635,7 @@
         [part, ((wide_rows, channels), BF16, True), ((frames, channels), BF16, True)],
         "backward",
         limit=24,
-        scratch=held + [grad_buf, pltpu.SemaphoreType.DMA((len(held) + tm,))],
+        scratch=held + [grad_buf, pltpu.SemaphoreType.DMA((len(held) + tm + 1,))],
         raw=range(len(inputs)),
         free=range(1, tm + 1),
     )
@@ -646,7 +651,7 @@
     )
     plane = ((tm // 2, part_rows, channels), BF16, True)
     own, *outgoing = local(first_sum_kernel, [keep, received], [plane] * 4, "first_sum")
-    arrived = [swap(outgoing[k - 1], k // 2, 0, 0, k % 2) for k in (3, 1, 2)]
+    arrived = [swap(outgoing[k - 1], k // 2, 0, 0, k % 2) for k in (3,2,1)]
     tail, grad_conv, own = lax.optimization_barrier((tail, grad_conv, own))
     incoming = passed_along(tail, "tm", 1)
     feature_grad, first_rows = local(
@@ -667,7 +672,7 @@
     )
     attn_t, first_rows, incoming, own = lax.optimization_barrier((attn_t, first_rows, incoming, own))
     own, *outgoing = local(second_sum_kernel, [own, *arrived], [piece] * 4, "second_sum")
-    arrived = [swap(outgoing[k - 1], 0, 0, k, 0) for k in (2, 3, 1)]
+    arrived = [swap(outgoing[k - 1], 0, 0, k, 0) for k in (2,1,3)]
     own_wide = 3 * channels // (dp * tm)
     wide, narrow, feature_grad = local(
         lambda *refs: last_sum_kernel(own_wide, *refs),

time: 74.4 us -> 73.2 us (0.984)
  waiting for transfers between devices: 18.2 us -> 14.1 us
  starting transfers between devices: 32.2 us -> 34.2 us
  Pallas kernels: 22.9 us -> 23.8 us
    ppermute x14, waiting for transfers between devices: 9.79 us -> 5.68 us  [swap(): return lax.ppermute(value, ('dp', 'tm'), flipped(dy, dc, dz, dx))]
    ppermute x14, starting transfers between devices: 23.1 us -> 24.3 us  [swap(): return lax.ppermute(value, ('dp', 'tm'), flipped(dy, dc, dz, dx))]
    ppermute x2, starting transfers between devices: 4.06 us -> 5.06 us  [passed_along(): lax.ppermute(value, axis, [(source, source + steps) for source in range(l...]
    ppermute x2, waiting for transfers between devices: 5.32 us -> 6.26 us  [passed_along(): lax.ppermute(value, axis, [(source, source + steps) for source in range(l...]
    pallas_call x10, Pallas kernels: 22.9 us -> 23.8 us  [local(): pl.pallas_call(kernel, out_shape=out_shape, in_specs=[pl.BlockSpec(memory...]
    all_to_all x1, waiting for transfers between devices: 3.07 us -> 2.19 us  [shards(): lax.all_to_all(proj_t.reshape(tm, pairs * depth, frames), 'tm', split_axi...]
  transfers between devices with their start and end apart: 17 -> 17, of which waited for: 8 -> 7; matrix products, arithmetic and copies ran while one was open for 0% -> 0% of each run, Pallas kernels for 28% -> 29%
where the time goes in v4:
time: 73.2 us; the launch traced here: 72.9 us
  starting transfers between devices  34.2 us (47%)
  Pallas kernels  23.8 us (33%)
  waiting for transfers between devices  14.1 us (19%)
  between operations  0.79 us (1%)
    ppermute x14, starting transfers between devices, swap(): return lax.ppermute(value, ('dp', 'tm'), flipped(dy, dc, dz, dx))  24.3 us
    pallas_call x10, Pallas kernels, local(): pl.pallas_call(kernel, out_shape=out_shape, in_specs=[pl.BlockSpec(memory...  23.8 us
    ppermute x2, waiting for transfers between devices, passed_along(): lax.ppermute(value, axis, [(source, source + steps) for source in range(l...  6.26 us
    ppermute x14, waiting for transfers between devices, swap(): return lax.ppermute(value, ('dp', 'tm'), flipped(dy, dc, dz, dx))  5.68 us
    ppermute x2, starting transfers between devices, passed_along(): lax.ppermute(value, axis, [(source, source + steps) for source in range(l...  5.06 us
    all_to_all x1, starting transfers between devices, shards(): lax.all_to_all(proj_t.reshape(tm, pairs * depth, frames), 'tm', split_axi...  4.88 us
    all_to_all x1, waiting for transfers between devices, shards(): lax.all_to_all(proj_t.reshape(tm, pairs * depth, frames), 'tm', split_axi...  2.19 us
  transfers between devices with their start and end apart: 17, of which 7 were waited for; matrix products, arithmetic and copies ran while one was open for 0% of the time, Pallas kernels for 29%

profile of v4, /device:TPU:0, one launch (start us, length us, event | category | flops | bytes accessed | tf_op | source)
XLA Modules:
  0.0 72.9 jit_solution(7570804922732387172)
XLA Ops:
  0.6 1.0 %cut.1 = (bf16[2,120,256]{2,1,0:T(8,128)(2,1)S(1)}, bf16[2,120,256]{2,1,0:T(8,128)(2,1)S(1)}, bf16[8,512]{1,0:T(8,128)(2,1)S(1)}) custom-call(bf16[2,120,2048]{2,1,0:T(8,128)(2,1)} %bitcast.24, bf16[1024,512]{1,0:T(8,128)(2,1)} %bitcast.22), custom_call_target="tpu_custom_call" | custom-call | flops 1000 | tf_op jit(solution)/shard_map/cut/pallas_call | solution.py:200
  1.6 3.0 %collective-permute-start.1 = (bf16[240,256]{1,0:T(8,128)(2,1)S(1)}, bf16[240,256]{1,0:T(8,128)(2,1)S(1)}, u32[]{:S(2)}, u32[]{:S(2)}) collective-permute-start(bf16[240,256]{1,0:T(8,128)(2,1)S(1)} %bitcast.21), channel_id=1, source_target_pairs={{0,1},{1,0},{2,3},{3,2},{4,5},{5,4},{6,7},{7,6},{8,9},{9,8},{10,11... | collective-permute-start | bytes 368648 | tf_op jit(solution)/shard_map/ppermute | solution.py:494
  4.6 3.6 %collective-permute-start.2 = (bf16[240,256]{1,0:T(8,128)(2,1)S(1)}, bf16[240,256]{1,0:T(8,128)(2,1)S(1)}, u32[]{:S(2)}, u32[]{:S(2)}) collective-permute-start(bf16[240,256]{1,0:T(8,128)(2,1)S(1)} %bitcast.20), channel_id=1, source_target_pairs={{0,7},{1,6},{2,5},{3,4},{4,3},{5,2},{6,1},{7,0},{8,15},{9,14},{10,... | collective-permute-start | bytes 368648 | tf_op jit(solution)/shard_map/ppermute | solution.py:494
  8.2 1.3 %collective-permute-start = (bf16[8,512]{1,0:T(8,128)(2,1)S(1)}, bf16[8,512]{1,0:T(8,128)(2,1)S(1)}, u32[]{:S(2)}, u32[]{:S(2)}) collective-permute-start(bf16[8,512]{1,0:T(8,128)(2,1)S(1)} %get-tuple-element.51), channel_id=1, source_target_pairs={{1,0},{2,1},{3,2},{4,3},{5,4},{6,5},{7,6},{9,8},{10,9},{11,10},{12... | collective-permute-start | bytes 24584 | tf_op jit(solution)/shard_map/ppermute | solution.py:22
  9.5 2.0 %rest_cut.1 = (bf16[2,120,256]{2,1,0:T(8,128)(2,1)}, bf16[2,120,256]{2,1,0:T(8,128)(2,1)}, bf16[2,120,256]{2,1,0:T(8,128)(2,1)}, bf16[2,120,256]{2,1,0:T(8,128)(...) custom-call(bf16[2,120,2048]{2,1,0:T(8,128)(2,1)} %bitcast.25), custom_call_target="tpu_custom_call" | custom-call | flops 1000 | tf_op jit(solution)/shard_map/rest_cut/pallas_call | solution.py:200
  11.5 2.5 %collective-permute-start.3 = (bf16[240,256]{1,0:T(8,128)(2,1)}, bf16[240,256]{1,0:T(8,128)(2,1)S(1)}, u32[]{:S(2)}, u32[]{:S(2)}) collective-permute-start(bf16[240,256]{1,0:T(8,128)(2,1)} %bitcast.36), channel_id=1, source_target_pairs={{0,6},{1,7},{2,4},{3,5},{4,2},{5,3},{6,0},{7,1},{8,14},{9,15},{10,... | collective-permute-start | bytes 368648 | tf_op jit(solution)/shard_map/ppermute | solution.py:494
  14.0 2.6 %collective-permute-start.4 = (bf16[240,256]{1,0:T(8,128)(2,1)}, bf16[240,256]{1,0:T(8,128)(2,1)S(1)}, u32[]{:S(2)}, u32[]{:S(2)}) collective-permute-start(bf16[240,256]{1,0:T(8,128)(2,1)} %bitcast.35), channel_id=1, source_target_pairs={{0,4},{1,5},{2,6},{3,7},{4,0},{5,1},{6,2},{7,3},{8,12},{9,13},{10,... | collective-permute-start | bytes 368648 | tf_op jit(solution)/shard_map/ppermute | solution.py:494
  16.6 0.0 collective-permute-done.refs_1_
  16.6 0.0 copy-start.2
  16.6 0.0 collective-permute-start.5
  16.6 0.0 collective-permute-done.1.refs_8_
  16.6 2.4 %collective-permute-start.6 = (bf16[240,256]{1,0:T(8,128)(2,1)}, bf16[240,256]{1,0:T(8,128)(2,1)S(1)}, u32[]{:S(2)}, u32[]{:S(2)}) collective-permute-start(bf16[240,256]{1,0:T(8,128)(2,1)} %bitcast.33), channel_id=1, source_target_pairs={{0,3},{1,2},{2,1},{3,0},{4,7},{5,6},{6,5},{7,4},{8,11},{9,10},{10,... | collective-permute-start | bytes 368648 | tf_op jit(solution)/shard_map/ppermute | solution.py:494
  19.0 0.0 collective-permute-done.2.refs_2_
  19.0 0.8 %collective-permute-start.7 = (bf16[240,256]{1,0:T(8,128)(2,1)}, bf16[240,256]{1,0:T(8,128)(2,1)S(1)}, u32[]{:S(2)}, u32[]{:S(2)}) collective-permute-start(bf16[240,256]{1,0:T(8,128)(2,1)} %bitcast.32), channel_id=1, source_target_pairs={{0,2},{1,3},{2,0},{3,1},{4,6},{5,7},{6,4},{7,5},{8,10},{9,11},{10,... | collective-permute-start | bytes 368648 | tf_op jit(solution)/shard_map/ppermute | solution.py:494
  19.9 0.0 copy-done.2
  19.9 6.5 %forward.1 = (bf16[1920,256]{1,0:T(8,128)(2,1)}, bf16[1536,512]{1,0:T(8,128)(2,1)}, bf16[1024,256]{1,0:T(8,128)(2,1)}, f32[512,512]{1,0:T(8,128)}, f32[512,512]{...) custom-call(bf16[1024,512]{1,0:T(8,128)(2,1)} %bitcast.23, ...), custom_call_target="tpu_custom_call" | custom-call | flops 1000 | tf_op jit(solution)/shard_map/forward/pallas_call | solution.py:200
  26.4 0.0 copy-start.1
  26.4 4.9 %all-to-all-start = ((bf16[8,240,256]{2,1,0:T(8,128)(2,1)}), bf16[8,240,256]{2,1,0:T(8,128)(2,1)S(1)}, u32[]{:S(2)}, u32[]{:S(2)}) async-start(bf16[8,240,256]{2,1,0:T(8,128)(2,1)} %bitcast.27), calls=%async_computation | async-start | bytes 1966080 | tf_op jit(solution)/shard_map/all_to_all | solution.py:601
  31.3 0.0 collective-permute-done.3.refs_3_
  31.3 0.0 collective-permute-done.4.refs_4_
  31.3 0.0 collective-permute-done.5.refs_5_
  31.3 0.0 collective-permute-done.6.refs_6_
  31.3 0.0 collective-permute-done.7.refs_7_
  31.3 0.0 copy-done.1
  31.3 7.1 %backward.1 = (bf16[2,8,80,512]{3,2,1,0:T(8,128)(2,1)S(1)}, bf16[512,512]{1,0:T(8,128)(2,1)S(1)}, bf16[256,512]{1,0:T(8,128)(2,1)S(1)}) custom-call(bf16[512,1920]{1,0:T(8,128)(2,1)} %refs_0_.1, bf16[240,256]{1,0:T(8,128)(2,1)S(1)} %bitcast.19, bf16[240,256]{1,0:T(8,128)(2,1)S(1)} %collective-permute-done.2.refs_2_, ...), custom_call_target="tpu_custom_call" | custom-call | flops 1000 | tf_op jit(solution)/shard_map/backward/pallas_call | solution.py:200
  38.4 0.1 collective-permute-start.8
  38.5 2.3 %own_grad.1 = (bf16[2,8,80,512]{3,2,1,0:T(8,128)(2,1)S(1)}, f32[8,512]{1,0:T(8,128)S(1)}) custom-call(bf16[1536,512]{1,0:T(8,128)(2,1)} %get-tuple-element.55.refs_19_.refs_0_, bf16[1024,256]{1,0:T(8,128)(2,1)} %get-tuple-element.56.refs_20_.refs_1_, bf16[1536,512]{1,0:T(8,128)(2,1)} %conv_wide.1, bf16[512,512]{1,0:T(8,128)(2,1)S(1)} %get-tuple-element.79.refs_3_.grad_conv, ...), custom_call_target="tpu_custom_call" | custom-call | flops 1000 | tf_op jit(solution)/shard_map/own_grad/pallas_call | solution.py:200
  40.8 0.0 copy-start
  40.9 0.7 collective-permute-done.8.received
  41.5 0.3 first_sum.1
  41.8 3.0 %collective-permute-start.10 = (bf16[4,80,512]{2,1,0:T(8,128)(2,1)S(1)}, bf16[4,80,512]{2,1,0:T(8,128)(2,1)S(1)}, u32[]{:S(2)}, u32[]{:S(2)}) collective-permute-start(bf16[4,80,512]{2,1,0:T(8,128)(2,1)S(1)} %get-tuple-element.85), channel_id=1, source_target_pairs={{0,17},{1,16},{2,19},{3,18},{4,21},{5,20},{6,23},{7,22},{8,25},{9,... | collective-permute-start | bytes 983048 | tf_op jit(solution)/shard_map/ppermute | solution.py:494
  44.9 0.5 collective-permute-start.11
  45.4 0.1 collective-permute-start.12
  45.5 3.8 %collective-permute-start.9 = (f32[8,512]{1,0:T(8,128)S(1)}, f32[8,512]{1,0:T(8,128)S(1)}, u32[]{:S(2)}, u32[]{:S(2)}) collective-permute-start(f32[8,512]{1,0:T(8,128)S(1)} %get-tuple-element.81), channel_id=1, source_target_pairs={{0,1},{1,2},{2,3},{3,4},{4,5},{5,6},{6,7},{8,9},{9,10},{10,11},{11... | collective-permute-start | bytes 49160 | tf_op jit(solution)/shard_map/ppermute | solution.py:22
  49.3 0.0 copy-done
  49.3 2.2 %input_grad.1 = (bf16[1024,512]{1,0:T(8,128)(2,1)}, f32[8,512]{1,0:T(8,128)S(1)}) custom-call(bf16[512,512]{1,0:T(8,128)(2,1)S(1)} %get-tuple-element.79.refs_3_.grad_conv, bf16[1536,512]{1,0:T(8,128)(2,1)S(1)} %copy-done), custom_call_target="tpu_custom_call" | custom-call | flops 1000 | tf_op jit(solution)/shard_map/input_grad/pallas_call | solution.py:200
  51.5 2.2 %all-to-all-done = bf16[8,240,256]{2,1,0:T(8,128)(2,1)S(1)} async-done(((bf16[8,240,256]{2,1,0:T(8,128)(2,1)}), bf16[8,240,256]{2,1,0:T(8,128)(2,1)S(1)}, u32[]{:S(2)}, u32[]{:S(2)}) %all-to-all-start) | async-done | bytes 983072 | tf_op jit(solution)/shard_map/all_to_all | solution.py:601
  53.7 1.0 %join.1 = bf16[2,120,2048]{2,1,0:T(8,128)(2,1)} custom-call(bf16[8,2,120,256]{3,2,1,0:T(8,128)(2,1)S(1)} %bitcast.18), custom_call_target="tpu_custom_call" | custom-call | flops 1000 | tf_op jit(solution)/shard_map/join/pallas_call | solution.py:200
  54.7 6.3 %collective-permute-done.9.refs_4_ = f32[8,512]{1,0:T(8,128)S(1)} collective-permute-done((f32[8,512]{1,0:T(8,128)S(1)}, f32[8,512]{1,0:T(8,128)S(1)}, u32[]{:S(2)}, u32[]{:S(2)}) %collective-permute-start.9) | collective-permute-done | bytes 16416 | tf_op jit(solution)/shard_map/ppermute | solution.py:22
  60.9 0.0 collective-permute-done.10.b
  60.9 0.0 collective-permute-done.11.c
  60.9 0.1 collective-permute-done.12.d
  61.0 0.2 second_sum.1
  61.2 4.1 %collective-permute-start.13 = (bf16[80,512]{1,0:T(8,128)(2,1)S(1)}, bf16[80,512]{1,0:T(8,128)(2,1)S(1)}, u32[]{:S(2)}, u32[]{:S(2)}) collective-permute-start(bf16[80,512]{1,0:T(8,128)(2,1)S(1)} %get-tuple-element.89), channel_id=1, source_target_pairs={{0,4},{1,5},{2,6},{3,7},{4,0},{5,1},{6,2},{7,3},{8,12},{9,13},{10,... | collective-permute-start | bytes 245768 | tf_op jit(solution)/shard_map/ppermute | solution.py:494
  65.2 0.2 collective-permute-start.14
  65.4 1.4 %collective-permute-start.15 = (bf16[80,512]{1,0:T(8,128)(2,1)S(1)}, bf16[80,512]{1,0:T(8,128)(2,1)S(1)}, u32[]{:S(2)}, u32[]{:S(2)}) collective-permute-start(bf16[80,512]{1,0:T(8,128)(2,1)S(1)} %get-tuple-element.91), channel_id=1, source_target_pairs={{0,6},{1,7},{2,4},{3,5},{4,2},{5,3},{6,0},{7,1},{8,14},{9,15},{10,... | collective-permute-start | bytes 245768 | tf_op jit(solution)/shard_map/ppermute | solution.py:494
  66.8 2.7 %collective-permute-done.13.refs_1_ = bf16[80,512]{1,0:T(8,128)(2,1)S(1)} collective-permute-done((bf16[80,512]{1,0:T(8,128)(2,1)S(1)}, bf16[80,512]{1,0:T(8,128)(2,1)S(1)}, u32[]{:S(2)}, u32[]{:S(2)}) %collective-permute-start.13) | collective-permute-done | bytes 81952 | tf_op jit(solution)/shard_map/ppermute | solution.py:494
  69.4 1.3 %collective-permute-done.14.refs_2_ = bf16[80,512]{1,0:T(8,128)(2,1)S(1)} collective-permute-done((bf16[80,512]{1,0:T(8,128)(2,1)S(1)}, bf16[80,512]{1,0:T(8,128)(2,1)S(1)}, u32[]{:S(2)}, u32[]{:S(2)}) %collective-permute-start.14) | collective-permute-done | bytes 81952 | tf_op jit(solution)/shard_map/ppermute | solution.py:494
  70.7 1.0 %collective-permute-done.15.refs_3_ = bf16[80,512]{1,0:T(8,128)(2,1)S(1)} collective-permute-done((bf16[80,512]{1,0:T(8,128)(2,1)S(1)}, bf16[80,512]{1,0:T(8,128)(2,1)S(1)}, u32[]{:S(2)}, u32[]{:S(2)}) %collective-permute-start.15) | collective-permute-done | bytes 81952 | tf_op jit(solution)/shard_map/ppermute | solution.py:494
  71.7 1.3 %last_sum.1 = (f32[192,128]{1,0:T(8,128)}, f32[128,128]{1,0:T(8,128)}, bf16[1024,512]{1,0:T(8,128)(2,1)}) custom-call(bf16[80,512]{1,0:T(8,128)(2,1)S(1)} %get-tuple-element.88.refs_0_, bf16[80,512]{1,0:T(8,128)(2,1)S(1)} %collective-permute-done.13.refs_1_, bf16[80,512]{1,0:T(8,128)(2,1)S(1)} %collective-permute-done.14.refs_2_, ...), custom_call_target="tpu_custom_call", output_to_operand_aliasing={{2}: (6, {})} | custom-call | flops 1000 | tf_op jit(solution)/shard_map/last_sum/pallas_call | solution.py:200
Async XLA Ops:
  1.6 15.0 %collective-permute-start.1 = (bf16[240,256]{1,0:T(8,128)(2,1)S(1)}, bf16[240,256]{1,0:T(8,128)(2,1)S(1)}, u32[]{:S(2)}, u32[]{:S(2)}) collective-permute-start(bf16[240,256]{1,0:T(8,128)(2,1)S(1)} %bitcast.21), channel_id=1, source_target_pairs={{0,1},{1,0},{2,3},{3,2},{4,5},{5,4},{6,7},{7,6},{8,9},{9,8},{10,11... | collective-permute-start | bytes 368648 | tf_op jit(solution)/shard_map/ppermute | solution.py:494
  4.6 14.4 %collective-permute-start.2 = (bf16[240,256]{1,0:T(8,128)(2,1)S(1)}, bf16[240,256]{1,0:T(8,128)(2,1)S(1)}, u32[]{:S(2)}, u32[]{:S(2)}) collective-permute-start(bf16[240,256]{1,0:T(8,128)(2,1)S(1)} %bitcast.20), channel_id=1, source_target_pairs={{0,7},{1,6},{2,5},{3,4},{4,3},{5,2},{6,1},{7,0},{8,15},{9,14},{10,... | collective-permute-start | bytes 368648 | tf_op jit(solution)/shard_map/ppermute | solution.py:494
  8.2 8.4 %collective-permute-start = (bf16[8,512]{1,0:T(8,128)(2,1)S(1)}, bf16[8,512]{1,0:T(8,128)(2,1)S(1)}, u32[]{:S(2)}, u32[]{:S(2)}) collective-permute-start(bf16[8,512]{1,0:T(8,128)(2,1)S(1)} %get-tuple-element.51), channel_id=1, source_target_pairs={{1,0},{2,1},{3,2},{4,3},{5,4},{6,5},{7,6},{9,8},{10,9},{11,10},{12... | collective-permute-start | bytes 24584 | tf_op jit(solution)/shard_map/ppermute | solution.py:22
  11.5 19.8 %collective-permute-start.3 = (bf16[240,256]{1,0:T(8,128)(2,1)}, bf16[240,256]{1,0:T(8,128)(2,1)S(1)}, u32[]{:S(2)}, u32[]{:S(2)}) collective-permute-start(bf16[240,256]{1,0:T(8,128)(2,1)} %bitcast.36), channel_id=1, source_target_pairs={{0,6},{1,7},{2,4},{3,5},{4,2},{5,3},{6,0},{7,1},{8,14},{9,15},{10,... | collective-permute-start | bytes 368648 | tf_op jit(solution)/shard_map/ppermute | solution.py:494
  14.0 17.3 %collective-permute-start.4 = (bf16[240,256]{1,0:T(8,128)(2,1)}, bf16[240,256]{1,0:T(8,128)(2,1)S(1)}, u32[]{:S(2)}, u32[]{:S(2)}) collective-permute-start(bf16[240,256]{1,0:T(8,128)(2,1)} %bitcast.35), channel_id=1, source_target_pairs={{0,4},{1,5},{2,6},{3,7},{4,0},{5,1},{6,2},{7,3},{8,12},{9,13},{10,... | collective-permute-start | bytes 368648 | tf_op jit(solution)/shard_map/ppermute | solution.py:494
  16.6 3.3 %copy-start.2 = (bf16[8,512]{1,0:T(8,128)(2,1)}, bf16[8,512]{1,0:T(8,128)(2,1)S(1)}, u32[]{:S(2)}) copy-start(bf16[8,512]{1,0:T(8,128)(2,1)S(1)} %collective-permute-done.refs_1_) | copy-start | bytes 24580
  16.6 14.7 %collective-permute-start.5 = (bf16[240,256]{1,0:T(8,128)(2,1)}, bf16[240,256]{1,0:T(8,128)(2,1)S(1)}, u32[]{:S(2)}, u32[]{:S(2)}) collective-permute-start(bf16[240,256]{1,0:T(8,128)(2,1)} %bitcast.34), channel_id=1, source_target_pairs={{0,5},{1,4},{2,7},{3,6},{4,1},{5,0},{6,3},{7,2},{8,13},{9,12},{10,... | collective-permute-start | bytes 368648 | tf_op jit(solution)/shard_map/ppermute | solution.py:494
  16.6 14.7 %collective-permute-start.6 = (bf16[240,256]{1,0:T(8,128)(2,1)}, bf16[240,256]{1,0:T(8,128)(2,1)S(1)}, u32[]{:S(2)}, u32[]{:S(2)}) collective-permute-start(bf16[240,256]{1,0:T(8,128)(2,1)} %bitcast.33), channel_id=1, source_target_pairs={{0,3},{1,2},{2,1},{3,0},{4,7},{5,6},{6,5},{7,4},{8,11},{9,10},{10,... | collective-permute-start | bytes 368648 | tf_op jit(solution)/shard_map/ppermute | solution.py:494
  19.0 12.3 %collective-permute-start.7 = (bf16[240,256]{1,0:T(8,128)(2,1)}, bf16[240,256]{1,0:T(8,128)(2,1)S(1)}, u32[]{:S(2)}, u32[]{:S(2)}) collective-permute-start(bf16[240,256]{1,0:T(8,128)(2,1)} %bitcast.32), channel_id=1, source_target_pairs={{0,2},{1,3},{2,0},{3,1},{4,6},{5,7},{6,4},{7,5},{8,10},{9,11},{10,... | collective-permute-start | bytes 368648 | tf_op jit(solution)/shard_map/ppermute | solution.py:494
  26.4 4.9 %copy-start.1 = (bf16[2,120,256]{2,1,0:T(8,128)(2,1)S(1)}, bf16[2,120,256]{2,1,0:T(8,128)(2,1)}, u32[]{:S(2)}) copy-start(bf16[2,120,256]{2,1,0:T(8,128)(2,1)} %get-tuple-element.57) | copy-start | bytes 368644
  26.4 27.3 %all-to-all-start = ((bf16[8,240,256]{2,1,0:T(8,128)(2,1)}), bf16[8,240,256]{2,1,0:T(8,128)(2,1)S(1)}, u32[]{:S(2)}, u32[]{:S(2)}) async-start(bf16[8,240,256]{2,1,0:T(8,128)(2,1)} %bitcast.27), calls=%async_computation | async-start | bytes 1966080 | tf_op jit(solution)/shard_map/all_to_all | solution.py:601
  38.4 3.1 %collective-permute-start.8 = (bf16[2,8,80,512]{3,2,1,0:T(8,128)(2,1)S(1)}, bf16[2,8,80,512]{3,2,1,0:T(8,128)(2,1)S(1)}, u32[]{:S(2)}, u32[]{:S(2)}) collective-permute-start(bf16[2,8,80,512]{3,2,1,0:T(8,128)(2,1)S(1)} %get-tuple-element.77), channel_id=1, source_target_pairs={{0,8},{1,9},{2,10},{3,11},{4,12},{5,13},{6,14},{7,15},{8,0},{9,1},... | collective-permute-start | bytes 3932168 | tf_op jit(solution)/shard_map/ppermute | solution.py:494
  40.8 8.5 %copy-start = (bf16[1536,512]{1,0:T(8,128)(2,1)S(1)}, bf16[1536,512]{1,0:T(8,128)(2,1)}, u32[]{:S(2)}) copy-start(bf16[1536,512]{1,0:T(8,128)(2,1)} %conv_wide.1) | copy-start | bytes 4718596
  41.8 19.1 %collective-permute-start.10 = (bf16[4,80,512]{2,1,0:T(8,128)(2,1)S(1)}, bf16[4,80,512]{2,1,0:T(8,128)(2,1)S(1)}, u32[]{:S(2)}, u32[]{:S(2)}) collective-permute-start(bf16[4,80,512]{2,1,0:T(8,128)(2,1)S(1)} %get-tuple-element.85), channel_id=1, source_target_pairs={{0,17},{1,16},{2,19},{3,18},{4,21},{5,20},{6,23},{7,22},{8,25},{9,... | collective-permute-start | bytes 983048 | tf_op jit(solution)/shard_map/ppermute | solution.py:494
  44.9 16.1 %collective-permute-start.11 = (bf16[4,80,512]{2,1,0:T(8,128)(2,1)S(1)}, bf16[4,80,512]{2,1,0:T(8,128)(2,1)S(1)}, u32[]{:S(2)}, u32[]{:S(2)}) collective-permute-start(bf16[4,80,512]{2,1,0:T(8,128)(2,1)S(1)} %get-tuple-element.86), channel_id=1, source_target_pairs={{0,16},{1,17},{2,18},{3,19},{4,20},{5,21},{6,22},{7,23},{8,24},{9,... | collective-permute-start | bytes 983048 | tf_op jit(solution)/shard_map/ppermute | solution.py:494
  45.4 15.6 %collective-permute-start.12 = (bf16[4,80,512]{2,1,0:T(8,128)(2,1)S(1)}, bf16[4,80,512]{2,1,0:T(8,128)(2,1)S(1)}, u32[]{:S(2)}, u32[]{:S(2)}) collective-permute-start(bf16[4,80,512]{2,1,0:T(8,128)(2,1)S(1)} %get-tuple-element.87), channel_id=1, source_target_pairs={{0,1},{1,0},{2,3},{3,2},{4,5},{5,4},{6,7},{7,6},{8,9},{9,8},{10,11... | collective-permute-start | bytes 983048 | tf_op jit(solution)/shard_map/ppermute | solution.py:494
  45.5 15.4 %collective-permute-start.9 = (f32[8,512]{1,0:T(8,128)S(1)}, f32[8,512]{1,0:T(8,128)S(1)}, u32[]{:S(2)}, u32[]{:S(2)}) collective-permute-start(f32[8,512]{1,0:T(8,128)S(1)} %get-tuple-element.81), channel_id=1, source_target_pairs={{0,1},{1,2},{2,3},{3,4},{4,5},{5,6},{6,7},{8,9},{9,10},{10,11},{11... | collective-permute-start | bytes 49160 | tf_op jit(solution)/shard_map/ppermute | solution.py:22
  61.2 8.3 %collective-permute-start.13 = (bf16[80,512]{1,0:T(8,128)(2,1)S(1)}, bf16[80,512]{1,0:T(8,128)(2,1)S(1)}, u32[]{:S(2)}, u32[]{:S(2)}) collective-permute-start(bf16[80,512]{1,0:T(8,128)(2,1)S(1)} %get-tuple-element.89), channel_id=1, source_target_pairs={{0,4},{1,5},{2,6},{3,7},{4,0},{5,1},{6,2},{7,3},{8,12},{9,13},{10,... | collective-permute-start | bytes 245768 | tf_op jit(solution)/shard_map/ppermute | solution.py:494
  65.2 5.5 %collective-permute-start.14 = (bf16[80,512]{1,0:T(8,128)(2,1)S(1)}, bf16[80,512]{1,0:T(8,128)(2,1)S(1)}, u32[]{:S(2)}, u32[]{:S(2)}) collective-permute-start(bf16[80,512]{1,0:T(8,128)(2,1)S(1)} %get-tuple-element.90), channel_id=1, source_target_pairs={{0,2},{1,3},{2,0},{3,1},{4,6},{5,7},{6,4},{7,5},{8,10},{9,11},{10,... | collective-permute-start | bytes 245768 | tf_op jit(solution)/shard_map/ppermute | solution.py:494
  65.4 6.3 %collective-permute-start.15 = (bf16[80,512]{1,0:T(8,128)(2,1)S(1)}, bf16[80,512]{1,0:T(8,128)(2,1)S(1)}, u32[]{:S(2)}, u32[]{:S(2)}) collective-permute-start(bf16[80,512]{1,0:T(8,128)(2,1)S(1)} %get-tuple-element.91), channel_id=1, source_target_pairs={{0,6},{1,7},{2,4},{3,5},{4,2},{5,3},{6,0},{7,1},{8,14},{9,15},{10,... | collective-permute-start | bytes 245768 | tf_op jit(solution)/shard_map/ppermute | solution.py:494

commit v5 on v4

--- a/solution.py
+++ b/solution.py
@@ -159,7 +159,7 @@
 
 
 F32 = jnp.float32
-ORDER = (0, 7, 6, 4, 5, 3, 2, 1)
+ORDER = (0, 7, 6, 4, 3, 5, 2, 1)
 BF16 = jnp.bfloat16
 NT = (((1,), (1,)), ((), ()))
 
@@ -467,11 +467,13 @@
         out[...] = total.astype(BF16)
 
 
-def last_sum_kernel(wide_rows, a, b, c, d, incoming, first_rows, grad_in, wide, narrow, grad_out, rows_buf, sem):
+def first_row_kernel(incoming, first_rows, grad_in, grad_out, rows_buf, sem):
     at_start = lax.broadcasted_iota(jnp.int32, (8, 1), 0) == 0
     rows_buf[...] = (first_rows[...] + jnp.where(at_start, incoming[7:8, :], 0.0)).astype(BF16)
-    put = pltpu.make_async_copy(rows_buf, grad_out.at[pl.ds(0, 8), :], sem)
-    put.start()
+    run_copies([(rows_buf, grad_out.at[pl.ds(0, 8), :])], sem)
+
+
+def last_sum_kernel(wide_rows, a, b, c, d, wide, narrow):
     total = (a[...].astype(F32) + b[...].astype(F32)) + (c[...].astype(F32) + d[...].astype(F32))
     rows, channels = total.shape
     pieces = channels // 128
@@ -479,7 +481,6 @@
         lanes = total[:, p * 128 : (p + 1) * 128]
         wide[pl.ds(p, wide_rows, stride=pieces), :] = lanes[:wide_rows]
         narrow[pl.ds(p, rows - wide_rows, stride=pieces), :] = lanes[wide_rows:]
-    put.wait()
 
 
 def flipped(dy, dc, dz, dx):
@@ -651,7 +652,7 @@
     )
     plane = ((tm // 2, part_rows, channels), BF16, True)
     own, *outgoing = local(first_sum_kernel, [keep, received], [plane] * 4, "first_sum")
-    arrived = [swap(outgoing[k - 1], k // 2, 0, 0, k % 2) for k in (3,2,1)]
+    arrived = [swap(outgoing[k - 1], k // 2, 0, 0, k % 2) for k in (3, 2, 1)]
     tail, grad_conv, own = lax.optimization_barrier((tail, grad_conv, own))
     incoming = passed_along(tail, "tm", 1)
     feature_grad, first_rows = local(
@@ -672,21 +673,28 @@
     )
     attn_t, first_rows, incoming, own = lax.optimization_barrier((attn_t, first_rows, incoming, own))
     own, *outgoing = local(second_sum_kernel, [own, *arrived], [piece] * 4, "second_sum")
-    arrived = [swap(outgoing[k - 1], 0, 0, k, 0) for k in (2,1,3)]
+    arrived = [swap(outgoing[k - 1], 0, 0, k, 0) for k in (2, 1, 3)]
     own_wide = 3 * channels // (dp * tm)
-    wide, narrow, feature_grad = local(
+    first_rows, own = lax.optimization_barrier((first_rows, own))
+    (feature_grad,) = local(
+        first_row_kernel,
+        [incoming, first_rows, feature_grad],
+        [((length, channels), BF16, False)],
+        "first_row",
+        scratch=[pltpu.VMEM((8, channels), BF16), pltpu.SemaphoreType.DMA((1,))],
+        raw=(2,),
+        raw_out=(0,),
+        aliases={2: 0},
+    )
+    feature_grad, own = lax.optimization_barrier((feature_grad, own))
+    wide, narrow = local(
         lambda *refs: last_sum_kernel(own_wide, *refs),
-        [own, *arrived, incoming, first_rows, feature_grad],
+        [own, *arrived],
         [
             ((own_wide * channels // 128, 128), F32, False),
             (((part_rows - own_wide) * channels // 128, 128), F32, False),
-            ((length, channels), BF16, False),
         ],
         "last_sum",
-        scratch=[pltpu.VMEM((8, channels), BF16), pltpu.SemaphoreType.DMA(())],
-        raw=(6,),
-        raw_out=(2,),
-        aliases={6: 2},
     )
     return (
         attn_t.transpose(0, 2, 1),

time: 73.2 us -> 72.7 us (level)
    pallas_call x10 -> x11, Pallas kernels: 23.8 us -> 23.8 us  [local(): pl.pallas_call(kernel, out_shape=out_shape, in_specs=[pl.BlockSpec(memory...]
  transfers between devices with their start and end apart: 17 -> 17, of which waited for: 7 -> 7; matrix products, arithmetic and copies ran while one was open for 0% -> 0% of each run, Pallas kernels for 29% -> 30%
where the time goes in v5:
time: 72.7 us; the launch traced here: 72.4 us
  starting transfers between devices  34.2 us (47%)
  Pallas kernels  23.8 us (33%)
  waiting for transfers between devices  13.5 us (19%)
  between operations  0.8 us (1%)
    ppermute x14, starting transfers between devices, swap(): return lax.ppermute(value, ('dp', 'tm'), flipped(dy, dc, dz, dx))  24.3 us
    pallas_call x11, Pallas kernels, local(): pl.pallas_call(kernel, out_shape=out_shape, in_specs=[pl.BlockSpec(memory...  23.8 us
    ppermute x2, waiting for transfers between devices, passed_along(): lax.ppermute(value, axis, [(source, source + steps) for source in range(l...  6.26 us
    ppermute x2, starting transfers between devices, passed_along(): lax.ppermute(value, axis, [(source, source + steps) for source in range(l...  5.06 us
    ppermute x14, waiting for transfers between devices, swap(): return lax.ppermute(value, ('dp', 'tm'), flipped(dy, dc, dz, dx))  5.06 us
    all_to_all x1, starting transfers between devices, shards(): lax.all_to_all(proj_t.reshape(tm, pairs * depth, frames), 'tm', split_axi...  4.88 us
    all_to_all x1, waiting for transfers between devices, shards(): lax.all_to_all(proj_t.reshape(tm, pairs * depth, frames), 'tm', split_axi...  2.19 us
  transfers between devices with their start and end apart: 17, of which 7 were waited for; matrix products, arithmetic and copies ran while one was open for 0% of the time, Pallas kernels for 30%

profile of v5, /device:TPU:0, one launch (start us, length us, event | category | flops | bytes accessed | tf_op | source)
XLA Modules:
  0.0 72.4 jit_solution(13221441747272340487)
XLA Ops:
  0.6 1.0 %cut.1 = (bf16[2,120,256]{2,1,0:T(8,128)(2,1)S(1)}, bf16[2,120,256]{2,1,0:T(8,128)(2,1)S(1)}, bf16[8,512]{1,0:T(8,128)(2,1)S(1)}) custom-call(bf16[2,120,2048]{2,1,0:T(8,128)(2,1)} %bitcast.24, bf16[1024,512]{1,0:T(8,128)(2,1)} %bitcast.22), custom_call_target="tpu_custom_call" | custom-call | flops 1000 | tf_op jit(solution)/shard_map/cut/pallas_call | solution.py:200
  1.6 3.0 %collective-permute-start.1 = (bf16[240,256]{1,0:T(8,128)(2,1)S(1)}, bf16[240,256]{1,0:T(8,128)(2,1)S(1)}, u32[]{:S(2)}, u32[]{:S(2)}) collective-permute-start(bf16[240,256]{1,0:T(8,128)(2,1)S(1)} %bitcast.21), channel_id=1, source_target_pairs={{0,1},{1,0},{2,3},{3,2},{4,5},{5,4},{6,7},{7,6},{8,9},{9,8},{10,11... | collective-permute-start | bytes 368648 | tf_op jit(solution)/shard_map/ppermute | solution.py:495
  4.6 3.6 %collective-permute-start.2 = (bf16[240,256]{1,0:T(8,128)(2,1)S(1)}, bf16[240,256]{1,0:T(8,128)(2,1)S(1)}, u32[]{:S(2)}, u32[]{:S(2)}) collective-permute-start(bf16[240,256]{1,0:T(8,128)(2,1)S(1)} %bitcast.20), channel_id=1, source_target_pairs={{0,7},{1,6},{2,5},{3,4},{4,3},{5,2},{6,1},{7,0},{8,15},{9,14},{10,... | collective-permute-start | bytes 368648 | tf_op jit(solution)/shard_map/ppermute | solution.py:495
  8.2 1.3 %collective-permute-start = (bf16[8,512]{1,0:T(8,128)(2,1)S(1)}, bf16[8,512]{1,0:T(8,128)(2,1)S(1)}, u32[]{:S(2)}, u32[]{:S(2)}) collective-permute-start(bf16[8,512]{1,0:T(8,128)(2,1)S(1)} %get-tuple-element.54), channel_id=1, source_target_pairs={{1,0},{2,1},{3,2},{4,3},{5,4},{6,5},{7,6},{9,8},{10,9},{11,10},{12... | collective-permute-start | bytes 24584 | tf_op jit(solution)/shard_map/ppermute | solution.py:22
  9.5 2.0 %rest_cut.1 = (bf16[2,120,256]{2,1,0:T(8,128)(2,1)}, bf16[2,120,256]{2,1,0:T(8,128)(2,1)}, bf16[2,120,256]{2,1,0:T(8,128)(2,1)}, bf16[2,120,256]{2,1,0:T(8,128)(...) custom-call(bf16[2,120,2048]{2,1,0:T(8,128)(2,1)} %bitcast.25), custom_call_target="tpu_custom_call" | custom-call | flops 1000 | tf_op jit(solution)/shard_map/rest_cut/pallas_call | solution.py:200
  11.5 2.5 %collective-permute-start.3 = (bf16[240,256]{1,0:T(8,128)(2,1)}, bf16[240,256]{1,0:T(8,128)(2,1)S(1)}, u32[]{:S(2)}, u32[]{:S(2)}) collective-permute-start(bf16[240,256]{1,0:T(8,128)(2,1)} %bitcast.36), channel_id=1, source_target_pairs={{0,6},{1,7},{2,4},{3,5},{4,2},{5,3},{6,0},{7,1},{8,14},{9,15},{10,... | collective-permute-start | bytes 368648 | tf_op jit(solution)/shard_map/ppermute | solution.py:495
  14.0 2.6 %collective-permute-start.4 = (bf16[240,256]{1,0:T(8,128)(2,1)}, bf16[240,256]{1,0:T(8,128)(2,1)S(1)}, u32[]{:S(2)}, u32[]{:S(2)}) collective-permute-start(bf16[240,256]{1,0:T(8,128)(2,1)} %bitcast.35), channel_id=1, source_target_pairs={{0,4},{1,5},{2,6},{3,7},{4,0},{5,1},{6,2},{7,3},{8,12},{9,13},{10,... | collective-permute-start | bytes 368648 | tf_op jit(solution)/shard_map/ppermute | solution.py:495
  16.6 0.0 collective-permute-done.refs_1_
  16.6 0.0 copy-start.2
  16.6 1.4 %collective-permute-start.5 = (bf16[240,256]{1,0:T(8,128)(2,1)}, bf16[240,256]{1,0:T(8,128)(2,1)S(1)}, u32[]{:S(2)}, u32[]{:S(2)}) collective-permute-start(bf16[240,256]{1,0:T(8,128)(2,1)} %bitcast.34), channel_id=1, source_target_pairs={{0,3},{1,2},{2,1},{3,0},{4,7},{5,6},{6,5},{7,4},{8,11},{9,10},{10,... | collective-permute-start | bytes 368648 | tf_op jit(solution)/shard_map/ppermute | solution.py:495
  18.0 0.0 collective-permute-done.1.refs_8_
  18.0 1.0 %collective-permute-start.6 = (bf16[240,256]{1,0:T(8,128)(2,1)}, bf16[240,256]{1,0:T(8,128)(2,1)S(1)}, u32[]{:S(2)}, u32[]{:S(2)}) collective-permute-start(bf16[240,256]{1,0:T(8,128)(2,1)} %bitcast.33), channel_id=1, source_target_pairs={{0,5},{1,4},{2,7},{3,6},{4,1},{5,0},{6,3},{7,2},{8,13},{9,12},{10,... | collective-permute-start | bytes 368648 | tf_op jit(solution)/shard_map/ppermute | solution.py:495
  19.0 0.0 collective-permute-done.2.refs_2_
  19.0 0.8 %collective-permute-start.7 = (bf16[240,256]{1,0:T(8,128)(2,1)}, bf16[240,256]{1,0:T(8,128)(2,1)S(1)}, u32[]{:S(2)}, u32[]{:S(2)}) collective-permute-start(bf16[240,256]{1,0:T(8,128)(2,1)} %bitcast.32), channel_id=1, source_target_pairs={{0,2},{1,3},{2,0},{3,1},{4,6},{5,7},{6,4},{7,5},{8,10},{9,11},{10,... | collective-permute-start | bytes 368648 | tf_op jit(solution)/shard_map/ppermute | solution.py:495
  19.9 0.0 copy-done.2
  19.9 6.5 %forward.1 = (bf16[1920,256]{1,0:T(8,128)(2,1)}, bf16[1536,512]{1,0:T(8,128)(2,1)}, bf16[1024,256]{1,0:T(8,128)(2,1)}, f32[512,512]{1,0:T(8,128)}, f32[512,512]{...) custom-call(bf16[1024,512]{1,0:T(8,128)(2,1)} %bitcast.23, ...), custom_call_target="tpu_custom_call" | custom-call | flops 1000 | tf_op jit(solution)/shard_map/forward/pallas_call | solution.py:200
  26.4 0.0 copy-start.1
  26.4 4.9 %all-to-all-start = ((bf16[8,240,256]{2,1,0:T(8,128)(2,1)}), bf16[8,240,256]{2,1,0:T(8,128)(2,1)S(1)}, u32[]{:S(2)}, u32[]{:S(2)}) async-start(bf16[8,240,256]{2,1,0:T(8,128)(2,1)} %bitcast.27), calls=%async_computation | async-start | bytes 1966080 | tf_op jit(solution)/shard_map/all_to_all | solution.py:602
  31.3 0.0 collective-permute-done.3.refs_3_
  31.3 0.0 collective-permute-done.4.refs_4_
  31.3 0.0 collective-permute-done.5.refs_5_
  31.3 0.0 collective-permute-done.6.refs_6_
  31.3 0.0 collective-permute-done.7.refs_7_
  31.3 0.0 copy-done.1
  31.3 7.1 %backward.1 = (bf16[2,8,80,512]{3,2,1,0:T(8,128)(2,1)S(1)}, bf16[512,512]{1,0:T(8,128)(2,1)S(1)}, bf16[256,512]{1,0:T(8,128)(2,1)S(1)}) custom-call(bf16[512,1920]{1,0:T(8,128)(2,1)} %refs_0_.1, bf16[240,256]{1,0:T(8,128)(2,1)S(1)} %bitcast.19, bf16[240,256]{1,0:T(8,128)(2,1)S(1)} %collective-permute-done.2.refs_2_, ...), custom_call_target="tpu_custom_call" | custom-call | flops 1000 | tf_op jit(solution)/shard_map/backward/pallas_call | solution.py:200
  38.4 0.1 collective-permute-start.8
  38.5 2.3 %own_grad.1 = (bf16[2,8,80,512]{3,2,1,0:T(8,128)(2,1)S(1)}, f32[8,512]{1,0:T(8,128)S(1)}) custom-call(bf16[1536,512]{1,0:T(8,128)(2,1)} %get-tuple-element.58.refs_19_.refs_0_, bf16[1024,256]{1,0:T(8,128)(2,1)} %get-tuple-element.59.refs_20_.refs_1_, bf16[1536,512]{1,0:T(8,128)(2,1)} %conv_wide.1, bf16[512,512]{1,0:T(8,128)(2,1)S(1)} %get-tuple-element.82.refs_3_.grad_conv, ...), custom_call_target="tpu_custom_call" | custom-call | flops 1000 | tf_op jit(solution)/shard_map/own_grad/pallas_call | solution.py:200
  40.8 0.0 copy-start
  40.9 0.7 collective-permute-done.8.received
  41.5 0.3 first_sum.1
  41.8 3.0 %collective-permute-start.10 = (bf16[4,80,512]{2,1,0:T(8,128)(2,1)S(1)}, bf16[4,80,512]{2,1,0:T(8,128)(2,1)S(1)}, u32[]{:S(2)}, u32[]{:S(2)}) collective-permute-start(bf16[4,80,512]{2,1,0:T(8,128)(2,1)S(1)} %get-tuple-element.90), channel_id=1, source_target_pairs={{0,17},{1,16},{2,19},{3,18},{4,21},{5,20},{6,23},{7,22},{8,25},{9,... | collective-permute-start | bytes 983048 | tf_op jit(solution)/shard_map/ppermute | solution.py:495
  44.9 0.5 collective-permute-start.11
  45.4 0.1 collective-permute-start.12
  45.5 3.8 %collective-permute-start.9 = (f32[8,512]{1,0:T(8,128)S(1)}, f32[8,512]{1,0:T(8,128)S(1)}, u32[]{:S(2)}, u32[]{:S(2)}) collective-permute-start(f32[8,512]{1,0:T(8,128)S(1)} %get-tuple-element.84), channel_id=1, source_target_pairs={{0,1},{1,2},{2,3},{3,4},{4,5},{5,6},{6,7},{8,9},{9,10},{10,11},{11... | collective-permute-start | bytes 49160 | tf_op jit(solution)/shard_map/ppermute | solution.py:22
  49.3 0.0 copy-done
  49.3 2.2 %input_grad.1 = (bf16[1024,512]{1,0:T(8,128)(2,1)}, f32[8,512]{1,0:T(8,128)S(1)}) custom-call(bf16[512,512]{1,0:T(8,128)(2,1)S(1)} %get-tuple-element.82.refs_3_.grad_conv, bf16[1536,512]{1,0:T(8,128)(2,1)S(1)} %copy-done), custom_call_target="tpu_custom_call" | custom-call | flops 1000 | tf_op jit(solution)/shard_map/input_grad/pallas_call | solution.py:200
  51.5 2.2 %all-to-all-done = bf16[8,240,256]{2,1,0:T(8,128)(2,1)S(1)} async-done(((bf16[8,240,256]{2,1,0:T(8,128)(2,1)}), bf16[8,240,256]{2,1,0:T(8,128)(2,1)S(1)}, u32[]{:S(2)}, u32[]{:S(2)}) %all-to-all-start) | async-done | bytes 983072 | tf_op jit(solution)/shard_map/all_to_all | solution.py:602
  53.7 1.0 %join.1 = bf16[2,120,2048]{2,1,0:T(8,128)(2,1)} custom-call(bf16[8,2,120,256]{3,2,1,0:T(8,128)(2,1)S(1)} %bitcast.18), custom_call_target="tpu_custom_call" | custom-call | flops 1000 | tf_op jit(solution)/shard_map/join/pallas_call | solution.py:200
  54.7 6.3 %collective-permute-done.9.incoming = f32[8,512]{1,0:T(8,128)S(1)} collective-permute-done((f32[8,512]{1,0:T(8,128)S(1)}, f32[8,512]{1,0:T(8,128)S(1)}, u32[]{:S(2)}, u32[]{:S(2)}) %collective-permute-start.9) | collective-permute-done | bytes 16416 | tf_op jit(solution)/shard_map/ppermute | solution.py:22
  60.9 0.0 collective-permute-done.10.b
  60.9 0.0 collective-permute-done.11.c
  60.9 0.1 collective-permute-done.12.d
  61.0 0.2 second_sum.1
  61.2 4.1 %collective-permute-start.13 = (bf16[80,512]{1,0:T(8,128)(2,1)S(1)}, bf16[80,512]{1,0:T(8,128)(2,1)S(1)}, u32[]{:S(2)}, u32[]{:S(2)}) collective-permute-start(bf16[80,512]{1,0:T(8,128)(2,1)S(1)} %get-tuple-element.99), channel_id=1, source_target_pairs={{0,4},{1,5},{2,6},{3,7},{4,0},{5,1},{6,2},{7,3},{8,12},{9,13},{10,... | collective-permute-start | bytes 245768 | tf_op jit(solution)/shard_map/ppermute | solution.py:495
  65.2 0.2 collective-permute-start.14
  65.4 1.4 %collective-permute-start.15 = (bf16[80,512]{1,0:T(8,128)(2,1)S(1)}, bf16[80,512]{1,0:T(8,128)(2,1)S(1)}, u32[]{:S(2)}, u32[]{:S(2)}) collective-permute-start(bf16[80,512]{1,0:T(8,128)(2,1)S(1)} %get-tuple-element.101), channel_id=1, source_target_pairs={{0,6},{1,7},{2,4},{3,5},{4,2},{5,3},{6,0},{7,1},{8,14},{9,15},{10,... | collective-permute-start | bytes 245768 | tf_op jit(solution)/shard_map/ppermute | solution.py:495
  66.8 0.6 first_row.1
  67.4 2.1 %collective-permute-done.13.refs_1_ = bf16[80,512]{1,0:T(8,128)(2,1)S(1)} collective-permute-done((bf16[80,512]{1,0:T(8,128)(2,1)S(1)}, bf16[80,512]{1,0:T(8,128)(2,1)S(1)}, u32[]{:S(2)}, u32[]{:S(2)}) %collective-permute-start.13) | collective-permute-done | bytes 81952 | tf_op jit(solution)/shard_map/ppermute | solution.py:495
  69.4 1.3 %collective-permute-done.14.refs_2_ = bf16[80,512]{1,0:T(8,128)(2,1)S(1)} collective-permute-done((bf16[80,512]{1,0:T(8,128)(2,1)S(1)}, bf16[80,512]{1,0:T(8,128)(2,1)S(1)}, u32[]{:S(2)}, u32[]{:S(2)}) %collective-permute-start.14) | collective-permute-done | bytes 81952 | tf_op jit(solution)/shard_map/ppermute | solution.py:495
  70.7 1.0 %collective-permute-done.15.refs_3_ = bf16[80,512]{1,0:T(8,128)(2,1)S(1)} collective-permute-done((bf16[80,512]{1,0:T(8,128)(2,1)S(1)}, bf16[80,512]{1,0:T(8,128)(2,1)S(1)}, u32[]{:S(2)}, u32[]{:S(2)}) %collective-permute-start.15) | collective-permute-done | bytes 81952 | tf_op jit(solution)/shard_map/ppermute | solution.py:495
  71.7 0.7 last_sum.1
Async XLA Ops:
  1.6 16.4 %collective-permute-start.1 = (bf16[240,256]{1,0:T(8,128)(2,1)S(1)}, bf16[240,256]{1,0:T(8,128)(2,1)S(1)}, u32[]{:S(2)}, u32[]{:S(2)}) collective-permute-start(bf16[240,256]{1,0:T(8,128)(2,1)S(1)} %bitcast.21), channel_id=1, source_target_pairs={{0,1},{1,0},{2,3},{3,2},{4,5},{5,4},{6,7},{7,6},{8,9},{9,8},{10,11... | collective-permute-start | bytes 368648 | tf_op jit(solution)/shard_map/ppermute | solution.py:495
  4.6 14.4 %collective-permute-start.2 = (bf16[240,256]{1,0:T(8,128)(2,1)S(1)}, bf16[240,256]{1,0:T(8,128)(2,1)S(1)}, u32[]{:S(2)}, u32[]{:S(2)}) collective-permute-start(bf16[240,256]{1,0:T(8,128)(2,1)S(1)} %bitcast.20), channel_id=1, source_target_pairs={{0,7},{1,6},{2,5},{3,4},{4,3},{5,2},{6,1},{7,0},{8,15},{9,14},{10,... | collective-permute-start | bytes 368648 | tf_op jit(solution)/shard_map/ppermute | solution.py:495
  8.2 8.4 %collective-permute-start = (bf16[8,512]{1,0:T(8,128)(2,1)S(1)}, bf16[8,512]{1,0:T(8,128)(2,1)S(1)}, u32[]{:S(2)}, u32[]{:S(2)}) collective-permute-start(bf16[8,512]{1,0:T(8,128)(2,1)S(1)} %get-tuple-element.54), channel_id=1, source_target_pairs={{1,0},{2,1},{3,2},{4,3},{5,4},{6,5},{7,6},{9,8},{10,9},{11,10},{12... | collective-permute-start | bytes 24584 | tf_op jit(solution)/shard_map/ppermute | solution.py:22
  11.5 19.8 %collective-permute-start.3 = (bf16[240,256]{1,0:T(8,128)(2,1)}, bf16[240,256]{1,0:T(8,128)(2,1)S(1)}, u32[]{:S(2)}, u32[]{:S(2)}) collective-permute-start(bf16[240,256]{1,0:T(8,128)(2,1)} %bitcast.36), channel_id=1, source_target_pairs={{0,6},{1,7},{2,4},{3,5},{4,2},{5,3},{6,0},{7,1},{8,14},{9,15},{10,... | collective-permute-start | bytes 368648 | tf_op jit(solution)/shard_map/ppermute | solution.py:495
  14.0 17.3 %collective-permute-start.4 = (bf16[240,256]{1,0:T(8,128)(2,1)}, bf16[240,256]{1,0:T(8,128)(2,1)S(1)}, u32[]{:S(2)}, u32[]{:S(2)}) collective-permute-start(bf16[240,256]{1,0:T(8,128)(2,1)} %bitcast.35), channel_id=1, source_target_pairs={{0,4},{1,5},{2,6},{3,7},{4,0},{5,1},{6,2},{7,3},{8,12},{9,13},{10,... | collective-permute-start | bytes 368648 | tf_op jit(solution)/shard_map/ppermute | solution.py:495
  16.6 3.3 %copy-start.2 = (bf16[8,512]{1,0:T(8,128)(2,1)}, bf16[8,512]{1,0:T(8,128)(2,1)S(1)}, u32[]{:S(2)}) copy-start(bf16[8,512]{1,0:T(8,128)(2,1)S(1)} %collective-permute-done.refs_1_) | copy-start | bytes 24580
  16.6 14.7 %collective-permute-start.5 = (bf16[240,256]{1,0:T(8,128)(2,1)}, bf16[240,256]{1,0:T(8,128)(2,1)S(1)}, u32[]{:S(2)}, u32[]{:S(2)}) collective-permute-start(bf16[240,256]{1,0:T(8,128)(2,1)} %bitcast.34), channel_id=1, source_target_pairs={{0,3},{1,2},{2,1},{3,0},{4,7},{5,6},{6,5},{7,4},{8,11},{9,10},{10,... | collective-permute-start | bytes 368648 | tf_op jit(solution)/shard_map/ppermute | solution.py:495
  18.0 13.3 %collective-permute-start.6 = (bf16[240,256]{1,0:T(8,128)(2,1)}, bf16[240,256]{1,0:T(8,128)(2,1)S(1)}, u32[]{:S(2)}, u32[]{:S(2)}) collective-permute-start(bf16[240,256]{1,0:T(8,128)(2,1)} %bitcast.33), channel_id=1, source_target_pairs={{0,5},{1,4},{2,7},{3,6},{4,1},{5,0},{6,3},{7,2},{8,13},{9,12},{10,... | collective-permute-start | bytes 368648 | tf_op jit(solution)/shard_map/ppermute | solution.py:495
  19.0 12.3 %collective-permute-start.7 = (bf16[240,256]{1,0:T(8,128)(2,1)}, bf16[240,256]{1,0:T(8,128)(2,1)S(1)}, u32[]{:S(2)}, u32[]{:S(2)}) collective-permute-start(bf16[240,256]{1,0:T(8,128)(2,1)} %bitcast.32), channel_id=1, source_target_pairs={{0,2},{1,3},{2,0},{3,1},{4,6},{5,7},{6,4},{7,5},{8,10},{9,11},{10,... | collective-permute-start | bytes 368648 | tf_op jit(solution)/shard_map/ppermute | solution.py:495
  26.4 4.9 %copy-start.1 = (bf16[2,120,256]{2,1,0:T(8,128)(2,1)S(1)}, bf16[2,120,256]{2,1,0:T(8,128)(2,1)}, u32[]{:S(2)}) copy-start(bf16[2,120,256]{2,1,0:T(8,128)(2,1)} %get-tuple-element.60) | copy-start | bytes 368644
  26.4 27.3 %all-to-all-start = ((bf16[8,240,256]{2,1,0:T(8,128)(2,1)}), bf16[8,240,256]{2,1,0:T(8,128)(2,1)S(1)}, u32[]{:S(2)}, u32[]{:S(2)}) async-start(bf16[8,240,256]{2,1,0:T(8,128)(2,1)} %bitcast.27), calls=%async_computation | async-start | bytes 1966080 | tf_op jit(solution)/shard_map/all_to_all | solution.py:602
  38.4 3.1 %collective-permute-start.8 = (bf16[2,8,80,512]{3,2,1,0:T(8,128)(2,1)S(1)}, bf16[2,8,80,512]{3,2,1,0:T(8,128)(2,1)S(1)}, u32[]{:S(2)}, u32[]{:S(2)}) collective-permute-start(bf16[2,8,80,512]{3,2,1,0:T(8,128)(2,1)S(1)} %get-tuple-element.80), channel_id=1, source_target_pairs={{0,8},{1,9},{2,10},{3,11},{4,12},{5,13},{6,14},{7,15},{8,0},{9,1},... | collective-permute-start | bytes 3932168 | tf_op jit(solution)/shard_map/ppermute | solution.py:495
  40.8 8.5 %copy-start = (bf16[1536,512]{1,0:T(8,128)(2,1)S(1)}, bf16[1536,512]{1,0:T(8,128)(2,1)}, u32[]{:S(2)}) copy-start(bf16[1536,512]{1,0:T(8,128)(2,1)} %conv_wide.1) | copy-start | bytes 4718596
  41.8 19.1 %collective-permute-start.10 = (bf16[4,80,512]{2,1,0:T(8,128)(2,1)S(1)}, bf16[4,80,512]{2,1,0:T(8,128)(2,1)S(1)}, u32[]{:S(2)}, u32[]{:S(2)}) collective-permute-start(bf16[4,80,512]{2,1,0:T(8,128)(2,1)S(1)} %get-tuple-element.90), channel_id=1, source_target_pairs={{0,17},{1,16},{2,19},{3,18},{4,21},{5,20},{6,23},{7,22},{8,25},{9,... | collective-permute-start | bytes 983048 | tf_op jit(solution)/shard_map/ppermute | solution.py:495
  44.9 16.1 %collective-permute-start.11 = (bf16[4,80,512]{2,1,0:T(8,128)(2,1)S(1)}, bf16[4,80,512]{2,1,0:T(8,128)(2,1)S(1)}, u32[]{:S(2)}, u32[]{:S(2)}) collective-permute-start(bf16[4,80,512]{2,1,0:T(8,128)(2,1)S(1)} %get-tuple-element.91), channel_id=1, source_target_pairs={{0,16},{1,17},{2,18},{3,19},{4,20},{5,21},{6,22},{7,23},{8,24},{9,... | collective-permute-start | bytes 983048 | tf_op jit(solution)/shard_map/ppermute | solution.py:495
  45.4 15.6 %collective-permute-start.12 = (bf16[4,80,512]{2,1,0:T(8,128)(2,1)S(1)}, bf16[4,80,512]{2,1,0:T(8,128)(2,1)S(1)}, u32[]{:S(2)}, u32[]{:S(2)}) collective-permute-start(bf16[4,80,512]{2,1,0:T(8,128)(2,1)S(1)} %get-tuple-element.92), channel_id=1, source_target_pairs={{0,1},{1,0},{2,3},{3,2},{4,5},{5,4},{6,7},{7,6},{8,9},{9,8},{10,11... | collective-permute-start | bytes 983048 | tf_op jit(solution)/shard_map/ppermute | solution.py:495
  45.5 15.4 %collective-permute-start.9 = (f32[8,512]{1,0:T(8,128)S(1)}, f32[8,512]{1,0:T(8,128)S(1)}, u32[]{:S(2)}, u32[]{:S(2)}) collective-permute-start(f32[8,512]{1,0:T(8,128)S(1)} %get-tuple-element.84), channel_id=1, source_target_pairs={{0,1},{1,2},{2,3},{3,4},{4,5},{5,6},{6,7},{8,9},{9,10},{10,11},{11... | collective-permute-start | bytes 49160 | tf_op jit(solution)/shard_map/ppermute | solution.py:22
  61.2 8.3 %collective-permute-start.13 = (bf16[80,512]{1,0:T(8,128)(2,1)S(1)}, bf16[80,512]{1,0:T(8,128)(2,1)S(1)}, u32[]{:S(2)}, u32[]{:S(2)}) collective-permute-start(bf16[80,512]{1,0:T(8,128)(2,1)S(1)} %get-tuple-element.99), channel_id=1, source_target_pairs={{0,4},{1,5},{2,6},{3,7},{4,0},{5,1},{6,2},{7,3},{8,12},{9,13},{10,... | collective-permute-start | bytes 245768 | tf_op jit(solution)/shard_map/ppermute | solution.py:495
  65.2 5.5 %collective-permute-start.14 = (bf16[80,512]{1,0:T(8,128)(2,1)S(1)}, bf16[80,512]{1,0:T(8,128)(2,1)S(1)}, u32[]{:S(2)}, u32[]{:S(2)}) collective-permute-start(bf16[80,512]{1,0:T(8,128)(2,1)S(1)} %get-tuple-element.100), channel_id=1, source_target_pairs={{0,2},{1,3},{2,0},{3,1},{4,6},{5,7},{6,4},{7,5},{8,10},{9,11},{10,... | collective-permute-start | bytes 245768 | tf_op jit(solution)/shard_map/ppermute | solution.py:495
  65.4 6.3 %collective-permute-start.15 = (bf16[80,512]{1,0:T(8,128)(2,1)S(1)}, bf16[80,512]{1,0:T(8,128)(2,1)S(1)}, u32[]{:S(2)}, u32[]{:S(2)}) collective-permute-start(bf16[80,512]{1,0:T(8,128)(2,1)S(1)} %get-tuple-element.101), channel_id=1, source_target_pairs={{0,6},{1,7},{2,4},{3,5},{4,2},{5,3},{6,0},{7,1},{8,14},{9,15},{10,... | collective-permute-start | bytes 245768 | tf_op jit(solution)/shard_map/ppermute | solution.py:495

commit v6 on v5

--- a/solution.py
+++ b/solution.py
@@ -671,7 +671,7 @@
         scratch=sems,
         raw_out=(0,),
     )
-    attn_t, first_rows, incoming, own = lax.optimization_barrier((attn_t, first_rows, incoming, own))
+    attn_t, first_rows, own = lax.optimization_barrier((attn_t, first_rows, own))
     own, *outgoing = local(second_sum_kernel, [own, *arrived], [piece] * 4, "second_sum")
     arrived = [swap(outgoing[k - 1], 0, 0, k, 0) for k in (2, 1, 3)]
     own_wide = 3 * channels // (dp * tm)

time: 72.7 us -> 72.7 us (level)
  starting transfers between devices: 34.2 us -> 33.2 us
  waiting for transfers between devices: 13.5 us -> 14.4 us
    ppermute x2, waiting for transfers between devices: 6.26 us -> 1.43 us  [passed_along(): lax.ppermute(value, axis, [(source, source + steps) for source in range(l...]
    all_to_all x1, waiting for transfers between devices: 2.19 us -> 5.98 us  [shards(): lax.all_to_all(proj_t.reshape(tm, pairs * depth, frames), 'tm', split_axi...]
    ppermute x14, waiting for transfers between devices: 5.06 us -> 7.04 us  [swap(): return lax.ppermute(value, ('dp', 'tm'), flipped(dy, dc, dz, dx))]
  transfers between devices with their start and end apart: 17 -> 17, of which waited for: 7 -> 6; matrix products, arithmetic and copies ran while one was open for 0% -> 0% of each run, Pallas kernels for 30% -> 30%
where the time goes in v6:
time: 72.7 us; the launch traced here: 72.4 us
  starting transfers between devices  33.2 us (46%)
  Pallas kernels  23.8 us (33%)
  waiting for transfers between devices  14.4 us (20%)
  between operations  0.81 us (1%)
    ppermute x14, starting transfers between devices, swap(): return lax.ppermute(value, ('dp', 'tm'), flipped(dy, dc, dz, dx))  24 us
    pallas_call x11, Pallas kernels, local(): pl.pallas_call(kernel, out_shape=out_shape, in_specs=[pl.BlockSpec(memory...  23.8 us
    ppermute x14, waiting for transfers between devices, swap(): return lax.ppermute(value, ('dp', 'tm'), flipped(dy, dc, dz, dx))  7.04 us
    all_to_all x1, waiting for transfers between devices, shards(): lax.all_to_all(proj_t.reshape(tm, pairs * depth, frames), 'tm', split_axi...  5.98 us
    all_to_all x1, starting transfers between devices, shards(): lax.all_to_all(proj_t.reshape(tm, pairs * depth, frames), 'tm', split_axi...  4.88 us
    ppermute x2, starting transfers between devices, passed_along(): lax.ppermute(value, axis, [(source, source + steps) for source in range(l...  4.4 us
  transfers between devices with their start and end apart: 17, of which 6 were waited for; matrix products, arithmetic and copies ran while one was open for 0% of the time, Pallas kernels for 30%

profile of v6, /device:TPU:0, one launch (start us, length us, event | category | flops | bytes accessed | tf_op | source)
XLA Modules:
  0.0 72.4 jit_solution(5051145134176851179)
XLA Ops:
  0.6 1.0 %cut.1 = (bf16[2,120,256]{2,1,0:T(8,128)(2,1)S(1)}, bf16[2,120,256]{2,1,0:T(8,128)(2,1)S(1)}, bf16[8,512]{1,0:T(8,128)(2,1)S(1)}) custom-call(bf16[2,120,2048]{2,1,0:T(8,128)(2,1)} %bitcast.24, bf16[1024,512]{1,0:T(8,128)(2,1)} %bitcast.22), custom_call_target="tpu_custom_call" | custom-call | flops 1000 | tf_op jit(solution)/shard_map/cut/pallas_call | solution.py:200
  1.6 3.0 %collective-permute-start.1 = (bf16[240,256]{1,0:T(8,128)(2,1)S(1)}, bf16[240,256]{1,0:T(8,128)(2,1)S(1)}, u32[]{:S(2)}, u32[]{:S(2)}) collective-permute-start(bf16[240,256]{1,0:T(8,128)(2,1)S(1)} %bitcast.21), channel_id=1, source_target_pairs={{0,1},{1,0},{2,3},{3,2},{4,5},{5,4},{6,7},{7,6},{8,9},{9,8},{10,11... | collective-permute-start | bytes 368648 | tf_op jit(solution)/shard_map/ppermute | solution.py:495
  4.6 3.6 %collective-permute-start.2 = (bf16[240,256]{1,0:T(8,128)(2,1)S(1)}, bf16[240,256]{1,0:T(8,128)(2,1)S(1)}, u32[]{:S(2)}, u32[]{:S(2)}) collective-permute-start(bf16[240,256]{1,0:T(8,128)(2,1)S(1)} %bitcast.20), channel_id=1, source_target_pairs={{0,7},{1,6},{2,5},{3,4},{4,3},{5,2},{6,1},{7,0},{8,15},{9,14},{10,... | collective-permute-start | bytes 368648 | tf_op jit(solution)/shard_map/ppermute | solution.py:495
  8.2 1.3 %collective-permute-start = (bf16[8,512]{1,0:T(8,128)(2,1)S(1)}, bf16[8,512]{1,0:T(8,128)(2,1)S(1)}, u32[]{:S(2)}, u32[]{:S(2)}) collective-permute-start(bf16[8,512]{1,0:T(8,128)(2,1)S(1)} %get-tuple-element.53), channel_id=1, source_target_pairs={{1,0},{2,1},{3,2},{4,3},{5,4},{6,5},{7,6},{9,8},{10,9},{11,10},{12... | collective-permute-start | bytes 24584 | tf_op jit(solution)/shard_map/ppermute | solution.py:22
  9.5 2.0 %rest_cut.1 = (bf16[2,120,256]{2,1,0:T(8,128)(2,1)}, bf16[2,120,256]{2,1,0:T(8,128)(2,1)}, bf16[2,120,256]{2,1,0:T(8,128)(2,1)}, bf16[2,120,256]{2,1,0:T(8,128)(...) custom-call(bf16[2,120,2048]{2,1,0:T(8,128)(2,1)} %bitcast.25), custom_call_target="tpu_custom_call" | custom-call | flops 1000 | tf_op jit(solution)/shard_map/rest_cut/pallas_call | solution.py:200
  11.5 2.5 %collective-permute-start.3 = (bf16[240,256]{1,0:T(8,128)(2,1)}, bf16[240,256]{1,0:T(8,128)(2,1)S(1)}, u32[]{:S(2)}, u32[]{:S(2)}) collective-permute-start(bf16[240,256]{1,0:T(8,128)(2,1)} %bitcast.36), channel_id=1, source_target_pairs={{0,6},{1,7},{2,4},{3,5},{4,2},{5,3},{6,0},{7,1},{8,14},{9,15},{10,... | collective-permute-start | bytes 368648 | tf_op jit(solution)/shard_map/ppermute | solution.py:495
  14.0 2.6 %collective-permute-start.4 = (bf16[240,256]{1,0:T(8,128)(2,1)}, bf16[240,256]{1,0:T(8,128)(2,1)S(1)}, u32[]{:S(2)}, u32[]{:S(2)}) collective-permute-start(bf16[240,256]{1,0:T(8,128)(2,1)} %bitcast.35), channel_id=1, source_target_pairs={{0,4},{1,5},{2,6},{3,7},{4,0},{5,1},{6,2},{7,3},{8,12},{9,13},{10,... | collective-permute-start | bytes 368648 | tf_op jit(solution)/shard_map/ppermute | solution.py:495
  16.6 0.0 collective-permute-done.refs_1_
  16.6 0.0 copy-start.2
  16.6 1.4 %collective-permute-start.5 = (bf16[240,256]{1,0:T(8,128)(2,1)}, bf16[240,256]{1,0:T(8,128)(2,1)S(1)}, u32[]{:S(2)}, u32[]{:S(2)}) collective-permute-start(bf16[240,256]{1,0:T(8,128)(2,1)} %bitcast.34), channel_id=1, source_target_pairs={{0,3},{1,2},{2,1},{3,0},{4,7},{5,6},{6,5},{7,4},{8,11},{9,10},{10,... | collective-permute-start | bytes 368648 | tf_op jit(solution)/shard_map/ppermute | solution.py:495
  18.0 0.0 collective-permute-done.1.refs_8_
  18.0 1.0 %collective-permute-start.6 = (bf16[240,256]{1,0:T(8,128)(2,1)}, bf16[240,256]{1,0:T(8,128)(2,1)S(1)}, u32[]{:S(2)}, u32[]{:S(2)}) collective-permute-start(bf16[240,256]{1,0:T(8,128)(2,1)} %bitcast.33), channel_id=1, source_target_pairs={{0,5},{1,4},{2,7},{3,6},{4,1},{5,0},{6,3},{7,2},{8,13},{9,12},{10,... | collective-permute-start | bytes 368648 | tf_op jit(solution)/shard_map/ppermute | solution.py:495
  19.0 0.0 collective-permute-done.2.refs_2_
  19.0 0.8 %collective-permute-start.7 = (bf16[240,256]{1,0:T(8,128)(2,1)}, bf16[240,256]{1,0:T(8,128)(2,1)S(1)}, u32[]{:S(2)}, u32[]{:S(2)}) collective-permute-start(bf16[240,256]{1,0:T(8,128)(2,1)} %bitcast.32), channel_id=1, source_target_pairs={{0,2},{1,3},{2,0},{3,1},{4,6},{5,7},{6,4},{7,5},{8,10},{9,11},{10,... | collective-permute-start | bytes 368648 | tf_op jit(solution)/shard_map/ppermute | solution.py:495
  19.9 0.0 copy-done.2
  19.9 6.5 %forward.1 = (bf16[1920,256]{1,0:T(8,128)(2,1)}, bf16[1536,512]{1,0:T(8,128)(2,1)}, bf16[1024,256]{1,0:T(8,128)(2,1)}, f32[512,512]{1,0:T(8,128)}, f32[512,512]{...) custom-call(bf16[1024,512]{1,0:T(8,128)(2,1)} %bitcast.23, ...), custom_call_target="tpu_custom_call" | custom-call | flops 1000 | tf_op jit(solution)/shard_map/forward/pallas_call | solution.py:200
  26.4 0.0 copy-start.1
  26.4 4.9 %all-to-all-start = ((bf16[8,240,256]{2,1,0:T(8,128)(2,1)}), bf16[8,240,256]{2,1,0:T(8,128)(2,1)S(1)}, u32[]{:S(2)}, u32[]{:S(2)}) async-start(bf16[8,240,256]{2,1,0:T(8,128)(2,1)} %bitcast.27), calls=%async_computation | async-start | bytes 1966080 | tf_op jit(solution)/shard_map/all_to_all | solution.py:602
  31.3 0.0 collective-permute-done.3.refs_3_
  31.3 0.0 collective-permute-done.4.refs_4_
  31.3 0.0 collective-permute-done.5.refs_5_
  31.3 0.0 collective-permute-done.6.refs_6_
  31.3 0.0 collective-permute-done.7.refs_7_
  31.3 0.0 copy-done.1
  31.3 7.1 %backward.1 = (bf16[2,8,80,512]{3,2,1,0:T(8,128)(2,1)S(1)}, bf16[512,512]{1,0:T(8,128)(2,1)S(1)}, bf16[256,512]{1,0:T(8,128)(2,1)S(1)}) custom-call(bf16[512,1920]{1,0:T(8,128)(2,1)} %refs_0_.1, bf16[240,256]{1,0:T(8,128)(2,1)S(1)} %bitcast.19, bf16[240,256]{1,0:T(8,128)(2,1)S(1)} %collective-permute-done.2.refs_2_, ...), custom_call_target="tpu_custom_call" | custom-call | flops 1000 | tf_op jit(solution)/shard_map/backward/pallas_call | solution.py:200
  38.4 0.1 collective-permute-start.8
  38.5 2.3 %own_grad.1 = (bf16[2,8,80,512]{3,2,1,0:T(8,128)(2,1)S(1)}, f32[8,512]{1,0:T(8,128)S(1)}) custom-call(bf16[1536,512]{1,0:T(8,128)(2,1)} %get-tuple-element.57.refs_19_.refs_0_, bf16[1024,256]{1,0:T(8,128)(2,1)} %get-tuple-element.58.refs_20_.refs_1_, bf16[1536,512]{1,0:T(8,128)(2,1)} %conv_wide.1, bf16[512,512]{1,0:T(8,128)(2,1)S(1)} %get-tuple-element.81.refs_3_.grad_conv, ...), custom_call_target="tpu_custom_call" | custom-call | flops 1000 | tf_op jit(solution)/shard_map/own_grad/pallas_call | solution.py:200
  40.8 0.0 copy-start
  40.9 0.7 collective-permute-done.8.received
  41.5 0.3 first_sum.1
  41.8 3.0 %collective-permute-start.10 = (bf16[4,80,512]{2,1,0:T(8,128)(2,1)S(1)}, bf16[4,80,512]{2,1,0:T(8,128)(2,1)S(1)}, u32[]{:S(2)}, u32[]{:S(2)}) collective-permute-start(bf16[4,80,512]{2,1,0:T(8,128)(2,1)S(1)} %get-tuple-element.88), channel_id=1, source_target_pairs={{0,17},{1,16},{2,19},{3,18},{4,21},{5,20},{6,23},{7,22},{8,25},{9,... | collective-permute-start | bytes 983048 | tf_op jit(solution)/shard_map/ppermute | solution.py:495
  44.9 0.5 collective-permute-start.11
  45.4 0.1 collective-permute-start.12
  45.5 0.0 copy-done
  45.5 2.2 %input_grad.1 = (bf16[1024,512]{1,0:T(8,128)(2,1)}, f32[8,512]{1,0:T(8,128)S(1)}) custom-call(bf16[512,512]{1,0:T(8,128)(2,1)S(1)} %get-tuple-element.81.refs_3_.grad_conv, bf16[1536,512]{1,0:T(8,128)(2,1)S(1)} %copy-done), custom_call_target="tpu_custom_call" | custom-call | flops 1000 | tf_op jit(solution)/shard_map/input_grad/pallas_call | solution.py:200
  47.7 6.0 %all-to-all-done = bf16[8,240,256]{2,1,0:T(8,128)(2,1)S(1)} async-done(((bf16[8,240,256]{2,1,0:T(8,128)(2,1)}), bf16[8,240,256]{2,1,0:T(8,128)(2,1)S(1)}, u32[]{:S(2)}, u32[]{:S(2)}) %all-to-all-start) | async-done | bytes 983072 | tf_op jit(solution)/shard_map/all_to_all | solution.py:602
  53.7 1.0 %join.1 = bf16[2,120,2048]{2,1,0:T(8,128)(2,1)} custom-call(bf16[8,2,120,256]{3,2,1,0:T(8,128)(2,1)S(1)} %bitcast.18), custom_call_target="tpu_custom_call" | custom-call | flops 1000 | tf_op jit(solution)/shard_map/join/pallas_call | solution.py:200
  54.7 0.1 collective-permute-done.10.b
  54.7 5.2 %collective-permute-done.11.c = bf16[4,80,512]{2,1,0:T(8,128)(2,1)S(1)} collective-permute-done((bf16[4,80,512]{2,1,0:T(8,128)(2,1)S(1)}, bf16[4,80,512]{2,1,0:T(8,128)(2,1)S(1)}, u32[]{:S(2)}, u32[]{:S(2)}) %collective-permute-start.11) | collective-permute-done | bytes 327712 | tf_op jit(solution)/shard_map/ppermute | solution.py:495
  59.9 1.1 %collective-permute-done.12.d = bf16[4,80,512]{2,1,0:T(8,128)(2,1)S(1)} collective-permute-done((bf16[4,80,512]{2,1,0:T(8,128)(2,1)S(1)}, bf16[4,80,512]{2,1,0:T(8,128)(2,1)S(1)}, u32[]{:S(2)}, u32[]{:S(2)}) %collective-permute-start.12) | collective-permute-done | bytes 327712 | tf_op jit(solution)/shard_map/ppermute | solution.py:495
  61.0 0.2 second_sum.1
  61.2 3.7 %collective-permute-start.13 = (bf16[80,512]{1,0:T(8,128)(2,1)S(1)}, bf16[80,512]{1,0:T(8,128)(2,1)S(1)}, u32[]{:S(2)}, u32[]{:S(2)}) collective-permute-start(bf16[80,512]{1,0:T(8,128)(2,1)S(1)} %get-tuple-element.97), channel_id=1, source_target_pairs={{0,4},{1,5},{2,6},{3,7},{4,0},{5,1},{6,2},{7,3},{8,12},{9,13},{10,... | collective-permute-start | bytes 245768 | tf_op jit(solution)/shard_map/ppermute | solution.py:495
  64.9 0.1 collective-permute-start.14
  65.0 1.5 %collective-permute-start.15 = (bf16[80,512]{1,0:T(8,128)(2,1)S(1)}, bf16[80,512]{1,0:T(8,128)(2,1)S(1)}, u32[]{:S(2)}, u32[]{:S(2)}) collective-permute-start(bf16[80,512]{1,0:T(8,128)(2,1)S(1)} %get-tuple-element.99), channel_id=1, source_target_pairs={{0,6},{1,7},{2,4},{3,5},{4,2},{5,3},{6,0},{7,1},{8,14},{9,15},{10,... | collective-permute-start | bytes 245768 | tf_op jit(solution)/shard_map/ppermute | solution.py:495
  66.5 3.1 %collective-permute-start.9 = (f32[8,512]{1,0:T(8,128)S(1)}, f32[8,512]{1,0:T(8,128)S(1)}, u32[]{:S(2)}, u32[]{:S(2)}) collective-permute-start(f32[8,512]{1,0:T(8,128)S(1)} %get-tuple-element.85), channel_id=1, source_target_pairs={{0,1},{1,2},{2,3},{3,4},{4,5},{5,6},{6,7},{8,9},{9,10},{10,11},{11... | collective-permute-start | bytes 49160 | tf_op jit(solution)/shard_map/ppermute | solution.py:22
  69.6 1.4 %collective-permute-done.9.incoming = f32[8,512]{1,0:T(8,128)S(1)} collective-permute-done((f32[8,512]{1,0:T(8,128)S(1)}, f32[8,512]{1,0:T(8,128)S(1)}, u32[]{:S(2)}, u32[]{:S(2)}) %collective-permute-start.9) | collective-permute-done | bytes 16416 | tf_op jit(solution)/shard_map/ppermute | solution.py:22
  71.0 0.6 first_row.1
  71.6 0.0 collective-permute-done.13.refs_1_
  71.6 0.0 collective-permute-done.14.refs_2_
  71.7 0.0 collective-permute-done.15.refs_3_
  71.7 0.7 last_sum.1
Async XLA Ops:
  1.6 16.4 %collective-permute-start.1 = (bf16[240,256]{1,0:T(8,128)(2,1)S(1)}, bf16[240,256]{1,0:T(8,128)(2,1)S(1)}, u32[]{:S(2)}, u32[]{:S(2)}) collective-permute-start(bf16[240,256]{1,0:T(8,128)(2,1)S(1)} %bitcast.21), channel_id=1, source_target_pairs={{0,1},{1,0},{2,3},{3,2},{4,5},{5,4},{6,7},{7,6},{8,9},{9,8},{10,11... | collective-permute-start | bytes 368648 | tf_op jit(solution)/shard_map/ppermute | solution.py:495
  4.6 14.4 %collective-permute-start.2 = (bf16[240,256]{1,0:T(8,128)(2,1)S(1)}, bf16[240,256]{1,0:T(8,128)(2,1)S(1)}, u32[]{:S(2)}, u32[]{:S(2)}) collective-permute-start(bf16[240,256]{1,0:T(8,128)(2,1)S(1)} %bitcast.20), channel_id=1, source_target_pairs={{0,7},{1,6},{2,5},{3,4},{4,3},{5,2},{6,1},{7,0},{8,15},{9,14},{10,... | collective-permute-start | bytes 368648 | tf_op jit(solution)/shard_map/ppermute | solution.py:495
  8.2 8.4 %collective-permute-start = (bf16[8,512]{1,0:T(8,128)(2,1)S(1)}, bf16[8,512]{1,0:T(8,128)(2,1)S(1)}, u32[]{:S(2)}, u32[]{:S(2)}) collective-permute-start(bf16[8,512]{1,0:T(8,128)(2,1)S(1)} %get-tuple-element.53), channel_id=1, source_target_pairs={{1,0},{2,1},{3,2},{4,3},{5,4},{6,5},{7,6},{9,8},{10,9},{11,10},{12... | collective-permute-start | bytes 24584 | tf_op jit(solution)/shard_map/ppermute | solution.py:22
  11.5 19.8 %collective-permute-start.3 = (bf16[240,256]{1,0:T(8,128)(2,1)}, bf16[240,256]{1,0:T(8,128)(2,1)S(1)}, u32[]{:S(2)}, u32[]{:S(2)}) collective-permute-start(bf16[240,256]{1,0:T(8,128)(2,1)} %bitcast.36), channel_id=1, source_target_pairs={{0,6},{1,7},{2,4},{3,5},{4,2},{5,3},{6,0},{7,1},{8,14},{9,15},{10,... | collective-permute-start | bytes 368648 | tf_op jit(solution)/shard_map/ppermute | solution.py:495
  14.0 17.3 %collective-permute-start.4 = (bf16[240,256]{1,0:T(8,128)(2,1)}, bf16[240,256]{1,0:T(8,128)(2,1)S(1)}, u32[]{:S(2)}, u32[]{:S(2)}) collective-permute-start(bf16[240,256]{1,0:T(8,128)(2,1)} %bitcast.35), channel_id=1, source_target_pairs={{0,4},{1,5},{2,6},{3,7},{4,0},{5,1},{6,2},{7,3},{8,12},{9,13},{10,... | collective-permute-start | bytes 368648 | tf_op jit(solution)/shard_map/ppermute | solution.py:495
  16.6 3.3 %copy-start.2 = (bf16[8,512]{1,0:T(8,128)(2,1)}, bf16[8,512]{1,0:T(8,128)(2,1)S(1)}, u32[]{:S(2)}) copy-start(bf16[8,512]{1,0:T(8,128)(2,1)S(1)} %collective-permute-done.refs_1_) | copy-start | bytes 24580
  16.6 14.7 %collective-permute-start.5 = (bf16[240,256]{1,0:T(8,128)(2,1)}, bf16[240,256]{1,0:T(8,128)(2,1)S(1)}, u32[]{:S(2)}, u32[]{:S(2)}) collective-permute-start(bf16[240,256]{1,0:T(8,128)(2,1)} %bitcast.34), channel_id=1, source_target_pairs={{0,3},{1,2},{2,1},{3,0},{4,7},{5,6},{6,5},{7,4},{8,11},{9,10},{10,... | collective-permute-start | bytes 368648 | tf_op jit(solution)/shard_map/ppermute | solution.py:495
  18.0 13.3 %collective-permute-start.6 = (bf16[240,256]{1,0:T(8,128)(2,1)}, bf16[240,256]{1,0:T(8,128)(2,1)S(1)}, u32[]{:S(2)}, u32[]{:S(2)}) collective-permute-start(bf16[240,256]{1,0:T(8,128)(2,1)} %bitcast.33), channel_id=1, source_target_pairs={{0,5},{1,4},{2,7},{3,6},{4,1},{5,0},{6,3},{7,2},{8,13},{9,12},{10,... | collective-permute-start | bytes 368648 | tf_op jit(solution)/shard_map/ppermute | solution.py:495
  19.0 12.3 %collective-permute-start.7 = (bf16[240,256]{1,0:T(8,128)(2,1)}, bf16[240,256]{1,0:T(8,128)(2,1)S(1)}, u32[]{:S(2)}, u32[]{:S(2)}) collective-permute-start(bf16[240,256]{1,0:T(8,128)(2,1)} %bitcast.32), channel_id=1, source_target_pairs={{0,2},{1,3},{2,0},{3,1},{4,6},{5,7},{6,4},{7,5},{8,10},{9,11},{10,... | collective-permute-start | bytes 368648 | tf_op jit(solution)/shard_map/ppermute | solution.py:495
  26.4 4.9 %copy-start.1 = (bf16[2,120,256]{2,1,0:T(8,128)(2,1)S(1)}, bf16[2,120,256]{2,1,0:T(8,128)(2,1)}, u32[]{:S(2)}) copy-start(bf16[2,120,256]{2,1,0:T(8,128)(2,1)} %get-tuple-element.59) | copy-start | bytes 368644
  26.4 27.3 %all-to-all-start = ((bf16[8,240,256]{2,1,0:T(8,128)(2,1)}), bf16[8,240,256]{2,1,0:T(8,128)(2,1)S(1)}, u32[]{:S(2)}, u32[]{:S(2)}) async-start(bf16[8,240,256]{2,1,0:T(8,128)(2,1)} %bitcast.27), calls=%async_computation | async-start | bytes 1966080 | tf_op jit(solution)/shard_map/all_to_all | solution.py:602
  38.4 3.1 %collective-permute-start.8 = (bf16[2,8,80,512]{3,2,1,0:T(8,128)(2,1)S(1)}, bf16[2,8,80,512]{3,2,1,0:T(8,128)(2,1)S(1)}, u32[]{:S(2)}, u32[]{:S(2)}) collective-permute-start(bf16[2,8,80,512]{3,2,1,0:T(8,128)(2,1)S(1)} %get-tuple-element.79), channel_id=1, source_target_pairs={{0,8},{1,9},{2,10},{3,11},{4,12},{5,13},{6,14},{7,15},{8,0},{9,1},... | collective-permute-start | bytes 3932168 | tf_op jit(solution)/shard_map/ppermute | solution.py:495
  40.8 4.7 %copy-start = (bf16[1536,512]{1,0:T(8,128)(2,1)S(1)}, bf16[1536,512]{1,0:T(8,128)(2,1)}, u32[]{:S(2)}) copy-start(bf16[1536,512]{1,0:T(8,128)(2,1)} %conv_wide.1) | copy-start | bytes 4718596
  41.8 12.9 %collective-permute-start.10 = (bf16[4,80,512]{2,1,0:T(8,128)(2,1)S(1)}, bf16[4,80,512]{2,1,0:T(8,128)(2,1)S(1)}, u32[]{:S(2)}, u32[]{:S(2)}) collective-permute-start(bf16[4,80,512]{2,1,0:T(8,128)(2,1)S(1)} %get-tuple-element.88), channel_id=1, source_target_pairs={{0,17},{1,16},{2,19},{3,18},{4,21},{5,20},{6,23},{7,22},{8,25},{9,... | collective-permute-start | bytes 983048 | tf_op jit(solution)/shard_map/ppermute | solution.py:495
  44.9 15.0 %collective-permute-start.11 = (bf16[4,80,512]{2,1,0:T(8,128)(2,1)S(1)}, bf16[4,80,512]{2,1,0:T(8,128)(2,1)S(1)}, u32[]{:S(2)}, u32[]{:S(2)}) collective-permute-start(bf16[4,80,512]{2,1,0:T(8,128)(2,1)S(1)} %get-tuple-element.89), channel_id=1, source_target_pairs={{0,16},{1,17},{2,18},{3,19},{4,20},{5,21},{6,22},{7,23},{8,24},{9,... | collective-permute-start | bytes 983048 | tf_op jit(solution)/shard_map/ppermute | solution.py:495
  45.4 15.6 %collective-permute-start.12 = (bf16[4,80,512]{2,1,0:T(8,128)(2,1)S(1)}, bf16[4,80,512]{2,1,0:T(8,128)(2,1)S(1)}, u32[]{:S(2)}, u32[]{:S(2)}) collective-permute-start(bf16[4,80,512]{2,1,0:T(8,128)(2,1)S(1)} %get-tuple-element.90), channel_id=1, source_target_pairs={{0,1},{1,0},{2,3},{3,2},{4,5},{5,4},{6,7},{7,6},{8,9},{9,8},{10,11... | collective-permute-start | bytes 983048 | tf_op jit(solution)/shard_map/ppermute | solution.py:495
  61.2 10.5 %collective-permute-start.13 = (bf16[80,512]{1,0:T(8,128)(2,1)S(1)}, bf16[80,512]{1,0:T(8,128)(2,1)S(1)}, u32[]{:S(2)}, u32[]{:S(2)}) collective-permute-start(bf16[80,512]{1,0:T(8,128)(2,1)S(1)} %get-tuple-element.97), channel_id=1, source_target_pairs={{0,4},{1,5},{2,6},{3,7},{4,0},{5,1},{6,2},{7,3},{8,12},{9,13},{10,... | collective-permute-start | bytes 245768 | tf_op jit(solution)/shard_map/ppermute | solution.py:495
  64.9 6.7 %collective-permute-start.14 = (bf16[80,512]{1,0:T(8,128)(2,1)S(1)}, bf16[80,512]{1,0:T(8,128)(2,1)S(1)}, u32[]{:S(2)}, u32[]{:S(2)}) collective-permute-start(bf16[80,512]{1,0:T(8,128)(2,1)S(1)} %get-tuple-element.98), channel_id=1, source_target_pairs={{0,2},{1,3},{2,0},{3,1},{4,6},{5,7},{6,4},{7,5},{8,10},{9,11},{10,... | collective-permute-start | bytes 245768 | tf_op jit(solution)/shard_map/ppermute | solution.py:495
  65.0 6.7 %collective-permute-start.15 = (bf16[80,512]{1,0:T(8,128)(2,1)S(1)}, bf16[80,512]{1,0:T(8,128)(2,1)S(1)}, u32[]{:S(2)}, u32[]{:S(2)}) collective-permute-start(bf16[80,512]{1,0:T(8,128)(2,1)S(1)} %get-tuple-element.99), channel_id=1, source_target_pairs={{0,6},{1,7},{2,4},{3,5},{4,2},{5,3},{6,0},{7,1},{8,14},{9,15},{10,... | collective-permute-start | bytes 245768 | tf_op jit(solution)/shard_map/ppermute | solution.py:495
  66.5 4.6 %collective-permute-start.9 = (f32[8,512]{1,0:T(8,128)S(1)}, f32[8,512]{1,0:T(8,128)S(1)}, u32[]{:S(2)}, u32[]{:S(2)}) collective-permute-start(f32[8,512]{1,0:T(8,128)S(1)} %get-tuple-element.85), channel_id=1, source_target_pairs={{0,1},{1,2},{2,3},{3,4},{4,5},{5,6},{6,7},{8,9},{9,10},{10,11},{11... | collective-permute-start | bytes 49160 | tf_op jit(solution)/shard_map/ppermute | solution.py:22
